TPU v7x, 256 devices: a whole 4x4x8 slice. The times are simulated.
256 devices in a mesh: vocab: 32 (over y_hi, z, core), width: 8 (over x, y_lo).
Axes of the slice: x: 4, y: 4 (y_hi: 2, y_lo: 2; y = y_hi * 2 + y_lo), z: 8, core: 2. Of those that a mesh axis runs over, the one named last changes fastest.
Arguments:
- hidden: bfloat16 [256, 4608], P('vocab', 'width'), may hold values from -72 to 72
- pre_gain: float32 [4608], P('width'), may hold values from 0.1 to 1.9
- post_gain: float32 [4608], P('width'), may hold values from 0.1 to 1.9
- final_gain: float32 [4608], P('width'), may hold values from 0.1 to 1.9
- gate_weight: bfloat16 [4608, 18432], P('width', 'vocab'), may hold values from -0.09375 to 0.09375
- up_weight: bfloat16 [4608, 18432], P('width', 'vocab'), may hold values from -0.09375 to 0.09375
- down_weight: bfloat16 [18432, 4608], P('vocab', 'width'), may hold values from -2 to 2
- head_weight: bfloat16 [4608, 131072], P('width', 'vocab'), may hold values from -0.25 to 0.25
- token_ids: int32 [256], replicated, may hold values from 0 to 131071
- rewards: float32 [32], replicated, may hold values from -3 to 3
Outputs:
- grad_hidden: bfloat16 [256, 4608], P('vocab', 'width')
- grad_gate: bfloat16 [4608, 18432], P('width', 'vocab')
- grad_up: bfloat16 [4608, 18432], P('width', 'vocab')
- grad_down: bfloat16 [18432, 4608], P('vocab', 'width')
- grad_head: bfloat16 [4608, 131072], P('width', 'vocab')
- loss: float32 [], replicated
All inputs are finite; a program needn't handle non-finite values.
Results may differ from a plain program's by a relative error of at most 0.013.
Values may be sent and summed in bfloat16 or wider, within the bound.
No kernel may reach another device: no remote copies, remote signals or barrier semaphores. Data moves between devices by JAX's collectives and lax.ppermute only.
A program may use at most 64 MiB of HBM per device.

v0:
```python
import math

import jax
import jax.numpy as jnp
from jax import lax
from jax.sharding import PartitionSpec as P

CAP = 30


EPS = 1e-06
ROOT_TWO_PI = math.sqrt(2.0 / math.pi)


def gelu_value(value):
    inner = ROOT_TWO_PI * (value + 0.044715 * value * value * value)
    return 0.5 * value * (1.0 + jnp.tanh(inner))


def gelu_slope(value):
    bent = jnp.tanh(ROOT_TWO_PI * (value + 0.044715 * value * value * value))
    return 0.5 * (1.0 + bent) + 0.5 * value * (1.0 - bent * bent) * ROOT_TWO_PI * (
        1.0 + 3.0 * 0.044715 * value * value
    )


def contract(left, right, left_dim, right_dim):
    return lax.dot_general(
        left, right, (((left_dim,), (right_dim,)), ((), ())), preferred_element_type=jnp.float32
    )


def shards(
    hidden,
    pre_gain,
    post_gain,
    final_gain,
    gate_weight,
    up_weight,
    down_weight,
    head_weight,
    token_ids,
    rewards,
):
    tok_dev = hidden.shape[0]
    width_dev = hidden.shape[1]
    model = width_dev * lax.axis_size("width")
    vocab_index = lax.axis_index("vocab")
    width_index = lax.axis_index("width")
    own_start = vocab_index * tok_dev
    gathered = lax.all_gather(hidden, "vocab", axis=0, tiled=True)
    inputs = gathered.astype(jnp.float32)
    squares_pre = lax.psum(jnp.sum(inputs * inputs, axis=1), "width")
    scale_pre = lax.rsqrt(squares_pre / model + EPS)[:, None]
    normed = (inputs * scale_pre * pre_gain).astype(jnp.bfloat16)
    gate_part = jnp.dot(normed, gate_weight, preferred_element_type=jnp.float32)
    upward_part = jnp.dot(normed, up_weight, preferred_element_type=jnp.float32)
    gate, upward = lax.psum((gate_part, upward_part), "width")
    gelu_gate = gelu_value(gate)
    active = (gelu_gate * upward).astype(jnp.bfloat16)
    branch = lax.psum(jnp.dot(active, down_weight, preferred_element_type=jnp.float32), "vocab")
    branch_gain = branch * post_gain
    squares_post = lax.psum(jnp.sum(branch * branch, axis=1), "width")
    scale_post = lax.rsqrt(squares_post / model + EPS)[:, None]
    resid = inputs + scale_post * branch_gain
    squares_final = lax.psum(jnp.sum(resid * resid, axis=1), "width")
    scale_final = lax.rsqrt(squares_final / model + EPS)[:, None]
    final = (resid * scale_final * final_gain).astype(jnp.bfloat16)
    vocab_dev = head_weight.shape[1]
    sub_rows = vocab_dev // lax.axis_size("width")
    columns = head_weight
    logits = lax.psum_scatter(
        contract(columns, final, 0, 1), "width", scatter_dimension=0, tiled=True
    )
    capped = CAP * jnp.tanh(logits / CAP)
    first_column = vocab_index * vocab_dev + width_index * sub_rows
    column_ids = first_column + jnp.arange(sub_rows, dtype=jnp.int32)
    hits = column_ids[:, None] == token_ids[None, :]
    total, target = lax.psum(
        (jnp.sum(jnp.exp(capped - CAP), axis=0), jnp.sum(jnp.where(hits, capped, 0.0), axis=0)),
        ("vocab", "width"),
    )
    lognorm = CAP + jnp.log(total)
    logprob = target - lognorm
    weights = jnp.repeat(rewards, token_ids.shape[0] // rewards.shape[0])
    loss = -jnp.mean(weights * logprob)
    prob = jnp.exp(capped - lognorm[None, :])
    slope = 1.0 - (capped / CAP) ** 2
    delta = (-weights[None, :] * (hits.astype(jnp.float32) - prob) * slope).astype(jnp.bfloat16)
    piece = lax.all_gather(delta, "width", axis=0, tiled=True)
    columns = head_weight
    block = contract(final, piece, 0, 1)
    grad_cols = block
    grad_rows = contract(piece, columns, 0, 1)
    grad_cols, grad_rows = (grad_cols, grad_rows)
    grad_head = grad_cols.astype(jnp.bfloat16)
    grad_final = lax.psum(grad_rows, "vocab")
    weighted = grad_final * final_gain
    back_final = lax.psum(jnp.sum(weighted * resid, axis=1), "width")[:, None]
    grad_resid = scale_final * weighted - resid * scale_final**3 * back_final / model
    weighted_post = grad_resid * post_gain
    back_post = lax.psum(jnp.sum(weighted_post * branch, axis=1), "width")[:, None]
    grad_branch = (
        scale_post * weighted_post - branch * scale_post**3 * back_post / model
    ).astype(jnp.bfloat16)
    resid_rows = lax.dynamic_slice_in_dim(grad_resid, own_start, tok_dev, 0)
    grad_down = contract(active, grad_branch, 0, 0).astype(jnp.bfloat16)
    grad_active = lax.psum(contract(grad_branch, down_weight, 1, 1), "width")
    grad_gate_in = (grad_active * upward * gelu_slope(gate)).astype(jnp.bfloat16)
    grad_up_in = (grad_active * gelu_gate).astype(jnp.bfloat16)
    grad_gate = contract(normed, grad_gate_in, 0, 0).astype(jnp.bfloat16)
    grad_up = contract(normed, grad_up_in, 0, 0).astype(jnp.bfloat16)
    grad_normed = lax.psum_scatter(
        contract(grad_gate_in, gate_weight, 1, 1) + contract(grad_up_in, up_weight, 1, 1),
        "vocab",
        scatter_dimension=0,
        tiled=True,
    )
    own_inputs = hidden.astype(jnp.float32)
    own_scale = lax.dynamic_slice_in_dim(scale_pre, own_start, tok_dev, 0)
    weighted_pre = grad_normed * pre_gain
    back_pre = lax.psum(jnp.sum(weighted_pre * own_inputs, axis=1), "width")[:, None]
    grad_hidden = (
        resid_rows + own_scale * weighted_pre - own_inputs * own_scale**3 * back_pre / model
    ).astype(jnp.bfloat16)
    return (grad_hidden, grad_gate, grad_up, grad_down, grad_head, loss)


def solution(mesh):
    return jax.shard_map(
        shards,
        mesh=mesh,
        in_specs=(
            P("vocab", "width"),
            P("width"),
            P("width"),
            P("width"),
            P("width", "vocab"),
            P("width", "vocab"),
            P("vocab", "width"),
            P("width", "vocab"),
            P(),
            P(),
        ),
        out_specs=(
            P("vocab", "width"),
            P("width", "vocab"),
            P("width", "vocab"),
            P("vocab", "width"),
            P("width", "vocab"),
            P(),
        ),
        check_vma=False,
    )
```

profile of v0, /device:TPU:1, one launch (start us, length us, event | category | flops | bytes accessed | tf_op | source)
XLA Modules:
  0.0 1347.1 jit_solution(14111036055207850782)
XLA Ops:
  7.2 47.5 %all_gather.6 = bf16[256,576]{1,0:T(8,128)(2,1)S(1)} all-gather(bf16[8,576]{1,0:T(8,128)(2,1)} %param.10), channel_id=1, replica_groups=mesh['vocab'=32,'width'=8] {'vocab'}, dimensions={0}, use_global_device_ids=true | all-gather | bytes 304128 | tf_op jit(solution)/shard_map/all_gather | solution.py:51
  54.7 0.1 fusion
  54.8 15.1 %psum.91 = f32[256]{0:T(256)S(1)} all-reduce(f32[256]{0:T(256)S(1)} %fusion), channel_id=1, replica_groups=mesh['vocab'=32,'width'=8] {'width'}, use_global_device_ids=true, to_apply=%region_1.0 | all-reduce | flops 256 | bytes 2048 | tf_op jit(solution)/shard_map/psum | solution.py:53
  69.9 2.5 fusion.23
  72.4 2.5 fusion.25
  75.0 76.9 %all-reduce.17.cloned.1.call-done = (f32[256,576]{0,1:T(8,128)}, f32[256,576]{0,1:T(8,128)}) async-done(((f32[256,576]{0,1:T(8,128)}, f32[256,576]{0,1:T(8,128)}), (f32[256,576]{0,1:T(8,128)}, f32[256,576]{0,1:T(8,128)})) %all-reduce.17.cloned.1.call-update) | async-done | bytes 1179664 | tf_op jit(solution)/shard_map/psum | solution.py:58
  151.9 1.4 multiply_convert_fusion.2
  153.3 0.7 copy-done.4
  154.0 1.3 fusion.27
  155.4 263.2 %all-reduce.9.cloned.1.call-done = f32[256,576]{1,0:T(8,128)} async-done(((f32[256,576]{1,0:T(8,128)}), f32[256,576]{1,0:T(8,128)}) %all-reduce.9.cloned.1.call-update) | async-done | bytes 589840 | tf_op jit(solution)/shard_map/psum | solution.py:61
  418.6 1.2 multiply_reduce_fusion.3
  419.9 15.0 %psum.95 = f32[256]{0:T(256)S(1)} all-reduce(f32[256]{0:T(256)S(1)} %multiply_reduce_fusion.3), channel_id=1, replica_groups=mesh['vocab'=32,'width'=8] {'width'}, use_global_device_ids=true, to_apply=%region_6.0 | all-reduce | flops 256 | bytes 2048 | tf_op jit(solution)/shard_map/psum | solution.py:63
  434.9 1.4 multiply_reduce_fusion.2
  436.2 12.8 psum.96
  449.0 6.2 convolution_bitcast_fusion
  455.3 0.6 copy-done.11
  455.9 0.1 broadcast_in_dim_reshape.3
  456.1 92.8 %reduce-scatter.3.cloned.1.call-done = f32[512,256]{0,1:T(8,128)} async-done(((f32[4096,256]{0,1:T(8,128)}), f32[512,256]{0,1:T(8,128)}) %reduce-scatter.3.cloned.1.call-update) | async-done | bytes 524304 | tf_op jit(solution)/shard_map/reduce_scatter | solution.py:72
  548.8 1.3 fusion.14
  550.2 77.2 %all-reduce.1 = (f32[256]{0:T(256)S(1)}, f32[256]{0:T(256)S(1)}) all-reduce(f32[256]{0:T(256)S(1)} %get-tuple-element.25, f32[256]{0:T(256)S(1)} %get-tuple-element.24), channel_id=1, replica_groups=mesh['vocab'=32,'width'=8] {'vocab','width'}, use_global_device_ids=true, to_apply=%region_11.12 | all-reduce | flops 512 | bytes 4096 | tf_op jit(solution)/shard_map/psum | solution.py:79
  627.4 0.6 multiply_reduce_fusion.4
  628.0 2.0 fusion.13
  630.1 49.5 %all-gather.2.cloned.1.call-done = bf16[4096,256]{0,1:T(8,128)(2,1)} async-done(((bf16[512,256]{0,1:T(8,128)(2,1)}), bf16[4096,256]{0,1:T(8,128)(2,1)}) %all-gather.2.cloned.1.call-update) | async-done | bytes 2097168 | tf_op jit(solution)/shard_map/all_gather | solution.py:90
  679.6 5.6 fusion.28
  685.3 261.1 %all-reduce.11.cloned.1.call-done = f32[256,576]{1,0:T(8,128)} async-done(((f32[256,576]{1,0:T(8,128)}), f32[256,576]{1,0:T(8,128)}) %all-reduce.11.cloned.1.call-update) | async-done | bytes 589840 | tf_op jit(solution)/shard_map/psum | solution.py:97
  946.4 1.2 multiply_reduce_fusion.1
  947.6 15.0 %psum.99 = f32[256]{0:T(256)S(1)} all-reduce(f32[256]{0:T(256)S(1)} %multiply_reduce_fusion.1), channel_id=1, replica_groups=mesh['vocab'=32,'width'=8] {'width'}, use_global_device_ids=true, to_apply=%region_14.15 | all-reduce | flops 256 | bytes 2048 | tf_op jit(solution)/shard_map/psum | solution.py:99
  962.6 2.3 multiply_reduce_fusion
  964.9 12.7 psum.100
  977.6 1.3 subtract_convert_fusion
  978.9 1.2 fusion.29
  980.2 0.2 all-reduce.15.cloned.1.call-start
  980.4 0.6 dynamic-slice.4
  982.4 73.4 %all-reduce.13.cloned.1.call-done = f32[256,576]{0,1:T(8,128)} async-done(((f32[256,576]{0,1:T(8,128)}), f32[256,576]{0,1:T(8,128)}) %all-reduce.13.cloned.1.call-update) | async-done | bytes 589840 | tf_op jit(solution)/shard_map/psum | solution.py:108
  1055.8 1.9 multiply_convert_fusion.1
  1057.7 0.5 fusion.30
  1058.3 0.5 convolution_add_fusion
  1058.8 1.0 copy.47
  1059.8 5.3 convolution_convert_fusion
  1065.2 1.3 convolution_convert_fusion.1
  1066.4 1.4 convolution_convert_fusion.2
  1067.8 252.2 %all-reduce.15.cloned.1.call-done = f32[256,576]{0,1:T(8,128)} async-done(((f32[256,576]{0,1:T(8,128)}), f32[256,576]{0,1:T(8,128)}) %all-reduce.15.cloned.1.call-update) | async-done | bytes 589840
  1320.1 1.1 constant_dynamic-slice_fusion
  1321.2 0.1 copy.48
  1321.3 0.1 fusion.20
  1321.4 1.4 convolution_convert_fusion.3
  1322.8 14.9 %psum.102 = f32[8]{0:T(128)S(1)} all-reduce(f32[8]{0:T(128)S(1)} %fusion.20), channel_id=1, replica_groups=mesh['vocab'=32,'width'=8] {'width'}, use_global_device_ids=true, to_apply=%region_20.21 | all-reduce | flops 8 | bytes 64 | tf_op jit(solution)/shard_map/psum | solution.py:122
  1337.7 1.4 fusion.19
  (43 shorter events, 0.6 us)
Async XLA Ops:
  7.2 146.9 %copy-start = (bf16[576,576]{1,0:T(8,128)(2,1)S(1)}, bf16[576,576]{1,0:T(8,128)(2,1)}, u32[]{:S(2)}) copy-start(bf16[576,576]{1,0:T(8,128)(2,1)} %param.16) | copy-start | bytes 1990660
  7.2 144.7 %all-reduce.17.cloned.1.call-start = ((), (), s32[]{:S(2)}) async-start(), calls=%async_computation.7 | async-start | bytes 2359296 | tf_op jit(solution)/shard_map/psum | solution.py:58
  69.9 365.0 %copy-start.9 = (f32[576]{0:T(1024)S(1)}, f32[576]{0:T(1024)}, u32[]{:S(2)}) copy-start(f32[576]{0:T(1024)} %param.12) | copy-start | bytes 6916
  72.4 376.6 %copy-start.6 = (f32[576]{0:T(1024)S(1)}, f32[576]{0:T(1024)}, u32[]{:S(2)}) copy-start(f32[576]{0:T(1024)} %param.13) | copy-start | bytes 6916
  74.9 343.7 %all-reduce.9.cloned.1.call-start = ((), (), s32[]{:S(2)}) async-start(), calls=%async_computation.1 | async-start | bytes 1310720 | tf_op jit(solution)/shard_map/psum | solution.py:61
  153.3 0.7 copy-start.4
  155.4 393.5 %reduce-scatter.3.cloned.1.call-start = ((), (), s32[]{:S(2)}) async-start(), calls=%async_computation.2 | async-start | bytes 4718592 | tf_op jit(solution)/shard_map/reduce_scatter | solution.py:72
  455.2 0.7 copy-start.11
  455.2 93.6 %copy-start.10 = (s32[256]{0:T(256)S(1)}, s32[256]{0:T(256)}, u32[]{:S(2)}) copy-start(s32[256]{0:T(256)} %param.18) | copy-start | bytes 3076
  455.3 224.3 %all-gather.2.cloned.1.call-start = ((), (), s32[]{:S(2)}) async-start(), calls=%async_computation.3 | async-start | bytes 2359296 | tf_op jit(solution)/shard_map/all_gather | solution.py:90
  630.0 332.6 %copy-start.1 = (f32[256,576]{1,0:T(8,128)S(1)}, f32[256,576]{1,0:T(8,128)}, u32[]{:S(2)}) copy-start(f32[256,576]{1,0:T(8,128)} %all-reduce.9.cloned.1.call-done) | copy-start | bytes 1769476
  630.1 316.3 %all-reduce.11.cloned.1.call-start = ((), (), s32[]{:S(2)}) async-start(), calls=%async_computation.4 | async-start | bytes 1310720 | tf_op jit(solution)/shard_map/psum | solution.py:97
  685.2 295.2 %copy-start.12 = (u32[256]{0:T(256)S(1)}, u32[256]{0:T(256)}, u32[]{:S(2)}) copy-start(u32[256]{0:T(256)} %constant.59) | copy-start | bytes 3076
  685.2 370.5 %all-reduce.13.cloned.1.call-start = ((), (), s32[]{:S(2)}) async-start(), calls=%async_computation.5 | async-start | bytes 1179648 | tf_op jit(solution)/shard_map/psum | solution.py:108
  962.6 95.1 %copy-start.2 = (bf16[576,576]{1,0:T(8,128)(2,1)S(1)}, bf16[576,576]{1,0:T(8,128)(2,1)}, u32[]{:S(2)}) copy-start(bf16[576,576]{1,0:T(8,128)(2,1)} %param.14) | copy-start | bytes 1990660
  980.2 339.9 %all-reduce.15.cloned.1.call-start = ((), (), s32[]{:S(2)}) async-start(), calls=%async_computation.6 | async-start | bytes 1179648
  1055.8 2.5 copy-start.3
  1059.8 5.4 copy-start.5
  1059.8 6.6 copy-start.7
  1059.8 261.5 %copy-start.8 = (bf16[8,576]{1,0:T(8,128)(2,1)S(1)}, bf16[8,576]{1,0:T(8,128)(2,1)}, u32[]{:S(2)}) copy-start(bf16[8,576]{1,0:T(8,128)(2,1)} %param.10) | copy-start | bytes 27652
Sparse Core Ops, SparseCore 0:
  75.0 76.8 all-reduce.16
  155.5 263.1 all-reduce.8
  455.4 93.4 reduce-scatter.2
  630.2 49.3 all-gather.1
  685.4 260.9 all-reduce.10
  980.3 75.4 all-reduce.12
  1059.9 260.0 all-reduce.14
where the time goes:
time: 1350 us
  waiting for transfers between devices  1070 us (79%)
  blocking collectives  210 us (16%)
  matrix products  29.8 us (2%)
  between operations  16.7 us (1%)
  other arithmetic  16.5 us (1%)
    psum x1, waiting for transfers between devices, shards(): lax.psum(jnp.dot(active, down_weight, preferred_element_type=jnp.float32)...  263 us
    psum x1, waiting for transfers between devices, shards(): grad_final = lax.psum(grad_rows, 'vocab')  261 us
    unnamed x8, waiting for transfers between devices  252 us
    reduce_scatter x1, waiting for transfers between devices, shards(): lax.psum_scatter(contract(columns, final, 0, 1), 'width', scatter_dimensi...  92.8 us
    psum x1, blocking collectives, shards(): lax.psum((jnp.sum(jnp.exp(capped - CAP), axis=0), jnp.sum(jnp.where(hits,...  77.2 us
    psum x1, waiting for transfers between devices, shards(): gate, upward = lax.psum((gate_part, upward_part), 'width')  76.9 us
    psum x1, waiting for transfers between devices, shards(): grad_active = lax.psum(contract(grad_branch, down_weight, 1, 1), 'width')  73.4 us
    all_gather x1, waiting for transfers between devices, shards(): piece = lax.all_gather(delta, 'width', axis=0, tiled=True)  49.5 us
  transfers between devices with their start and end apart: 7, of which 7 were waited for; matrix products, arithmetic and copies ran while one was open for 1% of the time, Pallas kernels for 0%

commit v1 on v0

v1 whole, which is shorter than its diff:
```python
import math

import jax
import jax.numpy as jnp
from jax import lax
from jax.sharding import PartitionSpec as P

CAP = 30.0
EPS = 1e-06
ROOT_TWO_PI = math.sqrt(2.0 / math.pi)
BF16 = jnp.bfloat16
F32 = jnp.float32


def gelu_parts(value):
    square = value * value
    bent = jnp.tanh(ROOT_TWO_PI * value * (1.0 + 0.044715 * square))
    half = 0.5 * (1.0 + bent)
    slope = half + 0.5 * value * (1.0 - bent * bent) * ROOT_TWO_PI * (1.0 + 3.0 * 0.044715 * square)
    return value * half, slope


def contract(left, right, left_dim, right_dim):
    return lax.dot_general(
        left, right, (((left_dim,), (right_dim,)), ((), ())), preferred_element_type=F32
    )


def split(stat):
    high = lax.reduce_precision(stat, 8, 7)
    rest = stat - high
    low = lax.reduce_precision(rest, 8, 7)
    return [high.astype(BF16)[..., None], low.astype(BF16)[..., None]]


def joined(columns, at):
    return columns[..., at].astype(F32) + columns[..., at + 1].astype(F32)


def scatter_sum(parts, axis):
    size = lax.axis_size(axis)
    moved = lax.all_to_all(
        parts.reshape(size, parts.shape[0] // size, parts.shape[1]), axis, 0, 0, tiled=True
    )
    return jnp.sum(moved.astype(F32), axis=0)


def gather(piece, axis):
    size = lax.axis_size(axis)
    moved = lax.all_to_all(
        jnp.broadcast_to(piece[None], (size, *piece.shape)), axis, 0, 0, tiled=True
    )
    return moved.reshape(size * piece.shape[0], piece.shape[1])


def width_sums(stats):
    rows = jnp.stack(stats, axis=-1)
    size = lax.axis_size("width")
    moved = lax.all_to_all(
        jnp.broadcast_to(rows[None], (size, *rows.shape)), "width", 0, 0, tiled=True
    )
    return jnp.sum(moved, axis=0)


def shards(
    hidden,
    pre_gain,
    post_gain,
    final_gain,
    gate_weight,
    up_weight,
    down_weight,
    head_weight,
    token_ids,
    rewards,
):
    tok_dev, width_dev = hidden.shape
    tokens = token_ids.shape[0]
    model = width_dev * lax.axis_size("width")
    ff_dev = gate_weight.shape[1]
    vocab_dev = head_weight.shape[1]
    vocab_index = lax.axis_index("vocab")
    width_index = lax.axis_index("width")
    own_start = vocab_index * tok_dev
    sub_tok = tokens // lax.axis_size("width")
    sub_start = width_index * sub_tok

    weights = jnp.repeat(rewards, tokens // rewards.shape[0])
    own_weights = lax.dynamic_slice_in_dim(weights, own_start, tok_dev, 0)
    column_ids = vocab_index * vocab_dev + jnp.arange(vocab_dev, dtype=jnp.int32)
    hits = column_ids[None, :] == token_ids[:, None]
    sub_ids = lax.dynamic_slice_in_dim(token_ids, sub_start, sub_tok, 0)
    sub_hits = column_ids[None, :] == sub_ids[:, None]

    target_rows = scatter_sum(
        contract(hits.astype(BF16), head_weight, 1, 1).astype(BF16), "vocab"
    )

    inputs = gather(hidden, "vocab").astype(F32)
    scaled = (inputs * pre_gain).astype(BF16)
    gate_part = jnp.dot(scaled, gate_weight, preferred_element_type=F32)
    up_part = jnp.dot(scaled, up_weight, preferred_element_type=F32)
    squares_part = jnp.sum(inputs * inputs, axis=1)
    message = jnp.concatenate(
        [gate_part.astype(BF16), up_part.astype(BF16), *split(squares_part)], axis=1
    )
    sums = scatter_sum(message, "width")
    sub_squares = sums[:, 2 * ff_dev] + sums[:, 2 * ff_dev + 1]
    sub_scale = lax.rsqrt(sub_squares / model + EPS)[:, None]
    gate = sums[:, :ff_dev] * sub_scale
    upward = sums[:, ff_dev : 2 * ff_dev] * sub_scale
    gelu_gate, gelu_slope = gelu_parts(gate)
    sub_active = (gelu_gate * upward).astype(BF16)
    message = gather(jnp.concatenate([sub_active, *split(sub_squares)], axis=1), "width")
    active = message[:, :ff_dev]
    squares_pre = joined(message, ff_dev)
    scale_pre = lax.rsqrt(squares_pre / model + EPS)[:, None]
    normed = (inputs * scale_pre * pre_gain).astype(BF16)
    own_squares = lax.dynamic_slice_in_dim(squares_pre, own_start, tok_dev, 0)

    branch = scatter_sum(
        jnp.dot(active, down_weight, preferred_element_type=F32).astype(BF16), "vocab"
    )
    own_inputs = hidden.astype(F32)
    bent = branch * post_gain
    stats = width_sums(
        [
            jnp.sum(branch * branch, axis=1),
            jnp.sum(own_inputs * bent, axis=1),
            jnp.sum(bent * bent, axis=1),
        ]
    )
    scale_post = lax.rsqrt(stats[:, 0] / model + EPS)
    squares_final = own_squares + scale_post * (2.0 * stats[:, 1] + scale_post * stats[:, 2])
    scale_final = lax.rsqrt(jnp.maximum(squares_final, 0.0) / model + EPS)[:, None]
    scale_post = scale_post[:, None]
    resid = own_inputs + scale_post * bent
    final = gather((resid * scale_final * final_gain).astype(BF16), "vocab")

    logits = scatter_sum(
        jnp.dot(final, head_weight, preferred_element_type=F32).astype(BF16), "width"
    )
    capped = CAP * jnp.tanh(logits / CAP)
    slope = 1.0 - (capped / CAP) ** 2
    raised = jnp.where(sub_hits, 0.0, jnp.exp(capped - CAP))
    sloped = raised * slope
    others_part = jnp.sum(raised, axis=1)
    cross_part = jnp.sum(sloped * logits, axis=1)
    target_part = jnp.sum(jnp.where(sub_hits, logits, 0.0), axis=1)
    message = gather(
        jnp.concatenate(
            [
                sloped.astype(BF16),
                *split(others_part),
                *split(cross_part),
                *split(target_part),
            ],
            axis=1,
        ),
        "width",
    )
    sloped_all = message[:, :vocab_dev]
    rows_part = contract(sloped_all, head_weight, 1, 1)
    own_sums = scatter_sum(
        jnp.concatenate([rows_part.astype(BF16), message[:, vocab_dev:]], axis=1), "vocab"
    )
    others = own_sums[:, width_dev] + own_sums[:, width_dev + 1]
    cross = own_sums[:, width_dev + 2] + own_sums[:, width_dev + 3]
    target_logit = own_sums[:, width_dev + 4] + own_sums[:, width_dev + 5]
    target = CAP * jnp.tanh(target_logit / CAP)
    total = others + jnp.exp(target - CAP)
    logprob = target - (CAP + jnp.log(total))
    spread = own_weights / total
    pull = -spread * others * (1.0 - (target / CAP) ** 2)

    grad_final = spread[:, None] * own_sums[:, :width_dev] + pull[:, None] * target_rows
    back_final = (spread * cross + pull * target_logit)[:, None] / scale_final
    weighted = grad_final * final_gain
    grad_resid = scale_final * weighted - resid * scale_final**3 * back_final / model
    weighted_post = grad_resid * post_gain
    back_post = width_sums([jnp.sum(weighted_post * branch, axis=1)])
    grad_branch = scale_post * weighted_post - branch * scale_post**3 * back_post / model

    message = gather(
        jnp.concatenate(
            [
                grad_branch.astype(BF16),
                *split(spread),
                *split(pull),
                *split(own_weights * logprob),
            ],
            axis=1,
        ),
        "vocab",
    )
    grad_branch = message[:, :width_dev]
    spread_all = joined(message, width_dev)[:, None]
    pull_all = joined(message, width_dev + 2)[:, None]
    loss = -jnp.mean(joined(message, width_dev + 4))

    grad_active = scatter_sum(contract(grad_branch, down_weight, 1, 1).astype(BF16), "width")
    sub_gate_in = (grad_active * upward * gelu_slope).astype(BF16)
    sub_up_in = (grad_active * gelu_gate).astype(BF16)
    back_part = jnp.sum(
        sub_gate_in.astype(F32) * gate + sub_up_in.astype(F32) * upward, axis=1
    )
    message = gather(
        jnp.concatenate([sub_gate_in, sub_up_in, *split(back_part)], axis=1), "width"
    )
    grad_gate_in = message[:, :ff_dev]
    grad_up_in = message[:, ff_dev : 2 * ff_dev]
    normed_part = contract(grad_gate_in, gate_weight, 1, 1) + contract(grad_up_in, up_weight, 1, 1)
    own_sums = scatter_sum(
        jnp.concatenate([normed_part.astype(BF16), message[:, 2 * ff_dev :]], axis=1), "vocab"
    )

    delta = (spread_all * sloped_all.astype(F32) + jnp.where(hits, pull_all, 0.0)).astype(BF16)
    grad_head = contract(final, delta, 0, 0).astype(BF16)
    grad_down = contract(active, grad_branch, 0, 0).astype(BF16)
    grad_gate = contract(normed, grad_gate_in, 0, 0).astype(BF16)
    grad_up = contract(normed, grad_up_in, 0, 0).astype(BF16)

    own_scale = lax.rsqrt(own_squares / model + EPS)[:, None]
    back_pre = (own_sums[:, width_dev] + own_sums[:, width_dev + 1])[:, None] / own_scale
    weighted_pre = own_sums[:, :width_dev] * pre_gain
    grad_hidden = (
        grad_resid + own_scale * weighted_pre - own_inputs * own_scale**3 * back_pre / model
    ).astype(BF16)
    return (grad_hidden, grad_gate, grad_up, grad_down, grad_head, loss)


def solution(mesh):
    return jax.shard_map(
        shards,
        mesh=mesh,
        in_specs=(
            P("vocab", "width"),
            P("width"),
            P("width"),
            P("width"),
            P("width", "vocab"),
            P("width", "vocab"),
            P("vocab", "width"),
            P("width", "vocab"),
            P(),
            P(),
        ),
        out_specs=(
            P("vocab", "width"),
            P("width", "vocab"),
            P("width", "vocab"),
            P("vocab", "width"),
            P("width", "vocab"),
            P(),
        ),
        check_vma=False,
    )
```

time: 1350 us -> 315 us (0.23)
  waiting for transfers between devices: 1070 us -> 108 us
  blocking collectives: 210 us -> 98.6 us
  starting transfers between devices: 0.47 us -> 49.8 us
  between operations: 16.7 us -> 2.91 us
    psum x4 -> x0, waiting for transfers between devices: 675 us -> none  [the longest x1 263 us: shards(): lax.psum(jnp.dot(active, down_weight, preferred_element_type=jnp.float32)...]
    unnamed x8 -> x0, waiting for transfers between devices: 252 us -> none
    psum x7 -> x0, blocking collectives: 163 us -> none  [the longest x1 77.2 us: shards(): lax.psum((jnp.sum(jnp.exp(capped - CAP), axis=0), jnp.sum(jnp.where(hits,...]
    all_to_all x0 -> x9, waiting for transfers between devices: none -> 108 us  [the longest x5 73.1 us: scatter_sum(): lax.all_to_all(parts.reshape(size, parts.shape[0] // size, parts.shape[1]...]
    all_to_all x0 -> x6, blocking collectives: none -> 98.6 us  [the longest x4 77.1 us: gather(): lax.all_to_all(jnp.broadcast_to(piece[None], (size, *piece.shape)), axis,...]
    reduce_scatter x1 -> x0, waiting for transfers between devices: 92.8 us -> none  [shards(): lax.psum_scatter(contract(columns, final, 0, 1), 'width', scatter_dimensi...]
    all_to_all x0 -> x9, starting transfers between devices: none -> 49.8 us  [the longest x5 34.6 us: scatter_sum(): lax.all_to_all(parts.reshape(size, parts.shape[0] // size, parts.shape[1]...]
    all_gather x1 -> x0, waiting for transfers between devices: 49.5 us -> none  [shards(): piece = lax.all_gather(delta, 'width', axis=0, tiled=True)]
  transfers between devices with their start and end apart: 7 -> 9, of which waited for: 7 -> 9; matrix products, arithmetic and copies ran while one was open for 1% -> 8% of each run, Pallas kernels for 0% -> 0%
where the time goes in v1:
time: 315 us; the launch traced here: 314 us
  waiting for transfers between devices  108 us (34%)
  blocking collectives  98.6 us (31%)
  starting transfers between devices  49.8 us (16%)
  matrix products  32.6 us (10%)
  local copies, waits for them, and re-layouts  14.6 us (5%)
  other arithmetic  6.74 us (2%)
    all_to_all x4, blocking collectives, gather(): lax.all_to_all(jnp.broadcast_to(piece[None], (size, *piece.shape)), axis,...  77.1 us
    all_to_all x5, waiting for transfers between devices, scatter_sum(): lax.all_to_all(parts.reshape(size, parts.shape[0] // size, parts.shape[1]...  73.1 us
    all_to_all x5, starting transfers between devices, scatter_sum(): lax.all_to_all(parts.reshape(size, parts.shape[0] // size, parts.shape[1]...  34.6 us
    all_to_all x2, waiting for transfers between devices, gather(): lax.all_to_all(jnp.broadcast_to(piece[None], (size, *piece.shape)), axis,...  26.8 us
    dot_general x9, matrix products, contract(): lax.dot_general(left, right, (((left_dim,), (right_dim,)), ((), ())), pre...  23.3 us
    all_to_all x2, blocking collectives, scatter_sum(): lax.all_to_all(parts.reshape(size, parts.shape[0] // size, parts.shape[1]...  21.5 us
    all_to_all x2, waiting for transfers between devices, width_sums(): lax.all_to_all(jnp.broadcast_to(rows[None], (size, *rows.shape)), 'width'...  8.65 us
    all_to_all x2, starting transfers between devices, gather(): lax.all_to_all(jnp.broadcast_to(piece[None], (size, *piece.shape)), axis,...  8.55 us
  transfers between devices with their start and end apart: 9, of which 9 were waited for; matrix products, arithmetic and copies ran while one was open for 8% of the time, Pallas kernels for 0%

profile of v1, /device:TPU:1, one launch (start us, length us, event | category | flops | bytes accessed | tf_op | source)
XLA Modules:
  0.0 313.8 jit_solution(3049435335450665873)
XLA Ops:
  0.6 0.8 broadcast_in_dim.46
  1.4 27.0 %all_to_all.75 = bf16[32,8,576]{2,1,0:T(8,128)(2,1)S(1)} all-to-all(bf16[32,8,576]{2,1,0:T(8,128)(2,1)S(1)} %broadcast_in_dim.46), channel_id=1, replica_groups=mesh['vocab'=32,'width'=8] {'vocab'}, dimensions={0} | all-to-all | bytes 589824 | tf_op jit(solution)/shard_map/all_to_all | solution.py:50
  29.0 1.6 convolution_convert_fusion.8
  30.8 1.6 convolution_convert_fusion.7
  33.1 12.6 %all_to_all.76 = bf16[8,32,1154]{2,1,0:T(8,128)(2,1)S(1)} all-to-all(bf16[8,32,1154]{2,1,0:T(8,128)(2,1)S(1)} %concatenate.28), channel_id=1, replica_groups=mesh['vocab'=32,'width'=8] {'width'}, dimensions={0} | all-to-all | bytes 1181696 | tf_op jit(solution)/shard_map/all_to_all | solution.py:42
  46.5 9.7 %all_to_all.77 = bf16[8,32,578]{2,1,0:T(8,128)(2,1)S(1)} all-to-all(bf16[8,32,578]{2,1,0:T(8,128)(2,1)S(1)} %broadcast_in_dim.47), channel_id=1, replica_groups=mesh['vocab'=32,'width'=8] {'width'}, dimensions={0} | all-to-all | bytes 591872 | tf_op jit(solution)/shard_map/all_to_all | solution.py:50
  56.7 0.9 copy.161
  57.6 8.5 %all-to-all-start.3 = ((bf16[32,8,576]{2,1,0:T(8,128)(2,1)}), bf16[32,8,576]{2,1,0:T(8,128)(2,1)S(1)}, u32[]{:S(2)}, u32[]{:S(2)}) async-start(bf16[32,8,576]{2,1,0:T(8,128)(2,1)} %bitcast.6), calls=%async_computation.3 | async-start | bytes 655360 | tf_op jit(solution)/shard_map/all_to_all | solution.py:42
  66.4 14.2 %all-to-all-done.3 = bf16[32,8,576]{2,1,0:T(8,128)(2,1)S(1)} async-done(((bf16[32,8,576]{2,1,0:T(8,128)(2,1)}), bf16[32,8,576]{2,1,0:T(8,128)(2,1)S(1)}, u32[]{:S(2)}, u32[]{:S(2)}) %all-to-all-start.3) | async-done | bytes 294944 | tf_op jit(solution)/shard_map/all_to_all | solution.py:42
  80.8 0.6 broadcast_in_dim.48
  81.4 3.3 %all-to-all-start.4 = ((f32[8,8,3]{1,2,0:T(4,128)}), f32[8,8,3]{1,2,0:T(4,128)S(1)}, u32[]{:S(2)}, u32[]{:S(2)}) async-start(f32[8,8,3]{1,2,0:T(4,128)} %broadcast_in_dim.48), calls=%async_computation.4 | async-start | bytes 32768 | tf_op jit(solution)/shard_map/all_to_all | solution.py:59
  85.4 4.4 %all-to-all-done.4 = f32[8,8,3]{1,2,0:T(4,128)S(1)} async-done(((f32[8,8,3]{1,2,0:T(4,128)}), f32[8,8,3]{1,2,0:T(4,128)S(1)}, u32[]{:S(2)}, u32[]{:S(2)}) %all-to-all-start.4) | async-done | bytes 800 | tf_op jit(solution)/shard_map/all_to_all | solution.py:59
  91.0 20.2 %all_to_all.78 = bf16[32,8,576]{2,1,0:T(8,128)(2,1)S(1)} all-to-all(bf16[32,8,576]{2,1,0:T(8,128)(2,1)S(1)} %broadcast_in_dim.51), channel_id=1, replica_groups=mesh['vocab'=32,'width'=8] {'vocab'}, dimensions={0} | all-to-all | bytes 589824 | tf_op jit(solution)/shard_map/all_to_all | solution.py:50
  111.2 5.6 %convolution_convert_fusion.1 = bf16[256,4096]{1,0:T(8,128)(2,1)} fusion(bf16[576,4096]{1,0:T(8,128)(2,1)} %param.17, bf16[32,8,576]{2,1,0:T(8,128)(2,1)S(1)} %all_to_all.78), kind=kOutput, calls=%fused_computation.4 | convolution fusion | flops 1209008128 | bytes 7110656 | tf_op jit(solution)/shard_map/dot_general | solution.py:141
  116.8 3.7 %all-to-all-start.6 = ((bf16[8,32,4096]{2,1,0:T(8,128)(2,1)}), bf16[8,32,4096]{2,1,0:T(8,128)(2,1)S(1)}, u32[]{:S(2)}, u32[]{:S(2)}) async-start(bf16[8,32,4096]{2,1,0:T(8,128)(2,1)} %bitcast.111), calls=%async_computation.6 | async-start | bytes 4194304 | tf_op jit(solution)/shard_map/all_to_all | solution.py:42
  121.2 28.7 %all-to-all-done.6 = bf16[8,32,4096]{2,1,0:T(8,128)(2,1)S(1)} async-done(((bf16[8,32,4096]{2,1,0:T(8,128)(2,1)}), bf16[8,32,4096]{2,1,0:T(8,128)(2,1)S(1)}, u32[]{:S(2)}, u32[]{:S(2)}) %all-to-all-start.6) | async-done | bytes 2097184 | tf_op jit(solution)/shard_map/all_to_all | solution.py:42
  150.2 1.1 fusion.28
  152.1 1.5 broadcast_in_dim.52
  153.6 4.4 %all-to-all-start.7 = ((bf16[8,32,4102]{2,1,0:T(8,128)(2,1)}), bf16[8,32,4102]{2,1,0:T(8,128)(2,1)}, u32[]{:S(2)}, u32[]{:S(2)}) async-start(bf16[8,32,4102]{2,1,0:T(8,128)(2,1)} %broadcast_in_dim.52), calls=%async_computation.7 | async-start | bytes 4325376 | tf_op jit(solution)/shard_map/all_to_all | solution.py:50
  157.9 3.9 %fusion.19 = bf16[256,576]{0,1:T(8,128)(2,1)S(1)} fusion(bf16[576,4096]{1,0:T(8,128)(2,1)} %param.17, s32[4096]{0:T(1024)S(1)} %iota_add_fusion, s32[256]{0:T(256)S(1)} %copy-done.19), kind=kOutput, calls=%fused_computation.25 | convolution fusion | flops 1209155584 | bytes 5030912 | tf_op jit(solution)/shard_map/dot_general | solution.py:24
  161.8 0.9 copy.170
  162.7 25.3 %all-to-all-done.7 = bf16[8,32,4102]{2,1,0:T(8,128)(2,1)} async-done(((bf16[8,32,4102]{2,1,0:T(8,128)(2,1)}), bf16[8,32,4102]{2,1,0:T(8,128)(2,1)}, u32[]{:S(2)}, u32[]{:S(2)}) %all-to-all-start.7) | async-done | bytes 2100256 | tf_op jit(solution)/shard_map/all_to_all | solution.py:50
  188.0 8.7 %all-to-all-start.9 = ((bf16[32,8,576]{2,1,0:T(8,128)(2,1)}), bf16[32,8,576]{2,1,0:T(8,128)(2,1)S(1)}, u32[]{:S(2)}, u32[]{:S(2)}) async-start(bf16[32,8,576]{2,1,0:T(8,128)(2,1)} %bitcast.20), calls=%async_computation.9 | async-start | bytes 655360 | tf_op jit(solution)/shard_map/all_to_all | solution.py:42
  196.7 0.8 slice.136
  197.6 4.4 %fusion.16 = bf16[256,576]{0,1:T(8,128)(2,1)S(1)} fusion(bf16[576,4096]{1,0:T(8,128)(2,1)} %param.17, bf16[256,4102]{1,0:T(8,128)(2,1)} %bitcast.18), kind=kOutput, calls=%fused_computation.24 | convolution fusion | flops 1208107008 | bytes 7110656 | tf_op jit(solution)/shard_map/dot_general | solution.py:24
  202.1 0.9 copy.169
  203.0 8.1 %all-to-all-done.9 = bf16[32,8,576]{2,1,0:T(8,128)(2,1)S(1)} async-done(((bf16[32,8,576]{2,1,0:T(8,128)(2,1)}), bf16[32,8,576]{2,1,0:T(8,128)(2,1)S(1)}, u32[]{:S(2)}, u32[]{:S(2)}) %all-to-all-start.9) | async-done | bytes 294944 | tf_op jit(solution)/shard_map/all_to_all | solution.py:42
  211.2 5.3 %all-to-all-start.8 = ((bf16[32,8,582]{2,1,0:T(8,128)(2,1)}), bf16[32,8,582]{2,1,0:T(8,128)(2,1)S(1)}, u32[]{:S(2)}, u32[]{:S(2)}) async-start(bf16[32,8,582]{2,1,0:T(8,128)(2,1)} %bitcast.19), calls=%async_computation.8 | async-start | bytes 655360 | tf_op jit(solution)/shard_map/all_to_all | solution.py:42
  216.7 14.4 %all-to-all-done.8 = bf16[32,8,582]{2,1,0:T(8,128)(2,1)S(1)} async-done(((bf16[32,8,582]{2,1,0:T(8,128)(2,1)}), bf16[32,8,582]{2,1,0:T(8,128)(2,1)S(1)}, u32[]{:S(2)}, u32[]{:S(2)}) %all-to-all-start.8) | async-done | bytes 298016 | tf_op jit(solution)/shard_map/all_to_all | solution.py:42
  232.3 3.3 %all-to-all-start.10 = ((f32[8,8,1]{1,2,0:T(1,128)}), f32[8,8,1]{1,2,0:T(1,128)S(1)}, u32[]{:S(2)}, u32[]{:S(2)}) async-start(f32[8,8,1]{1,2,0:T(1,128)} %broadcast_in_dim.53), calls=%async_computation.10 | async-start | bytes 8192 | tf_op jit(solution)/shard_map/all_to_all | solution.py:59
  236.2 4.3 %all-to-all-done.10 = f32[8,8,1]{1,2,0:T(1,128)S(1)} async-done(((f32[8,8,1]{1,2,0:T(1,128)}), f32[8,8,1]{1,2,0:T(1,128)S(1)}, u32[]{:S(2)}, u32[]{:S(2)}) %all-to-all-start.10) | async-done | bytes 288 | tf_op jit(solution)/shard_map/all_to_all | solution.py:59
  240.7 20.2 %all_to_all.79 = bf16[32,8,582]{2,1,0:T(8,128)(2,1)S(1)} all-to-all(bf16[32,8,582]{2,1,0:T(8,128)(2,1)S(1)} %broadcast_in_dim.60), channel_id=1, replica_groups=mesh['vocab'=32,'width'=8] {'vocab'}, dimensions={0} | all-to-all | bytes 595968 | tf_op jit(solution)/shard_map/all_to_all | solution.py:50
  261.5 9.0 %all_to_all.80 = bf16[8,32,576]{2,1,0:T(8,128)(2,1)S(1)} all-to-all(bf16[8,32,576]{2,1,0:T(8,128)(2,1)S(1)} %bitcast.112), channel_id=1, replica_groups=mesh['vocab'=32,'width'=8] {'width'}, dimensions={0} | all-to-all | bytes 589824 | tf_op jit(solution)/shard_map/all_to_all | solution.py:42
  271.2 0.9 broadcast_in_dim.61
  272.0 4.2 %all-to-all-start.13 = ((bf16[8,32,1154]{2,1,0:T(8,128)(2,1)}), bf16[8,32,1154]{2,1,0:T(8,128)(2,1)}, u32[]{:S(2)}, u32[]{:S(2)}) async-start(bf16[8,32,1154]{2,1,0:T(8,128)(2,1)} %broadcast_in_dim.61), calls=%async_computation.13 | async-start | bytes 1310720 | tf_op jit(solution)/shard_map/all_to_all | solution.py:50
  276.3 0.8 add_reduce_fusion
  277.1 5.6 %convolution_convert_fusion = bf16[576,4096]{1,0:T(8,128)(2,1)} fusion(f32[256]{0:T(256)S(1)} %get-tuple-element.10, f32[256]{0:T(256)S(1)} %get-tuple-element.11, s32[4096]{0:T(1024)S(1)} %iota_add_fusion, s32[256]{0:T(256)S(1)} %copy-done.19, bf16[256,4102]{1,0:T(8,128)(2,1)} %bitcast.18, bf16[32,8,576]{2,1,0:T(8,128)(2,1)} %copy-done.5), kind=kOutput, calls=%fused_computation | convolution fusion | flops 1216610304 | bytes 7162880 | tf_op jit(solution)/shard_map/dot_general | solution.py:24
  282.6 1.5 all-to-all-done.13
  284.1 1.4 fusion.36
  285.5 0.8 slice.147
  286.4 1.5 fusion.15
  288.0 0.9 copy.181
  288.9 8.3 %all-to-all-start.14 = ((bf16[32,8,578]{2,1,0:T(8,128)(2,1)}), bf16[32,8,578]{2,1,0:T(8,128)(2,1)S(1)}, u32[]{:S(2)}, u32[]{:S(2)}) async-start(bf16[32,8,578]{2,1,0:T(8,128)(2,1)} %bitcast.32), calls=%async_computation.14 | async-start | bytes 655360 | tf_op jit(solution)/shard_map/all_to_all | solution.py:42
  297.3 1.3 convolution_convert_fusion.2
  299.2 2.5 convolution_convert_fusion.3
  301.7 2.4 convolution_convert_fusion.4
  304.1 7.7 %all-to-all-done.14 = bf16[32,8,578]{2,1,0:T(8,128)(2,1)S(1)} async-done(((bf16[32,8,578]{2,1,0:T(8,128)(2,1)}), bf16[32,8,578]{2,1,0:T(8,128)(2,1)S(1)}, u32[]{:S(2)}, u32[]{:S(2)}) %all-to-all-start.14) | async-done | bytes 295968 | tf_op jit(solution)/shard_map/all_to_all | solution.py:42
  312.0 0.7 fusion.51
  (118 shorter events, 10.6 us)
Async XLA Ops:
  0.6 55.5 %copy-start = (bf16[576,576]{1,0:T(8,128)(2,1)S(1)}, bf16[576,576]{1,0:T(8,128)(2,1)}, u32[]{:S(2)}) copy-start(bf16[576,576]{1,0:T(8,128)(2,1)} %param.16) | copy-start | bytes 1990660
  32.6 48.0 %copy-start.6 = (bf16[8,576]{1,0:T(8,128)(2,1)S(1)}, bf16[8,576]{1,0:T(8,128)(2,1)}, u32[]{:S(2)}) copy-start(bf16[8,576]{1,0:T(8,128)(2,1)} %param.10) | copy-start | bytes 27652
  32.7 48.0 %copy-start.7 = (f32[576]{0:T(1024)S(1)}, f32[576]{0:T(1024)}, u32[]{:S(2)}) copy-start(f32[576]{0:T(1024)} %param.12) | copy-start | bytes 6916
  32.7 58.2 %copy-start.9 = (f32[576]{0:T(1024)S(1)}, f32[576]{0:T(1024)}, u32[]{:S(2)}) copy-start(f32[576]{0:T(1024)} %param.13) | copy-start | bytes 6916
  45.8 0.7 copy-start.3
  46.0 34.8 %copy-start.10 = (f32[32]{0:T(128)}, f32[32]{0:T(128)S(1)}, u32[]{:S(2)}) copy-start(f32[32]{0:T(128)S(1)} %get-tuple-element.48) | copy-start | bytes 388
  57.6 23.0 %all-to-all-start.3 = ((bf16[32,8,576]{2,1,0:T(8,128)(2,1)}), bf16[32,8,576]{2,1,0:T(8,128)(2,1)S(1)}, u32[]{:S(2)}, u32[]{:S(2)}) async-start(bf16[32,8,576]{2,1,0:T(8,128)(2,1)} %bitcast.6), calls=%async_computation.3 | async-start | bytes 655360 | tf_op jit(solution)/shard_map/all_to_all | solution.py:42
  81.4 8.3 %all-to-all-start.4 = ((f32[8,8,3]{1,2,0:T(4,128)}), f32[8,8,3]{1,2,0:T(4,128)S(1)}, u32[]{:S(2)}, u32[]{:S(2)}) async-start(f32[8,8,3]{1,2,0:T(4,128)} %broadcast_in_dim.48), calls=%async_computation.4 | async-start | bytes 32768 | tf_op jit(solution)/shard_map/all_to_all | solution.py:59
  111.2 5.6 %copy-start.5 = (bf16[32,8,576]{2,1,0:T(8,128)(2,1)}, bf16[32,8,576]{2,1,0:T(8,128)(2,1)S(1)}, u32[]{:S(2)}) copy-start(bf16[32,8,576]{2,1,0:T(8,128)(2,1)S(1)} %all_to_all.78) | copy-start | bytes 884740
  116.8 3.8 %copy-start.18 = (s32[256]{0:T(256)S(1)}, s32[256]{0:T(256)}, u32[]{:S(2)}) copy-start(s32[256]{0:T(256)} %param.18) | copy-start | bytes 3076
  116.8 33.1 %all-to-all-start.6 = ((bf16[8,32,4096]{2,1,0:T(8,128)(2,1)}), bf16[8,32,4096]{2,1,0:T(8,128)(2,1)S(1)}, u32[]{:S(2)}, u32[]{:S(2)}) async-start(bf16[8,32,4096]{2,1,0:T(8,128)(2,1)} %bitcast.111), calls=%async_computation.6 | async-start | bytes 4194304 | tf_op jit(solution)/shard_map/all_to_all | solution.py:42
  150.2 7.7 %copy-start.19 = (s32[256]{0:T(256)S(1)}, s32[256]{0:T(256)}, u32[]{:S(2)}) copy-start(s32[256]{0:T(256)} %param.18) | copy-start | bytes 3076
  153.6 34.4 %all-to-all-start.7 = ((bf16[8,32,4102]{2,1,0:T(8,128)(2,1)}), bf16[8,32,4102]{2,1,0:T(8,128)(2,1)}, u32[]{:S(2)}, u32[]{:S(2)}) async-start(bf16[8,32,4102]{2,1,0:T(8,128)(2,1)} %broadcast_in_dim.52), calls=%async_computation.7 | async-start | bytes 4325376 | tf_op jit(solution)/shard_map/all_to_all | solution.py:50
  188.0 23.2 %all-to-all-start.9 = ((bf16[32,8,576]{2,1,0:T(8,128)(2,1)}), bf16[32,8,576]{2,1,0:T(8,128)(2,1)S(1)}, u32[]{:S(2)}, u32[]{:S(2)}) async-start(bf16[32,8,576]{2,1,0:T(8,128)(2,1)} %bitcast.20), calls=%async_computation.9 | async-start | bytes 655360 | tf_op jit(solution)/shard_map/all_to_all | solution.py:42
  197.6 18.9 %copy-start.17 = (f32[32]{0:T(128)S(1)}, f32[32]{0:T(128)}, u32[]{:S(2)}) copy-start(f32[32]{0:T(128)} %param.19) | copy-start | bytes 388
  197.6 33.9 %copy-start.14 = (f32[8]{0:T(128)S(1)}, f32[8]{0:T(128)}, u32[]{:S(2)}) copy-start(f32[8]{0:T(128)} %get-tuple-element.46) | copy-start | bytes 100
  197.6 42.9 %copy-start.16 = (f32[8]{0:T(128)S(1)}, f32[8]{0:T(128)}, u32[]{:S(2)}) copy-start(f32[8]{0:T(128)} %get-tuple-element.44) | copy-start | bytes 100
  202.1 68.5 %copy-start.4 = (f32[32,1154]{1,0:T(8,128)S(1)}, f32[32,1154]{1,0:T(8,128)}, u32[]{:S(2)}) copy-start(f32[32,1154]{1,0:T(8,128)} %copy-done.3) | copy-start | bytes 443140
  202.1 68.5 %copy-start.11 = (f32[32]{0:T(128)S(1)}, f32[32]{0:T(128)}, u32[]{:S(2)}) copy-start(f32[32]{0:T(128)} %copy-done.10) | copy-start | bytes 388
  211.2 20.0 %all-to-all-start.8 = ((bf16[32,8,582]{2,1,0:T(8,128)(2,1)}), bf16[32,8,582]{2,1,0:T(8,128)(2,1)S(1)}, u32[]{:S(2)}, u32[]{:S(2)}) async-start(bf16[32,8,582]{2,1,0:T(8,128)(2,1)} %bitcast.19), calls=%async_computation.8 | async-start | bytes 655360 | tf_op jit(solution)/shard_map/all_to_all | solution.py:42
  232.3 8.2 %all-to-all-start.10 = ((f32[8,8,1]{1,2,0:T(1,128)}), f32[8,8,1]{1,2,0:T(1,128)S(1)}, u32[]{:S(2)}, u32[]{:S(2)}) async-start(f32[8,8,1]{1,2,0:T(1,128)} %broadcast_in_dim.53), calls=%async_computation.10 | async-start | bytes 8192 | tf_op jit(solution)/shard_map/all_to_all | solution.py:59
  272.0 12.1 %all-to-all-start.13 = ((bf16[8,32,1154]{2,1,0:T(8,128)(2,1)}), bf16[8,32,1154]{2,1,0:T(8,128)(2,1)}, u32[]{:S(2)}, u32[]{:S(2)}) async-start(bf16[8,32,1154]{2,1,0:T(8,128)(2,1)} %broadcast_in_dim.61), calls=%async_computation.13 | async-start | bytes 1310720 | tf_op jit(solution)/shard_map/all_to_all | solution.py:50
  277.1 7.1 %copy-start.1 = (bf16[576,576]{1,0:T(8,128)(2,1)S(1)}, bf16[576,576]{1,0:T(8,128)(2,1)}, u32[]{:S(2)}) copy-start(bf16[576,576]{1,0:T(8,128)(2,1)} %param.14) | copy-start | bytes 1990660
  277.1 9.3 %copy-start.2 = (bf16[576,576]{1,0:T(8,128)(2,1)S(1)}, bf16[576,576]{1,0:T(8,128)(2,1)}, u32[]{:S(2)}) copy-start(bf16[576,576]{1,0:T(8,128)(2,1)} %param.15) | copy-start | bytes 1990660
  282.6 16.6 %copy-start.8 = (f32[576]{0:T(1024)S(1)}, f32[576]{0:T(1024)}, u32[]{:S(2)}) copy-start(f32[576]{0:T(1024)} %param.11) | copy-start | bytes 6916
  282.6 16.6 %copy-start.15 = (f32[256,1]{0,1:T(1,128)S(1)}, f32[256,1]{0,1:T(1,128)}, u32[]{:S(2)}) copy-start(f32[256,1]{0,1:T(1,128)} %get-tuple-element.18) | copy-start | bytes 3076
  286.4 25.6 %copy-start.13 = (f32[8]{0:T(128)S(1)}, f32[8]{0:T(128)}, u32[]{:S(2)}) copy-start(f32[8]{0:T(128)} %get-tuple-element.21) | copy-start | bytes 100
  286.4 25.6 %copy-start.12 = (f32[8]{0:T(128)S(1)}, f32[8]{0:T(128)}, u32[]{:S(2)}) copy-start(f32[8]{0:T(128)} %get-tuple-element.20) | copy-start | bytes 100
  288.9 22.8 %all-to-all-start.14 = ((bf16[32,8,578]{2,1,0:T(8,128)(2,1)}), bf16[32,8,578]{2,1,0:T(8,128)(2,1)S(1)}, u32[]{:S(2)}, u32[]{:S(2)}) async-start(bf16[32,8,578]{2,1,0:T(8,128)(2,1)} %bitcast.32), calls=%async_computation.14 | async-start | bytes 655360 | tf_op jit(solution)/shard_map/all_to_all | solution.py:42

commit v2 on v1

--- a/solution.py
+++ b/solution.py
@@ -51,15 +51,6 @@
         jnp.broadcast_to(piece[None], (size, *piece.shape)), axis, 0, 0, tiled=True
     )
     return moved.reshape(size * piece.shape[0], piece.shape[1])
-
-
-def width_sums(stats):
-    rows = jnp.stack(stats, axis=-1)
-    size = lax.axis_size("width")
-    moved = lax.all_to_all(
-        jnp.broadcast_to(rows[None], (size, *rows.shape)), "width", 0, 0, tiled=True
-    )
-    return jnp.sum(moved, axis=0)
 
 
 def shards(
@@ -92,11 +83,15 @@
     sub_ids = lax.dynamic_slice_in_dim(token_ids, sub_start, sub_tok, 0)
     sub_hits = column_ids[None, :] == sub_ids[:, None]
 
-    target_rows = scatter_sum(
-        contract(hits.astype(BF16), head_weight, 1, 1).astype(BF16), "vocab"
-    )
+    target_part = contract(hits.astype(BF16), head_weight, 1, 1).astype(BF16)
 
     inputs = gather(hidden, "vocab").astype(F32)
+    first_logits = lax.psum_scatter(
+        jnp.dot((inputs * final_gain).astype(BF16), head_weight, preferred_element_type=F32),
+        "width",
+        scatter_dimension=0,
+        tiled=True,
+    )
     scaled = (inputs * pre_gain).astype(BF16)
     gate_part = jnp.dot(scaled, gate_weight, preferred_element_type=F32)
     up_part = jnp.dot(scaled, up_weight, preferred_element_type=F32)
@@ -118,55 +113,71 @@
     normed = (inputs * scale_pre * pre_gain).astype(BF16)
     own_squares = lax.dynamic_slice_in_dim(squares_pre, own_start, tok_dev, 0)
 
-    branch = scatter_sum(
-        jnp.dot(active, down_weight, preferred_element_type=F32).astype(BF16), "vocab"
-    )
+    own_sums = scatter_sum(
+        jnp.concatenate(
+            [jnp.dot(active, down_weight, preferred_element_type=F32).astype(BF16), target_part],
+            axis=1,
+        ),
+        "vocab",
+    )
+    branch = own_sums[:, :width_dev]
+    target_rows = own_sums[:, width_dev:]
     own_inputs = hidden.astype(F32)
     bent = branch * post_gain
-    stats = width_sums(
-        [
-            jnp.sum(branch * branch, axis=1),
-            jnp.sum(own_inputs * bent, axis=1),
-            jnp.sum(bent * bent, axis=1),
-        ]
-    )
-    scale_post = lax.rsqrt(stats[:, 0] / model + EPS)
-    squares_final = own_squares + scale_post * (2.0 * stats[:, 1] + scale_post * stats[:, 2])
-    scale_final = lax.rsqrt(jnp.maximum(squares_final, 0.0) / model + EPS)[:, None]
-    scale_post = scale_post[:, None]
-    resid = own_inputs + scale_post * bent
-    final = gather((resid * scale_final * final_gain).astype(BF16), "vocab")
-
-    logits = scatter_sum(
-        jnp.dot(final, head_weight, preferred_element_type=F32).astype(BF16), "width"
-    )
+    message = gather(
+        jnp.concatenate(
+            [
+                branch.astype(BF16),
+                *split(jnp.sum(branch * branch, axis=1)),
+                *split(jnp.sum(own_inputs * bent, axis=1)),
+                *split(jnp.sum(bent * bent, axis=1)),
+            ],
+            axis=1,
+        ),
+        "vocab",
+    )
+    branch_all = message[:, :width_dev].astype(F32)
+    second_part = jnp.dot(
+        (branch_all * (post_gain * final_gain)).astype(BF16),
+        head_weight,
+        preferred_element_type=F32,
+    ).astype(BF16)
+    sums = scatter_sum(jnp.concatenate([second_part, message[:, width_dev:]], axis=1), "width")
+    second_logits = sums[:, :vocab_dev]
+    stats = [sums[:, vocab_dev + 2 * i] + sums[:, vocab_dev + 2 * i + 1] for i in range(3)]
+    sub_post = lax.rsqrt(stats[0] / model + EPS)
+    along = stats[1] + sub_post * stats[2]
+    squares_final = sub_squares + sub_post * (stats[1] + along)
+    sub_final = lax.rsqrt(jnp.maximum(squares_final, 0.0) / model + EPS)
+    logits = sub_final[:, None] * (first_logits + sub_post[:, None] * second_logits)
     capped = CAP * jnp.tanh(logits / CAP)
     slope = 1.0 - (capped / CAP) ** 2
     raised = jnp.where(sub_hits, 0.0, jnp.exp(capped - CAP))
     sloped = raised * slope
-    others_part = jnp.sum(raised, axis=1)
-    cross_part = jnp.sum(sloped * logits, axis=1)
-    target_part = jnp.sum(jnp.where(sub_hits, logits, 0.0), axis=1)
-    message = gather(
-        jnp.concatenate(
-            [
-                sloped.astype(BF16),
-                *split(others_part),
-                *split(cross_part),
-                *split(target_part),
-            ],
-            axis=1,
-        ),
-        "width",
-    )
+    stats = [
+        jnp.sum(raised, axis=1),
+        jnp.sum(sloped * logits, axis=1),
+        jnp.sum(sloped * second_logits, axis=1),
+        jnp.sum(jnp.where(sub_hits, logits, 0.0), axis=1),
+        jnp.sum(jnp.where(sub_hits, second_logits, 0.0), axis=1),
+    ]
+    columns = [c for stat in [*stats, sub_post, sub_final, along] for c in split(stat)]
+    message = gather(jnp.concatenate([sloped.astype(BF16), *columns], axis=1), "width")
     sloped_all = message[:, :vocab_dev]
     rows_part = contract(sloped_all, head_weight, 1, 1)
+    stats_all = message[:, vocab_dev:]
+    post_all = joined(stats_all, 10)[:, None]
+    final_all = joined(stats_all, 12)[:, None]
+    own_stats = lax.dynamic_slice_in_dim(stats_all, own_start, tok_dev, 0)
+    scale_post = joined(own_stats, 10)[:, None]
+    scale_final = joined(own_stats, 12)[:, None]
+    along = joined(own_stats, 14)[:, None]
     own_sums = scatter_sum(
-        jnp.concatenate([rows_part.astype(BF16), message[:, vocab_dev:]], axis=1), "vocab"
-    )
-    others = own_sums[:, width_dev] + own_sums[:, width_dev + 1]
-    cross = own_sums[:, width_dev + 2] + own_sums[:, width_dev + 3]
-    target_logit = own_sums[:, width_dev + 4] + own_sums[:, width_dev + 5]
+        jnp.concatenate([rows_part.astype(BF16), stats_all[:, :10]], axis=1), "vocab"
+    )
+    others, cross, cross_second, target_logit, target_second = [
+        own_sums[:, width_dev + 2 * i] + own_sums[:, width_dev + 2 * i + 1] for i in range(5)
+    ]
     target = CAP * jnp.tanh(target_logit / CAP)
     total = others + jnp.exp(target - CAP)
     logprob = target - (CAP + jnp.log(total))
@@ -175,10 +186,14 @@
 
     grad_final = spread[:, None] * own_sums[:, :width_dev] + pull[:, None] * target_rows
     back_final = (spread * cross + pull * target_logit)[:, None] / scale_final
+    resid = own_inputs + scale_post * bent
     weighted = grad_final * final_gain
     grad_resid = scale_final * weighted - resid * scale_final**3 * back_final / model
     weighted_post = grad_resid * post_gain
-    back_post = width_sums([jnp.sum(weighted_post * branch, axis=1)])
+    back_post = (
+        scale_final * (spread * cross_second + pull * target_second)[:, None]
+        - scale_final**3 * back_final / model * along
+    )
     grad_branch = scale_post * weighted_post - branch * scale_post**3 * back_post / model
 
     message = gather(
@@ -215,6 +230,7 @@
     )
 
     delta = (spread_all * sloped_all.astype(F32) + jnp.where(hits, pull_all, 0.0)).astype(BF16)
+    final = ((inputs + post_all * branch_all * post_gain) * final_all * final_gain).astype(BF16)
     grad_head = contract(final, delta, 0, 0).astype(BF16)
     grad_down = contract(active, grad_branch, 0, 0).astype(BF16)
     grad_gate = contract(normed, grad_gate_in, 0, 0).astype(BF16)

time: 315 us -> 335 us (1.063)
  blocking collectives: 98.6 us -> 55.2 us
  between operations: 2.91 us -> 16.4 us
  waiting for transfers between devices: 108 us -> 121 us
  starting transfers between devices: 49.8 us -> 61.1 us
  local copies, waits for them, and re-layouts: 14.6 us -> 24.3 us
  other arithmetic: 6.74 us -> 16.3 us
  matrix products: 32.6 us -> 38.3 us
    all_to_all x4 -> x1, blocking collectives: 77.1 us -> 30.8 us  [gather(): lax.all_to_all(jnp.broadcast_to(piece[None], (size, *piece.shape)), axis,...]
    all_to_all x2 -> x5, waiting for transfers between devices: 26.8 us -> 54 us  [gather(): lax.all_to_all(jnp.broadcast_to(piece[None], (size, *piece.shape)), axis,...]
    all_to_all x2 -> x5, starting transfers between devices: 8.55 us -> 32.8 us  [gather(): lax.all_to_all(jnp.broadcast_to(piece[None], (size, *piece.shape)), axis,...]
    all_to_all x5, waiting for transfers between devices: 73.1 us -> 61.1 us  [scatter_sum(): lax.all_to_all(parts.reshape(size, parts.shape[0] // size, parts.shape[1]...]
    all_to_all x2 -> x0, waiting for transfers between devices: 8.65 us -> none  [width_sums(): lax.all_to_all(jnp.broadcast_to(rows[None], (size, *rows.shape)), 'width'...]
    all_to_all x2 -> x0, starting transfers between devices: 6.65 us -> none  [width_sums(): lax.all_to_all(jnp.broadcast_to(rows[None], (size, *rows.shape)), 'width'...]
    reduce_scatter x0 -> x1, waiting for transfers between devices: none -> 6.4 us  [shards(): lax.psum_scatter(jnp.dot((inputs * final_gain).astype(BF16), head_weight,...]
    all_to_all x5, starting transfers between devices: 34.6 us -> 28.3 us  [scatter_sum(): lax.all_to_all(parts.reshape(size, parts.shape[0] // size, parts.shape[1]...]
  transfers between devices with their start and end apart: 9 -> 11, of which waited for: 9 -> 11; matrix products, arithmetic and copies ran while one was open for 8% -> 12% of each run, Pallas kernels for 0% -> 0%
where the time goes in v2:
time: 335 us; the launch traced here: 333 us
  waiting for transfers between devices  121 us (36%)
  starting transfers between devices  61.1 us (18%)
  blocking collectives  55.2 us (16%)
  matrix products  38.3 us (11%)
  local copies, waits for them, and re-layouts  24.3 us (7%)
  between operations  16.4 us (5%)
  other arithmetic  16.3 us (5%)
    all_to_all x5, waiting for transfers between devices, scatter_sum(): lax.all_to_all(parts.reshape(size, parts.shape[0] // size, parts.shape[1]...  61.1 us
    all_to_all x5, waiting for transfers between devices, gather(): lax.all_to_all(jnp.broadcast_to(piece[None], (size, *piece.shape)), axis,...  54 us
    all_to_all x5, starting transfers between devices, gather(): lax.all_to_all(jnp.broadcast_to(piece[None], (size, *piece.shape)), axis,...  32.8 us
    all_to_all x1, blocking collectives, gather(): lax.all_to_all(jnp.broadcast_to(piece[None], (size, *piece.shape)), axis,...  30.8 us
    all_to_all x5, starting transfers between devices, scatter_sum(): lax.all_to_all(parts.reshape(size, parts.shape[0] // size, parts.shape[1]...  28.3 us
    all_to_all x1, blocking collectives, scatter_sum(): lax.all_to_all(parts.reshape(size, parts.shape[0] // size, parts.shape[1]...  24.4 us
    dot_general x9, matrix products, contract(): lax.dot_general(left, right, (((left_dim,), (right_dim,)), ((), ())), pre...  24.2 us
  transfers between devices with their start and end apart: 11, of which 11 were waited for; matrix products, arithmetic and copies ran while one was open for 12% of the time, Pallas kernels for 0%

profile of v2, /device:TPU:1, one launch (start us, length us, event | category | flops | bytes accessed | tf_op | source)
XLA Modules:
  0.0 333.1 jit_solution(15083569180473238927)
XLA Ops:
  7.2 1.5 broadcast_in_dim.44
  8.7 12.8 %all-to-all-start = ((bf16[32,8,576]{2,1,0:T(8,128)(2,1)}), bf16[32,8,576]{2,1,0:T(8,128)(2,1)S(1)}, u32[]{:S(2)}, u32[]{:S(2)}) async-start(bf16[32,8,576]{2,1,0:T(8,128)(2,1)} %broadcast_in_dim.44), calls=%async_computation | async-start | bytes 655360 | tf_op jit(solution)/shard_map/all_to_all | solution.py:50
  21.5 14.5 %all-to-all-done = bf16[32,8,576]{2,1,0:T(8,128)(2,1)S(1)} async-done(((bf16[32,8,576]{2,1,0:T(8,128)(2,1)}), bf16[32,8,576]{2,1,0:T(8,128)(2,1)S(1)}, u32[]{:S(2)}, u32[]{:S(2)}) %all-to-all-start) | async-done | bytes 294944 | tf_op jit(solution)/shard_map/all_to_all | solution.py:50
  36.5 1.6 convolution_convert_fusion.8
  38.3 1.6 convolution_convert_fusion.7
  40.1 1.2 concatenate.37
  41.3 4.1 %all-to-all-start.1 = ((bf16[8,32,1154]{2,1,0:T(8,128)(2,1)}), bf16[8,32,1154]{2,1,0:T(8,128)(2,1)S(1)}, u32[]{:S(2)}, u32[]{:S(2)}) async-start(bf16[8,32,1154]{2,1,0:T(8,128)(2,1)} %concatenate.37), calls=%async_computation.1 | async-start | bytes 1310720 | tf_op jit(solution)/shard_map/all_to_all | solution.py:42
  45.5 6.2 %fusion.40 = f32[256,4096]{1,0:T(8,128)} fusion(bf16[576,4096]{1,0:T(8,128)(2,1)} %param.17, bf16[32,8,576]{2,1,0:T(8,128)(2,1)S(1)} %all-to-all-done, f32[576]{0:T(1024)S(1)} %copy-done.12), kind=kOutput, calls=%fused_computation.65 | convolution fusion | flops 1208401920 | bytes 9210112
  51.7 2.6 all-to-all-done.1
  56.1 5.0 %all-to-all-start.2 = ((bf16[8,32,578]{2,1,0:T(8,128)(2,1)}), bf16[8,32,578]{2,1,0:T(8,128)(2,1)S(1)}, u32[]{:S(2)}, u32[]{:S(2)}) async-start(bf16[8,32,578]{2,1,0:T(8,128)(2,1)} %broadcast_in_dim.45), calls=%async_computation.2 | async-start | bytes 655360 | tf_op jit(solution)/shard_map/all_to_all | solution.py:50
  61.1 3.9 %fusion.19 = bf16[256,576]{0,1:T(8,128)(2,1)S(1)} fusion(bf16[576,4096]{1,0:T(8,128)(2,1)} %param.17, s32[4096]{0:T(1024)S(1)} %iota_add_fusion, s32[256]{0:T(256)S(1)} %copy-done.24), kind=kOutput, calls=%fused_computation.26 | convolution fusion | flops 1209155584 | bytes 5030912 | tf_op jit(solution)/shard_map/dot_general | solution.py:24
  64.9 9.0 %all-to-all-done.2 = bf16[8,32,578]{2,1,0:T(8,128)(2,1)S(1)} async-done(((bf16[8,32,578]{2,1,0:T(8,128)(2,1)}), bf16[8,32,578]{2,1,0:T(8,128)(2,1)S(1)}, u32[]{:S(2)}, u32[]{:S(2)}) %all-to-all-start.2) | async-done | bytes 295968 | tf_op jit(solution)/shard_map/all_to_all | solution.py:50
  74.8 24.4 %all_to_all.60 = bf16[32,8,1152]{2,1,0:T(8,128)(2,1)S(1)} all-to-all(bf16[32,8,1152]{2,1,0:T(8,128)(2,1)S(1)} %bitcast.112), channel_id=1, replica_groups=mesh['vocab'=32,'width'=8] {'vocab'}, dimensions={0} | all-to-all | bytes 1179648 | tf_op jit(solution)/shard_map/all_to_all | solution.py:42
  101.6 5.5 %all-to-all-start.4 = ((bf16[32,8,582]{2,1,0:T(8,128)(2,1)}), bf16[32,8,582]{2,1,0:T(8,128)(2,1)S(1)}, u32[]{:S(2)}, u32[]{:S(2)}) async-start(bf16[32,8,582]{2,1,0:T(8,128)(2,1)} %broadcast_in_dim.46), calls=%async_computation.4 | async-start | bytes 655360 | tf_op jit(solution)/shard_map/all_to_all | solution.py:50
  107.1 14.8 %all-to-all-done.4 = bf16[32,8,582]{2,1,0:T(8,128)(2,1)S(1)} async-done(((bf16[32,8,582]{2,1,0:T(8,128)(2,1)}), bf16[32,8,582]{2,1,0:T(8,128)(2,1)S(1)}, u32[]{:S(2)}, u32[]{:S(2)}) %all-to-all-start.4) | async-done | bytes 298016 | tf_op jit(solution)/shard_map/all_to_all | solution.py:50
  122.0 4.2 %convolution_convert_fusion.1 = bf16[256,4096]{1,0:T(8,128)(2,1)S(1)} fusion(bf16[576,4096]{1,0:T(8,128)(2,1)} %param.17, f32[576]{0:T(1024)S(1)} %mul.421, bf16[256,582]{1,0:T(8,128)(2,1)S(1)} %bitcast.117), kind=kOutput, calls=%fused_computation.4 | convolution fusion | flops 1209450496 | bytes 7116032 | tf_op jit(solution)/shard_map/dot_general | solution.py:140
  126.2 1.5 pad_maximum_fusion
  127.8 3.6 %all-to-all-start.5 = ((bf16[8,32,4102]{2,1,0:T(8,128)(2,1)}), bf16[8,32,4102]{2,1,0:T(8,128)(2,1)S(1)}, u32[]{:S(2)}, u32[]{:S(2)}) async-start(bf16[8,32,4102]{2,1,0:T(8,128)(2,1)} %bitcast.100), calls=%async_computation.5 | async-start | bytes 4325376 | tf_op jit(solution)/shard_map/all_to_all | solution.py:42
  131.4 1.3 dynamic_slice.12
  132.7 35.9 %all-to-all-done.5 = bf16[8,32,4102]{2,1,0:T(8,128)(2,1)S(1)} async-done(((bf16[8,32,4102]{2,1,0:T(8,128)(2,1)}), bf16[8,32,4102]{2,1,0:T(8,128)(2,1)S(1)}, u32[]{:S(2)}, u32[]{:S(2)}) %all-to-all-start.5) | async-done | bytes 2100256 | tf_op jit(solution)/shard_map/all_to_all | solution.py:42
  171.5 6.4 %reduce-scatter.4.cloned.1.call-done = f32[32,4096]{1,0:T(8,128)} async-done(((f32[256,4096]{1,0:T(8,128)}), f32[32,4096]{1,0:T(8,128)}) %reduce-scatter.4.cloned.1.call-update) | async-done | bytes 524304 | tf_op jit(solution)/shard_map/reduce_scatter | solution.py:89
  177.9 1.9 fusion.37
  182.1 30.8 %all_to_all.61 = bf16[8,32,4112]{2,1,0:T(8,128)(2,1)S(1)} all-to-all(bf16[8,32,4112]{2,1,0:T(8,128)(2,1)S(1)} %broadcast_in_dim.47), channel_id=1, replica_groups=mesh['vocab'=32,'width'=8] {'width'}, dimensions={0} | all-to-all | bytes 4210688 | tf_op jit(solution)/shard_map/all_to_all | solution.py:50
  212.9 5.3 %fusion.16 = bf16[256,576]{0,1:T(8,128)(2,1)} fusion(bf16[576,4096]{1,0:T(8,128)(2,1)} %param.17, bf16[256,4112]{1,0:T(8,128)(2,1)S(1)} %bitcast.107), kind=kOutput, calls=%fused_computation.25 | convolution fusion | flops 1208107008 | bytes 7110656 | tf_op jit(solution)/shard_map/dot_general | solution.py:24
  218.8 1.5 copy.205
  220.3 1.7 pad_maximum_fusion.2
  222.0 1.9 copy.180
  223.9 8.3 %all-to-all-start.7 = ((bf16[32,8,586]{2,1,0:T(8,128)(2,1)}), bf16[32,8,586]{2,1,0:T(8,128)(2,1)}, u32[]{:S(2)}, u32[]{:S(2)}) async-start(bf16[32,8,586]{2,1,0:T(8,128)(2,1)} %bitcast.113), calls=%async_computation.7 | async-start | bytes 655360 | tf_op jit(solution)/shard_map/all_to_all | solution.py:42
  232.2 1.3 broadcast_in_dim.48
  233.5 1.4 reshape.361
  235.2 11.5 %all-to-all-done.7 = bf16[32,8,586]{2,1,0:T(8,128)(2,1)} async-done(((bf16[32,8,586]{2,1,0:T(8,128)(2,1)}), bf16[32,8,586]{2,1,0:T(8,128)(2,1)}, u32[]{:S(2)}, u32[]{:S(2)}) %all-to-all-start.7) | async-done | bytes 300064 | tf_op jit(solution)/shard_map/all_to_all | solution.py:42
  246.7 1.0 convert_reduce_fusion.5
  249.4 1.5 subtract_convert_fusion
  251.7 5.3 %all-to-all-start.8 = ((bf16[32,8,582]{2,1,0:T(8,128)(2,1)}), bf16[32,8,582]{2,1,0:T(8,128)(2,1)S(1)}, u32[]{:S(2)}, u32[]{:S(2)}) async-start(bf16[32,8,582]{2,1,0:T(8,128)(2,1)} %broadcast_in_dim.55), calls=%async_computation.8 | async-start | bytes 655360 | tf_op jit(solution)/shard_map/all_to_all | solution.py:50
  257.3 14.3 %all-to-all-done.8 = bf16[32,8,582]{2,1,0:T(8,128)(2,1)S(1)} async-done(((bf16[32,8,582]{2,1,0:T(8,128)(2,1)}), bf16[32,8,582]{2,1,0:T(8,128)(2,1)S(1)}, u32[]{:S(2)}, u32[]{:S(2)}) %all-to-all-start.8) | async-done | bytes 298016 | tf_op jit(solution)/shard_map/all_to_all | solution.py:50
  273.0 3.4 %all-to-all-start.9 = ((bf16[8,32,576]{2,1,0:T(8,128)(2,1)}), bf16[8,32,576]{2,1,0:T(8,128)(2,1)S(1)}, u32[]{:S(2)}, u32[]{:S(2)}) async-start(bf16[8,32,576]{2,1,0:T(8,128)(2,1)} %bitcast.28), calls=%async_computation.9 | async-start | bytes 655360 | tf_op jit(solution)/shard_map/all_to_all | solution.py:42
  277.1 1.9 add_reduce_fusion.4
  279.0 3.5 %all-to-all-done.9 = bf16[8,32,576]{2,1,0:T(8,128)(2,1)S(1)} async-done(((bf16[8,32,576]{2,1,0:T(8,128)(2,1)}), bf16[8,32,576]{2,1,0:T(8,128)(2,1)S(1)}, u32[]{:S(2)}, u32[]{:S(2)}) %all-to-all-start.9) | async-done | bytes 294944 | tf_op jit(solution)/shard_map/all_to_all | solution.py:42
  284.0 4.2 %all-to-all-start.10 = ((bf16[8,32,1154]{2,1,0:T(8,128)(2,1)}), bf16[8,32,1154]{2,1,0:T(8,128)(2,1)}, u32[]{:S(2)}, u32[]{:S(2)}) async-start(bf16[8,32,1154]{2,1,0:T(8,128)(2,1)} %broadcast_in_dim.56), calls=%async_computation.10 | async-start | bytes 1310720 | tf_op jit(solution)/shard_map/all_to_all | solution.py:50
  289.1 5.7 %convolution_convert_fusion = bf16[576,4096]{1,0:T(8,128)(2,1)} fusion(f32[256]{0:T(256)S(1)} %get-tuple-element.14, f32[256]{0:T(256)S(1)} %get-tuple-element.15, s32[4096]{0:T(1024)S(1)} %copy-done.15, s32[256]{0:T(256)} %param.18, bf16[256,4112]{1,0:T(8,128)(2,1)} %bitcast.111, bf16[32,8,576]{2,1,0:T(8,128)(2,1)S(1)} %all-to-all-done, ...), kind=kOutput, calls=%fused_computation | convolution fusion | flops 1217789952 | bytes 7434752 | tf_op jit(solution)/shard_map/dot_general | solution.py:24
  294.7 1.3 all-to-all-done.10
  296.1 1.4 fusion.52
  298.3 1.5 fusion.15
  300.9 8.8 %all-to-all-start.11 = ((bf16[32,8,578]{2,1,0:T(8,128)(2,1)}), bf16[32,8,578]{2,1,0:T(8,128)(2,1)S(1)}, u32[]{:S(2)}, u32[]{:S(2)}) async-start(bf16[32,8,578]{2,1,0:T(8,128)(2,1)} %bitcast.31), calls=%async_computation.11 | async-start | bytes 655360 | tf_op jit(solution)/shard_map/all_to_all | solution.py:42
  309.7 1.3 convolution_convert_fusion.2
  311.7 2.5 convolution_convert_fusion.3
  314.1 2.4 convolution_convert_fusion.4
  316.5 7.7 %all-to-all-done.11 = bf16[32,8,578]{2,1,0:T(8,128)(2,1)S(1)} async-done(((bf16[32,8,578]{2,1,0:T(8,128)(2,1)}), bf16[32,8,578]{2,1,0:T(8,128)(2,1)S(1)}, u32[]{:S(2)}, u32[]{:S(2)}) %all-to-all-start.11) | async-done | bytes 295968 | tf_op jit(solution)/shard_map/all_to_all | solution.py:42
  (163 shorter events, 22.0 us)
Async XLA Ops:
  7.2 66.8 %copy-start = (bf16[576,576]{1,0:T(8,128)(2,1)S(1)}, bf16[576,576]{1,0:T(8,128)(2,1)}, u32[]{:S(2)}) copy-start(bf16[576,576]{1,0:T(8,128)(2,1)} %param.16) | copy-start | bytes 1990660
  7.2 38.3 %copy-start.12 = (f32[576]{0:T(1024)S(1)}, f32[576]{0:T(1024)}, u32[]{:S(2)}) copy-start(f32[576]{0:T(1024)} %param.13) | copy-start | bytes 6916
  8.7 27.2 %all-to-all-start = ((bf16[32,8,576]{2,1,0:T(8,128)(2,1)}), bf16[32,8,576]{2,1,0:T(8,128)(2,1)S(1)}, u32[]{:S(2)}, u32[]{:S(2)}) async-start(bf16[32,8,576]{2,1,0:T(8,128)(2,1)} %broadcast_in_dim.44), calls=%async_computation | async-start | bytes 655360 | tf_op jit(solution)/shard_map/all_to_all | solution.py:50
  41.3 13.0 %all-to-all-start.1 = ((bf16[8,32,1154]{2,1,0:T(8,128)(2,1)}), bf16[8,32,1154]{2,1,0:T(8,128)(2,1)S(1)}, u32[]{:S(2)}, u32[]{:S(2)}) async-start(bf16[8,32,1154]{2,1,0:T(8,128)(2,1)} %concatenate.37), calls=%async_computation.1 | async-start | bytes 1310720 | tf_op jit(solution)/shard_map/all_to_all | solution.py:42
  45.4 132.5 %reduce-scatter.4.cloned.1.call-start = ((), (), s32[]{:S(2)}) async-start(), calls=%async_computation.13 | async-start | bytes 4718592 | tf_op jit(solution)/shard_map/reduce_scatter | solution.py:89
  45.5 15.6 %copy-start.14 = (s32[4096]{0:T(1024)}, s32[4096]{0:T(1024)S(1)}, u32[]{:S(2)}) copy-start(s32[4096]{0:T(1024)S(1)} %iota_add_fusion) | copy-start | bytes 49156
  51.6 9.4 %copy-start.24 = (s32[256]{0:T(256)S(1)}, s32[256]{0:T(256)}, u32[]{:S(2)}) copy-start(s32[256]{0:T(256)} %param.18) | copy-start | bytes 3076
  54.3 1.7 copy-start.5
  54.6 0.5 copy-start.22
  54.6 0.5 copy-start.20
  56.1 17.9 %all-to-all-start.2 = ((bf16[8,32,578]{2,1,0:T(8,128)(2,1)}), bf16[8,32,578]{2,1,0:T(8,128)(2,1)S(1)}, u32[]{:S(2)}, u32[]{:S(2)}) async-start(bf16[8,32,578]{2,1,0:T(8,128)(2,1)} %broadcast_in_dim.45), calls=%async_computation.2 | async-start | bytes 655360 | tf_op jit(solution)/shard_map/all_to_all | solution.py:50
  64.9 35.0 %copy-start.10 = (bf16[8,576]{1,0:T(8,128)(2,1)S(1)}, bf16[8,576]{1,0:T(8,128)(2,1)}, u32[]{:S(2)}) copy-start(bf16[8,576]{1,0:T(8,128)(2,1)} %param.10) | copy-start | bytes 27652
  64.9 35.0 %copy-start.18 = (f32[576]{0:T(1024)S(1)}, f32[576]{0:T(1024)}, u32[]{:S(2)}) copy-start(f32[576]{0:T(1024)} %param.12) | copy-start | bytes 6916
  99.4 0.6 copy-start.9
  101.6 20.3 %all-to-all-start.4 = ((bf16[32,8,582]{2,1,0:T(8,128)(2,1)}), bf16[32,8,582]{2,1,0:T(8,128)(2,1)S(1)}, u32[]{:S(2)}, u32[]{:S(2)}) async-start(bf16[32,8,582]{2,1,0:T(8,128)(2,1)} %broadcast_in_dim.46), calls=%async_computation.4 | async-start | bytes 655360 | tf_op jit(solution)/shard_map/all_to_all | solution.py:50
  121.9 4.3 %copy-start.7 = (bf16[32,8,582]{2,1,0:T(8,128)(2,1)}, bf16[32,8,582]{2,1,0:T(8,128)(2,1)S(1)}, u32[]{:S(2)}) copy-start(bf16[32,8,582]{2,1,0:T(8,128)(2,1)S(1)} %all-to-all-done.4) | copy-start | bytes 893956
  127.8 40.7 %all-to-all-start.5 = ((bf16[8,32,4102]{2,1,0:T(8,128)(2,1)}), bf16[8,32,4102]{2,1,0:T(8,128)(2,1)S(1)}, u32[]{:S(2)}, u32[]{:S(2)}) async-start(bf16[8,32,4102]{2,1,0:T(8,128)(2,1)} %bitcast.100), calls=%async_computation.5 | async-start | bytes 4325376 | tf_op jit(solution)/shard_map/all_to_all | solution.py:42
  168.8 0.8 copy-start.4
  212.9 22.0 %copy-start.1 = (bf16[8,32,4112]{2,1,0:T(8,128)(2,1)}, bf16[8,32,4112]{2,1,0:T(8,128)(2,1)S(1)}, u32[]{:S(2)}) copy-start(bf16[8,32,4112]{2,1,0:T(8,128)(2,1)S(1)} %all_to_all.61) | copy-start | bytes 6316036
  223.9 22.8 %all-to-all-start.7 = ((bf16[32,8,586]{2,1,0:T(8,128)(2,1)}), bf16[32,8,586]{2,1,0:T(8,128)(2,1)}, u32[]{:S(2)}, u32[]{:S(2)}) async-start(bf16[32,8,586]{2,1,0:T(8,128)(2,1)} %bitcast.113), calls=%async_computation.7 | async-start | bytes 655360 | tf_op jit(solution)/shard_map/all_to_all | solution.py:42
  234.9 47.6 %copy-start.6 = (f32[32,1154]{1,0:T(8,128)S(1)}, f32[32,1154]{1,0:T(8,128)}, u32[]{:S(2)}) copy-start(f32[32,1154]{1,0:T(8,128)} %copy-done.5) | copy-start | bytes 443140
  234.9 47.6 %copy-start.21 = (f32[32]{0:T(128)S(1)}, f32[32]{0:T(128)}, u32[]{:S(2)}) copy-start(f32[32]{0:T(128)} %copy-done.20) | copy-start | bytes 388
  234.9 54.1 %copy-start.8 = (bf16[32,8,582]{2,1,0:T(8,128)(2,1)S(1)}, bf16[32,8,582]{2,1,0:T(8,128)(2,1)}, u32[]{:S(2)}) copy-start(bf16[32,8,582]{2,1,0:T(8,128)(2,1)} %copy-done.7) | copy-start | bytes 893956
  234.9 54.1 %copy-start.13 = (f32[576]{0:T(1024)S(1)}, f32[576]{0:T(1024)}, u32[]{:S(2)}) copy-start(f32[576]{0:T(1024)} %param.13) | copy-start | bytes 6916
  234.9 54.1 %copy-start.15 = (s32[4096]{0:T(1024)S(1)}, s32[4096]{0:T(1024)}, u32[]{:S(2)}) copy-start(s32[4096]{0:T(1024)} %copy-done.14) | copy-start | bytes 49156
  235.0 54.1 %copy-start.19 = (f32[576]{0:T(1024)S(1)}, f32[576]{0:T(1024)}, u32[]{:S(2)}) copy-start(f32[576]{0:T(1024)} %param.12) | copy-start | bytes 6916
  251.7 20.0 %all-to-all-start.8 = ((bf16[32,8,582]{2,1,0:T(8,128)(2,1)}), bf16[32,8,582]{2,1,0:T(8,128)(2,1)S(1)}, u32[]{:S(2)}, u32[]{:S(2)}) async-start(bf16[32,8,582]{2,1,0:T(8,128)(2,1)} %broadcast_in_dim.55), calls=%async_computation.8 | async-start | bytes 655360 | tf_op jit(solution)/shard_map/all_to_all | solution.py:50
  273.0 9.5 %all-to-all-start.9 = ((bf16[8,32,576]{2,1,0:T(8,128)(2,1)}), bf16[8,32,576]{2,1,0:T(8,128)(2,1)S(1)}, u32[]{:S(2)}, u32[]{:S(2)}) async-start(bf16[8,32,576]{2,1,0:T(8,128)(2,1)} %bitcast.28), calls=%async_computation.9 | async-start | bytes 655360 | tf_op jit(solution)/shard_map/all_to_all | solution.py:42
  284.0 12.1 %all-to-all-start.10 = ((bf16[8,32,1154]{2,1,0:T(8,128)(2,1)}), bf16[8,32,1154]{2,1,0:T(8,128)(2,1)}, u32[]{:S(2)}, u32[]{:S(2)}) async-start(bf16[8,32,1154]{2,1,0:T(8,128)(2,1)} %broadcast_in_dim.56), calls=%async_computation.10 | async-start | bytes 1310720 | tf_op jit(solution)/shard_map/all_to_all | solution.py:50
  289.0 7.1 %copy-start.2 = (bf16[576,576]{1,0:T(8,128)(2,1)S(1)}, bf16[576,576]{1,0:T(8,128)(2,1)}, u32[]{:S(2)}) copy-start(bf16[576,576]{1,0:T(8,128)(2,1)} %param.14) | copy-start | bytes 1990660
  289.0 9.3 %copy-start.3 = (bf16[576,576]{1,0:T(8,128)(2,1)S(1)}, bf16[576,576]{1,0:T(8,128)(2,1)}, u32[]{:S(2)}) copy-start(bf16[576,576]{1,0:T(8,128)(2,1)} %param.15) | copy-start | bytes 1990660
  294.7 16.9 %copy-start.17 = (f32[576]{0:T(1024)S(1)}, f32[576]{0:T(1024)}, u32[]{:S(2)}) copy-start(f32[576]{0:T(1024)} %param.11) | copy-start | bytes 6916
  294.7 16.9 %copy-start.23 = (f32[256,1]{0,1:T(1,128)S(1)}, f32[256,1]{0,1:T(1,128)}, u32[]{:S(2)}) copy-start(f32[256,1]{0,1:T(1,128)} %get-tuple-element.29) | copy-start | bytes 3076
  298.3 26.1 %copy-start.11 = (bf16[8,576]{1,0:T(8,128)(2,1)S(1)}, bf16[8,576]{1,0:T(8,128)(2,1)}, u32[]{:S(2)}) copy-start(bf16[8,576]{1,0:T(8,128)(2,1)} %param.10) | copy-start | bytes 27652
  298.3 26.1 %copy-start.16 = (f32[8,576]{1,0:T(8,128)S(1)}, f32[8,576]{1,0:T(8,128)}, u32[]{:S(2)}) copy-start(f32[8,576]{1,0:T(8,128)} %get-tuple-element.42) | copy-start | bytes 55300
  300.9 23.3 %all-to-all-start.11 = ((bf16[32,8,578]{2,1,0:T(8,128)(2,1)}), bf16[32,8,578]{2,1,0:T(8,128)(2,1)S(1)}, u32[]{:S(2)}, u32[]{:S(2)}) async-start(bf16[32,8,578]{2,1,0:T(8,128)(2,1)} %bitcast.31), calls=%async_computation.11 | async-start | bytes 655360 | tf_op jit(solution)/shard_map/all_to_all | solution.py:42
Sparse Core Ops, SparseCore 0:
  51.8 126.0 reduce-scatter.3

commit v3 on v0

v3 whole, which is shorter than its diff:
```python
import math

import jax
import jax.numpy as jnp
from jax import lax
from jax.experimental import pallas as pl
from jax.experimental.pallas import tpu as pltpu
from jax.sharding import PartitionSpec as P

CAP = 30.0
EPS = 1e-06
ROOT_TWO_PI = math.sqrt(2.0 / math.pi)
BF16 = jnp.bfloat16
F32 = jnp.float32
LANES = 128
CHUNK = 512


def contract(left, right, left_dim, right_dim):
    return lax.dot_general(
        left, right, (((left_dim,), (right_dim,)), ((), ())), preferred_element_type=F32
    )


def gelu_parts(value):
    square = value * value
    bent = jnp.tanh(ROOT_TWO_PI * value * (1.0 + 0.044715 * square))
    half = 0.5 * (1.0 + bent)
    slope = half + 0.5 * value * (1.0 - bent * bent) * ROOT_TWO_PI * (1.0 + 3.0 * 0.044715 * square)
    return value * half, slope


def padded(width):
    return width // LANES * LANES + LANES


def pick(tile, at):
    lane = lax.broadcasted_iota(jnp.int32, tile.shape, 1)
    return jnp.sum(jnp.where((lane == at) | (lane == at + 1), tile, 0.0), axis=1, keepdims=True)


def read_stats(tile, width, count):
    return [pick(tile, width % LANES + 2 * i) for i in range(count)]


def tail_of(width):
    return slice(width // LANES * LANES, padded(width))


def with_stats(tile, width, stats):
    lane = lax.broadcasted_iota(jnp.int32, tile.shape, 1)
    at = width % LANES
    tile = jnp.where(lane < at, tile, 0.0)
    for i, stat in enumerate(stats):
        high = stat.astype(BF16).astype(F32)
        tile = jnp.where(lane == at + 2 * i, high, tile)
        tile = jnp.where(lane == at + 2 * i + 1, stat - high, tile)
    return tile.astype(BF16)


def put(ref, block, stats):
    width = block.shape[1]
    ref[:, :width] = block
    tail = tail_of(width)
    ref[:, tail] = with_stats(ref[:, tail].astype(F32), width, stats)


def put_copies(ref, block, stats):
    put(ref.at[0], block, stats)
    whole = ref[0]
    for i in range(1, ref.shape[0]):
        ref[i] = whole


def summed(ref, columns):
    total = ref[0, :, columns].astype(F32)
    for i in range(1, ref.shape[0]):
        total = total + ref[i, :, columns].astype(F32)
    return total


def local(body, outs, *args, scratch=(), hbm=(), smem=()):
    spaces = {**{i: pl.ANY for i in hbm}, **{i: pltpu.SMEM for i in smem}}
    return pl.pallas_call(
        body,
        out_shape=tuple(jax.ShapeDtypeStruct(s, d) for s, d in outs),
        in_specs=[
            pl.BlockSpec(memory_space=spaces.get(i, pltpu.VMEM)) for i in range(len(args))
        ],
        out_specs=tuple(pl.BlockSpec(memory_space=pltpu.VMEM) for _ in outs),
        scratch_shapes=scratch,
        compiler_params=pltpu.CompilerParams(vmem_limit_bytes=40 << 20),
    )(*args)


def exchange(parts, axis):
    size = lax.axis_size(axis)
    if parts.ndim == 2:
        parts = parts.reshape(size, parts.shape[0] // size, parts.shape[1])
    return lax.all_to_all(parts, axis, 0, 0, tiled=True)


def flat(message):
    return message.reshape(message.shape[0] * message.shape[1], message.shape[2])


def chunk_copies(source, buffer, sems):
    width = buffer.shape[2]
    return [
        pltpu.make_async_copy(source.at[:, pl.ds(i * width, width)], buffer.at[i], sems.at[i])
        for i in range(buffer.shape[0])
    ]


def gate_step(inputs, pre_gain, gate_weight, up_weight, out):
    width = gate_weight.shape[1]
    values = inputs[...].astype(F32)
    scaled = (values * pre_gain[...]).astype(BF16)
    squares = jnp.sum(values * values, axis=1, keepdims=True)
    put(out, contract(scaled, gate_weight[...], 1, 0).astype(BF16), [squares])
    out[:, padded(width) : padded(width) + width] = contract(
        scaled, up_weight[...], 1, 0
    ).astype(BF16)


def active_step(model, width, message, gate, upward, gelu_gate, gelu_slope, out):
    (squares,) = read_stats(summed(message, tail_of(width)), width, 1)
    scale = lax.rsqrt(squares / model + EPS)
    gate_value = summed(message, slice(0, width)) * scale
    up_value = summed(message, slice(padded(width), padded(width) + width)) * scale
    value, slope = gelu_parts(gate_value)
    gate[...] = gate_value
    upward[...] = up_value
    gelu_gate[...] = value
    gelu_slope[...] = slope
    put_copies(out, (value * up_value).astype(BF16), [squares])


def branch_step(message, down_weight, target_rows, out):
    width = down_weight.shape[0]
    depth = down_weight.shape[1]
    out[:, :depth] = contract(message[:, :width], down_weight[...], 1, 0).astype(BF16)
    out[:, padded(depth) : padded(depth) + depth] = target_rows[...]


def norm_step(message, inputs, post_gain, branch, target, out):
    width = branch.shape[1]
    value = summed(message, slice(0, width))
    branch[...] = value
    target[...] = summed(message, slice(padded(width), padded(width) + width))
    bent = value * post_gain[...]
    stats = [
        jnp.sum(value * value, axis=1, keepdims=True),
        jnp.sum(inputs[...].astype(F32) * bent, axis=1, keepdims=True),
        jnp.sum(bent * bent, axis=1, keepdims=True),
    ]
    lane = lax.broadcasted_iota(jnp.int32, out.shape[1:], 1)
    tile = jnp.zeros(out.shape[1:], F32)
    for i, stat in enumerate(stats):
        tile = jnp.where(lane == i, stat, tile)
    for i in range(out.shape[0]):
        out[i] = tile


def scale_step(model, ff_width, index, message, active, branch, scale_post, scale_final, out):
    tile = message[0]
    for i in range(1, message.shape[0]):
        tile = tile + message[i]
    lane = lax.broadcasted_iota(jnp.int32, tile.shape, 1)
    square, cross, bent = [
        jnp.sum(jnp.where(lane == i, tile, 0.0), axis=1, keepdims=True) for i in range(3)
    ]
    rows = pl.ds(pl.multiple_of(index[0] * tile.shape[0], tile.shape[0]), tile.shape[0])
    (own_squares,) = read_stats(active[rows, tail_of(ff_width)].astype(F32), ff_width, 1)
    post = lax.rsqrt(square / model + EPS)
    final_squares = own_squares + post * (2.0 * cross + post * bent)
    final = lax.rsqrt(jnp.maximum(final_squares, 0.0) / model + EPS)
    scale_post[...] = post
    scale_final[...] = final
    put_copies(out, branch[...].astype(BF16), [post, final])


def logit_step(message, inputs, post_gain, final_gain, down_weight, head, out, final, buffer, sems):
    copies = chunk_copies(head, buffer, sems)
    for copy in copies:
        copy.start()
    width = final.shape[1]
    branch = message[:, :width]
    post, scale = read_stats(message[:, tail_of(width)].astype(F32), width, 2)
    resid = inputs[...].astype(F32) + branch.astype(F32) * post * post_gain[...]
    final[...] = (resid * scale * final_gain[...]).astype(BF16)
    chunk = buffer.shape[2]
    vocab = chunk * buffer.shape[0]
    out[:, vocab : vocab + down_weight.shape[0]] = contract(
        branch, down_weight[...], 1, 1
    ).astype(BF16)
    for i, copy in enumerate(copies):
        copy.wait()
        out[:, i * chunk : (i + 1) * chunk] = contract(final[...], buffer[i], 1, 0).astype(BF16)


def soft_step(vocab, message, ids, out, branch_down):
    rows = message.shape[1]
    step = 256
    others = jnp.zeros((rows, step), F32)
    cross = jnp.zeros((rows, step), F32)
    target = jnp.zeros((rows, step), F32)
    lane = lax.broadcasted_iota(jnp.int32, (rows, step), 1)
    for i in range(vocab // step):
        columns = slice(i * step, (i + 1) * step)
        logits = summed(message, columns)
        hits = lane == ids[...] - i * step
        bent = jnp.tanh(logits / CAP)
        raised = jnp.where(hits, 0.0, jnp.exp(CAP * bent - CAP))
        sloped = raised * (1.0 - bent * bent)
        others = others + raised
        cross = cross + sloped * logits
        target = target + jnp.where(hits, logits, 0.0)
        part = sloped.astype(BF16)
        for j in range(out.shape[0]):
            out[j, :, columns] = part
    stats = [jnp.sum(x, axis=1, keepdims=True) for x in (others, cross, target)]
    tile = with_stats(jnp.zeros((rows, LANES), F32), vocab, stats)
    for j in range(out.shape[0]):
        out[j, :, vocab : vocab + LANES] = tile
    branch_down[...] = summed(message, slice(vocab, vocab + branch_down.shape[1]))


def row_step(message, head, out, buffer, sems):
    copies = chunk_copies(head, buffer, sems)
    for copy in copies:
        copy.start()
    chunk = buffer.shape[2]
    vocab = chunk * buffer.shape[0]
    total = jnp.zeros((message.shape[0], buffer.shape[1]), F32)
    for i, copy in enumerate(copies):
        copy.wait()
        total = total + contract(message[:, i * chunk : (i + 1) * chunk], buffer[i], 1, 1)
    put(
        out,
        total.astype(BF16),
        read_stats(message[:, vocab : vocab + LANES].astype(F32), vocab, 3),
    )


def resid_step(
    model,
    message,
    target_rows,
    branch,
    inputs,
    scale_post,
    scale_final,
    weights,
    post_gain,
    final_gain,
    grad_resid,
    out,
):
    width = branch.shape[1]
    others, cross, logit = read_stats(summed(message, tail_of(width)), width, 3)
    bent = jnp.tanh(logit / CAP)
    target = CAP * bent
    total = others + jnp.exp(target - CAP)
    logprob = target - CAP - jnp.log(total)
    spread = weights[...] / total
    pull = -spread * others * (1.0 - bent * bent)
    post = scale_post[...]
    final = scale_final[...]
    grad_final = spread * summed(message, slice(0, width)) + pull * target_rows[...]
    back_final = (spread * cross + pull * logit) / final
    value = branch[...]
    resid = inputs[...].astype(F32) + post * value * post_gain[...]
    grad = final * grad_final * final_gain[...] - resid * (
        final * final * final * back_final / model
    )
    grad_resid[...] = grad
    weighted = grad * post_gain[...]
    back_post = jnp.sum(weighted * value, axis=1, keepdims=True)
    put_copies(
        out,
        (post * weighted).astype(BF16),
        [spread, pull, weights[...] * logprob, back_post],
    )


def down_step(message, down_weight, out, loss):
    width = down_weight.shape[1]
    _, _, score, back_post = read_stats(message[:, tail_of(width)].astype(F32), width, 4)
    put(
        out,
        contract(message[:, :width], down_weight[...], 1, 1).astype(BF16),
        [back_post],
    )
    loss[...] = -jnp.sum(score, axis=0, keepdims=True) / message.shape[0]


def hidden_step(
    model, depth, index, message, branch_down, gate, upward, gelu_gate, gelu_slope, scales, out
):
    rows, width = gate.shape
    (back_post,) = read_stats(summed(message, tail_of(width)), width, 1)
    own = pl.ds(pl.multiple_of(index[0] * rows, rows), rows)
    (post,) = read_stats(scales[own, tail_of(depth)].astype(F32), depth, 1)
    grad = summed(message, slice(0, width)) - branch_down[...] * (
        post * post * post * back_post / model
    )
    gate_in = (grad * upward[...] * gelu_slope[...]).astype(BF16)
    up_in = (grad * gelu_gate[...]).astype(BF16)
    back = jnp.sum(
        gate_in.astype(F32) * gate[...] + up_in.astype(F32) * upward[...], axis=1, keepdims=True
    )
    start = padded(width)
    put(out.at[0], gate_in, [back, back_post])
    out[0, :, start : start + width] = up_in
    whole = out[0]
    for i in range(1, out.shape[0]):
        out[i] = whole


def normed_step(message, gate_weight, up_weight, out):
    width = gate_weight.shape[1]
    start = padded(width)
    total = contract(message[:, :width], gate_weight[...], 1, 1) + contract(
        message[:, start : start + width], up_weight[...], 1, 1
    )
    put(
        out,
        total.astype(BF16),
        read_stats(message[:, tail_of(width)].astype(F32), width, 1),
    )


def last_step(model, ff_width, index, message, grad_resid, inputs, active, pre_gain, out):
    rows, width = out.shape
    own = pl.ds(pl.multiple_of(index[0] * rows, rows), rows)
    (squares,) = read_stats(active[own, tail_of(ff_width)].astype(F32), ff_width, 1)
    scale = lax.rsqrt(squares / model + EPS)
    (back,) = read_stats(summed(message, tail_of(width)), width, 1)
    weighted = summed(message, slice(0, width)) * pre_gain[...]
    out[...] = (
        grad_resid[...] + scale * weighted - inputs[...].astype(F32) * (scale * scale * back / model)
    ).astype(BF16)


def joined(message, width, i):
    at = width + 2 * i
    return message[:, at : at + 1].astype(F32) + message[:, at + 1 : at + 2].astype(F32)


def shards(
    hidden,
    pre_gain,
    post_gain,
    final_gain,
    gate_weight,
    up_weight,
    down_weight,
    head_weight,
    token_ids,
    rewards,
):
    tok_dev, width = hidden.shape
    tokens = token_ids.shape[0]
    rows_n = lax.axis_size("vocab")
    cols_n = lax.axis_size("width")
    model = width * cols_n
    ff = gate_weight.shape[1]
    vocab = head_weight.shape[1]
    sub = tokens // cols_n
    vocab_index = lax.axis_index("vocab")
    width_index = lax.axis_index("width")
    row_at = vocab_index[None].astype(jnp.int32)
    col_at = width_index[None].astype(jnp.int32)
    pre_gain = pre_gain[None, :]
    post_gain = post_gain[None, :]
    final_gain = final_gain[None, :]

    weights = jnp.repeat(rewards, tokens // rewards.shape[0])
    own_weights = lax.dynamic_slice_in_dim(weights, vocab_index * tok_dev, tok_dev, 0)[:, None]
    ids = token_ids - vocab_index * vocab
    hits = jnp.arange(vocab, dtype=jnp.int32)[None, :] == ids[:, None]
    sub_ids = lax.dynamic_slice_in_dim(ids, width_index * sub, sub, 0)[:, None]
    target_part = contract(hits.astype(BF16), head_weight, 1, 1).astype(BF16)
    buffer = (
        pltpu.VMEM((vocab // CHUNK, width, CHUNK), BF16),
        pltpu.SemaphoreType.DMA((vocab // CHUNK,)),
    )

    inputs = flat(exchange(jnp.broadcast_to(hidden[None], (rows_n, tok_dev, width)), "vocab"))
    (message,) = local(
        gate_step,
        [((tokens, padded(ff) * 2), BF16)],
        inputs,
        pre_gain,
        gate_weight,
        up_weight,
    )
    gate, upward, gelu_gate, gelu_slope, message = local(
        lambda *refs: active_step(model, ff, *refs),
        [((sub, ff), F32)] * 4 + [((cols_n, sub, padded(ff)), BF16)],
        exchange(message, "width"),
    )
    active = flat(exchange(message, "width"))
    (message,) = local(
        branch_step, [((tokens, padded(width) * 2), BF16)], active, down_weight, target_part
    )
    branch, target_rows, message = local(
        norm_step,
        [((tok_dev, width), F32)] * 2 + [((cols_n, tok_dev, LANES), F32)],
        exchange(message, "vocab"),
        hidden,
        post_gain,
    )
    scale_post, scale_final, message = local(
        lambda *refs: scale_step(model, ff, *refs),
        [((tok_dev, 1), F32)] * 2 + [((rows_n, tok_dev, padded(width)), BF16)],
        row_at,
        exchange(message, "width"),
        active,
        branch,
        smem=(0,),
    )
    branch_all = flat(exchange(message, "vocab"))
    message, final = local(
        logit_step,
        [((tokens, vocab + ff), BF16), ((tokens, width), BF16)],
        branch_all,
        inputs,
        post_gain,
        final_gain,
        down_weight,
        head_weight,
        scratch=buffer,
        hbm=(5,),
    )
    message, branch_down = local(
        lambda *refs: soft_step(vocab, *refs),
        [((cols_n, sub, vocab + LANES), BF16), ((sub, ff), F32)],
        exchange(message, "width"),
        sub_ids,
    )
    sloped = flat(exchange(message, "width"))
    (message,) = local(
        row_step,
        [((tokens, padded(width)), BF16)],
        sloped,
        head_weight,
        scratch=buffer,
        hbm=(1,),
    )
    grad_resid, message = local(
        lambda *refs: resid_step(model, *refs),
        [((tok_dev, width), F32), ((rows_n, tok_dev, padded(width)), BF16)],
        exchange(message, "vocab"),
        target_rows,
        branch,
        hidden,
        scale_post,
        scale_final,
        own_weights,
        post_gain,
        final_gain,
    )
    weighted = flat(exchange(message, "vocab"))
    message, loss = local(
        down_step,
        [((tokens, padded(ff)), BF16), ((1, 1), F32)],
        weighted,
        down_weight,
    )
    (message,) = local(
        lambda *refs: hidden_step(model, width, *refs),
        [((cols_n, sub, padded(ff) * 2), BF16)],
        col_at,
        exchange(message, "width"),
        branch_down,
        gate,
        upward,
        gelu_gate,
        gelu_slope,
        branch_all,
        smem=(0,),
    )
    grads_in = flat(exchange(message, "width"))
    (message,) = local(
        normed_step, [((tokens, padded(width)), BF16)], grads_in, gate_weight, up_weight
    )
    (grad_hidden,) = local(
        lambda *refs: last_step(model, ff, *refs),
        [((tok_dev, width), BF16)],
        row_at,
        exchange(message, "vocab"),
        grad_resid,
        hidden,
        active,
        pre_gain,
        smem=(0,),
    )

    spread = joined(weighted, width, 0)
    pull = joined(weighted, width, 1)
    delta = (spread * sloped[:, :vocab].astype(F32) + jnp.where(hits, pull, 0.0)).astype(BF16)
    grad_head = contract(final, delta, 0, 0).astype(BF16)
    post = joined(branch_all, width, 0)
    back_post = joined(grads_in, ff, 1)
    grad_branch = (
        weighted[:, :width].astype(F32)
        - branch_all[:, :width].astype(F32) * (post**3 * back_post / model)
    ).astype(BF16)
    grad_down = contract(active[:, :ff], grad_branch, 0, 0).astype(BF16)
    scale_pre = lax.rsqrt(joined(active, ff, 0) / model + EPS)
    normed = (inputs.astype(F32) * scale_pre * pre_gain).astype(BF16)
    grad_gate = contract(normed, grads_in[:, :ff], 0, 0).astype(BF16)
    grad_up = contract(normed, grads_in[:, padded(ff) : padded(ff) + ff], 0, 0).astype(BF16)
    return (grad_hidden, grad_gate, grad_up, grad_down, grad_head, loss[0, 0])


def solution(mesh):
    return jax.shard_map(
        shards,
        mesh=mesh,
        in_specs=(
            P("vocab", "width"),
            P("width"),
            P("width"),
            P("width"),
            P("width", "vocab"),
            P("width", "vocab"),
            P("vocab", "width"),
            P("width", "vocab"),
            P(),
            P(),
        ),
        out_specs=(
            P("vocab", "width"),
            P("width", "vocab"),
            P("width", "vocab"),
            P("vocab", "width"),
            P("width", "vocab"),
            P(),
        ),
        check_vma=False,
    )
```

time: 1350 us -> 309 us (0.23)
  waiting for transfers between devices: 1070 us -> 113 us
  blocking collectives: 210 us -> 63.2 us
  starting transfers between devices: 0.47 us -> 60.6 us
  local copies, waits for them, and re-layouts: 4.32 us -> 34.9 us
  Pallas kernels: 0 us -> 18.2 us
  between operations: 16.7 us -> 0.99 us
  other arithmetic: 16.5 us -> 1.24 us
  matrix products: 29.8 us -> 14.7 us
    psum x4 -> x0, waiting for transfers between devices: 675 us -> none  [the longest x1 263 us: shards(): lax.psum(jnp.dot(active, down_weight, preferred_element_type=jnp.float32)...]
    unnamed x8 -> x0, waiting for transfers between devices: 252 us -> none
    psum x7 -> x0, blocking collectives: 163 us -> none  [the longest x1 77.2 us: shards(): lax.psum((jnp.sum(jnp.exp(capped - CAP), axis=0), jnp.sum(jnp.where(hits,...]
    all_to_all x0 -> x9, waiting for transfers between devices: none -> 113 us  [exchange(): return lax.all_to_all(parts, axis, 0, 0, tiled=True)]
    reduce_scatter x1 -> x0, waiting for transfers between devices: 92.8 us -> none  [shards(): lax.psum_scatter(contract(columns, final, 0, 1), 'width', scatter_dimensi...]
    all_to_all x0 -> x4, blocking collectives: none -> 63.2 us  [exchange(): return lax.all_to_all(parts, axis, 0, 0, tiled=True)]
    all_to_all x0 -> x9, starting transfers between devices: none -> 60.6 us  [exchange(): return lax.all_to_all(parts, axis, 0, 0, tiled=True)]
    all_gather x1 -> x0, waiting for transfers between devices: 49.5 us -> none  [shards(): piece = lax.all_gather(delta, 'width', axis=0, tiled=True)]
  transfers between devices with their start and end apart: 7 -> 9, of which waited for: 7 -> 9; matrix products, arithmetic and copies ran while one was open for 1% -> 7% of each run, Pallas kernels for 0% -> 0%
where the time goes in v3:
time: 309 us; the launch traced here: 307 us
  waiting for transfers between devices  113 us (37%)
  blocking collectives  63.2 us (20%)
  starting transfers between devices  60.6 us (20%)
  local copies, waits for them, and re-layouts  34.9 us (11%)
  Pallas kernels  18.2 us (6%)
  matrix products  14.7 us (5%)
    all_to_all x9, waiting for transfers between devices, exchange(): return lax.all_to_all(parts, axis, 0, 0, tiled=True)  113 us
    all_to_all x4, blocking collectives, exchange(): return lax.all_to_all(parts, axis, 0, 0, tiled=True)  63.2 us
    all_to_all x9, starting transfers between devices, exchange(): return lax.all_to_all(parts, axis, 0, 0, tiled=True)  60.6 us
    unnamed x104, local copies, waits for them, and re-layouts  27.1 us
    pallas_call x13, Pallas kernels, local(): pl.pallas_call(body, out_shape=tuple((jax.ShapeDtypeStruct(s, d) for s, d...  18.2 us
    dot_general x5, matrix products, contract(): lax.dot_general(left, right, (((left_dim,), (right_dim,)), ((), ())), pre...  14.7 us
  transfers between devices with their start and end apart: 9, of which 9 were waited for; matrix products, arithmetic and copies ran while one was open for 7% of the time, Pallas kernels for 0%

profile of v3, /device:TPU:1, one launch (start us, length us, event | category | flops | bytes accessed | tf_op | source)
XLA Modules:
  0.0 306.7 jit_solution(772484276397955919)
XLA Ops:
  0.6 1.5 broadcast_in_dim.48
  2.1 12.8 %all-to-all-start = ((bf16[32,8,576]{2,1,0:T(8,128)(2,1)}), bf16[32,8,576]{2,1,0:T(8,128)(2,1)S(1)}, u32[]{:S(2)}, u32[]{:S(2)}) async-start(bf16[32,8,576]{2,1,0:T(8,128)(2,1)} %broadcast_in_dim.48), calls=%async_computation | async-start | bytes 655360 | tf_op jit(solution)/shard_map/all_to_all | solution.py:100
  15.6 13.8 %all-to-all-done = bf16[32,8,576]{2,1,0:T(8,128)(2,1)S(1)} async-done(((bf16[32,8,576]{2,1,0:T(8,128)(2,1)}), bf16[32,8,576]{2,1,0:T(8,128)(2,1)S(1)}, u32[]{:S(2)}, u32[]{:S(2)}) %all-to-all-start) | async-done | bytes 294944 | tf_op jit(solution)/shard_map/all_to_all | solution.py:100
  29.3 1.2 copy-done.8
  30.6 1.1 copy-done.10
  31.7 1.6 shard_map.145
  33.3 4.1 %all-to-all-start.1 = ((bf16[8,32,1280]{2,1,0:T(8,128)(2,1)}), bf16[8,32,1280]{2,1,0:T(8,128)(2,1)S(1)}, u32[]{:S(2)}, u32[]{:S(2)}) async-start(bf16[8,32,1280]{2,1,0:T(8,128)(2,1)} %bitcast.3), calls=%async_computation.1 | async-start | bytes 1310720 | tf_op jit(solution)/shard_map/all_to_all | solution.py:100
  37.5 8.8 %all-to-all-done.1.refs_0_ = bf16[8,32,1280]{2,1,0:T(8,128)(2,1)S(1)} async-done(((bf16[8,32,1280]{2,1,0:T(8,128)(2,1)}), bf16[8,32,1280]{2,1,0:T(8,128)(2,1)S(1)}, u32[]{:S(2)}, u32[]{:S(2)}) %all-to-all-start.1) | async-done | bytes 655392 | tf_op jit(solution)/shard_map/all_to_all | solution.py:100
  46.3 0.9 shard_map.146
  49.7 5.0 %all-to-all-start.2 = ((bf16[8,32,640]{2,1,0:T(8,128)(2,1)}), bf16[8,32,640]{2,1,0:T(8,128)(2,1)S(1)}, u32[]{:S(2)}, u32[]{:S(2)}) async-start(bf16[8,32,640]{2,1,0:T(8,128)(2,1)} %get-tuple-element.25), calls=%async_computation.2 | async-start | bytes 655360 | tf_op jit(solution)/shard_map/all_to_all | solution.py:100
  54.7 4.0 %fusion.7 = bf16[256,576]{0,1:T(8,128)(2,1)S(1)} fusion(bf16[576,4096]{1,0:T(8,128)(2,1)} %head.3, s32[256]{0:T(256)S(1)} %broadcast_subtract_fusion), kind=kOutput, calls=%fused_computation.13 | convolution fusion | flops 1209155584 | bytes 5014528 | tf_op jit(solution)/shard_map/dot_general | solution.py:20
  58.9 1.9 all-to-all-done.2
  60.8 1.3 shard_map.147
  62.1 6.9 %all-to-all-start.3 = ((bf16[32,8,1280]{2,1,0:T(8,128)(2,1)}), bf16[32,8,1280]{2,1,0:T(8,128)(2,1)S(1)}, u32[]{:S(2)}, u32[]{:S(2)}) async-start(bf16[32,8,1280]{2,1,0:T(8,128)(2,1)} %bitcast.5), calls=%async_computation.3 | async-start | bytes 1310720 | tf_op jit(solution)/shard_map/all_to_all | solution.py:100
  69.0 20.5 %all-to-all-done.3.message = bf16[32,8,1280]{2,1,0:T(8,128)(2,1)S(1)} async-done(((bf16[32,8,1280]{2,1,0:T(8,128)(2,1)}), bf16[32,8,1280]{2,1,0:T(8,128)(2,1)S(1)}, u32[]{:S(2)}, u32[]{:S(2)}) %all-to-all-start.3) | async-done | bytes 655392 | tf_op jit(solution)/shard_map/all_to_all | solution.py:100
  89.6 7.5 %all_to_all.65.refs_1_ = f32[8,8,128]{2,1,0:T(8,128)S(1)} all-to-all(f32[8,8,128]{2,1,0:T(8,128)S(1)} %get-tuple-element.26), channel_id=1, replica_groups=mesh['vocab'=32,'width'=8] {'width'}, dimensions={0} | all-to-all | bytes 65536 | tf_op jit(solution)/shard_map/all_to_all | solution.py:100
  99.1 7.0 %all-to-all-start.5 = ((bf16[32,8,640]{2,1,0:T(8,128)(2,1)}), bf16[32,8,640]{2,1,0:T(8,128)(2,1)S(1)}, u32[]{:S(2)}, u32[]{:S(2)}) async-start(bf16[32,8,640]{2,1,0:T(8,128)(2,1)} %get-tuple-element.28), calls=%async_computation.5 | async-start | bytes 655360 | tf_op jit(solution)/shard_map/all_to_all | solution.py:100
  106.1 14.5 %all-to-all-done.5 = bf16[32,8,640]{2,1,0:T(8,128)(2,1)S(1)} async-done(((bf16[32,8,640]{2,1,0:T(8,128)(2,1)}), bf16[32,8,640]{2,1,0:T(8,128)(2,1)S(1)}, u32[]{:S(2)}, u32[]{:S(2)}) %all-to-all-start.5) | async-done | bytes 327712 | tf_op jit(solution)/shard_map/all_to_all | solution.py:100
  120.7 2.5 copy-done
  123.2 4.3 %shard_map.150 = (bf16[256,4672]{1,0:T(8,128)(2,1)S(1)}, bf16[256,576]{1,0:T(8,128)(2,1)S(1)}) custom-call(bf16[256,640]{1,0:T(8,128)(2,1)S(1)} %bitcast.36, bf16[256,576]{1,0:T(8,128)(2,1)S(1)} %bitcast.45, f32[1,576]{1,0:T(1,128)S(1)} %broadcast_in_dim.50.post_gain.refs_7_, f32[1,576]{1,0:T(1,128)S(1)} %broadcast_in_dim.51.final_gain.refs_8_, ...), custom_call_target="tpu_custom_call" | custom-call | tf_op jit(solution)/shard_map/pallas_call | solution.py:84
  127.5 1.4 copy-done.14
  129.6 3.6 %all-to-all-start.6 = ((bf16[8,32,4672]{2,1,0:T(8,128)(2,1)}), bf16[8,32,4672]{2,1,0:T(8,128)(2,1)S(1)}, u32[]{:S(2)}, u32[]{:S(2)}) async-start(bf16[8,32,4672]{2,1,0:T(8,128)(2,1)} %bitcast.49), calls=%async_computation.6 | async-start | bytes 4849664 | tf_op jit(solution)/shard_map/all_to_all | solution.py:100
  133.4 34.0 %all-to-all-done.6.refs_0_ = bf16[8,32,4672]{2,1,0:T(8,128)(2,1)S(1)} async-done(((bf16[8,32,4672]{2,1,0:T(8,128)(2,1)}), bf16[8,32,4672]{2,1,0:T(8,128)(2,1)S(1)}, u32[]{:S(2)}, u32[]{:S(2)}) %all-to-all-start.6) | async-done | bytes 2392096 | tf_op jit(solution)/shard_map/all_to_all | solution.py:100
  168.1 27.8 %all_to_all.66 = bf16[8,32,4224]{2,1,0:T(8,128)(2,1)S(1)} all-to-all(bf16[8,32,4224]{2,1,0:T(8,128)(2,1)S(1)} %get-tuple-element.30), channel_id=1, replica_groups=mesh['vocab'=32,'width'=8] {'width'}, dimensions={0} | all-to-all | bytes 4325376 | tf_op jit(solution)/shard_map/all_to_all | solution.py:100
  195.9 2.3 copy-done.1
  198.2 4.8 %shard_map.152 = bf16[256,640]{1,0:T(8,128)(2,1)} custom-call(bf16[256,4224]{1,0:T(8,128)(2,1)S(1)} %bitcast.29, bf16[576,4096]{1,0:T(8,128)(2,1)S(1)} %copy-done.1), custom_call_target="tpu_custom_call" | custom-call | tf_op jit(solution)/shard_map/pallas_call | solution.py:84
  203.0 9.0 %all-to-all-start.8 = ((bf16[32,8,640]{2,1,0:T(8,128)(2,1)}), bf16[32,8,640]{2,1,0:T(8,128)(2,1)S(1)}, u32[]{:S(2)}, u32[]{:S(2)}) async-start(bf16[32,8,640]{2,1,0:T(8,128)(2,1)} %bitcast.10), calls=%async_computation.8 | async-start | bytes 655360 | tf_op jit(solution)/shard_map/all_to_all | solution.py:100
  212.1 1.3 broadcast_in_dim.53
  213.4 1.4 reshape.62
  214.8 1.2 dynamic-slice_bitcast_fusion
  216.0 1.3 copy.24.refs_6_
  217.3 9.2 %all-to-all-done.8.refs_0_ = bf16[32,8,640]{2,1,0:T(8,128)(2,1)S(1)} async-done(((bf16[32,8,640]{2,1,0:T(8,128)(2,1)}), bf16[32,8,640]{2,1,0:T(8,128)(2,1)S(1)}, u32[]{:S(2)}, u32[]{:S(2)}) %all-to-all-start.8) | async-done | bytes 327712 | tf_op jit(solution)/shard_map/all_to_all | solution.py:100
  232.4 19.1 %all_to_all.67 = bf16[32,8,640]{2,1,0:T(8,128)(2,1)S(1)} all-to-all(bf16[32,8,640]{2,1,0:T(8,128)(2,1)S(1)} %get-tuple-element.34), channel_id=1, replica_groups=mesh['vocab'=32,'width'=8] {'vocab'}, dimensions={0} | all-to-all | bytes 655360 | tf_op jit(solution)/shard_map/all_to_all | solution.py:100
  252.4 8.9 %all_to_all.68.refs_1_ = bf16[8,32,640]{2,1,0:T(8,128)(2,1)S(1)} all-to-all(bf16[8,32,640]{2,1,0:T(8,128)(2,1)S(1)} %bitcast.50), channel_id=1, replica_groups=mesh['vocab'=32,'width'=8] {'width'}, dimensions={0} | all-to-all | bytes 655360 | tf_op jit(solution)/shard_map/all_to_all | solution.py:100
  261.3 1.0 copy-done.4
  263.1 0.9 copy-done.21
  264.0 0.9 copy-done.23
  267.7 3.5 %all-to-all-start.11 = ((bf16[8,32,1280]{2,1,0:T(8,128)(2,1)}), bf16[8,32,1280]{2,1,0:T(8,128)(2,1)S(1)}, u32[]{:S(2)}, u32[]{:S(2)}) async-start(bf16[8,32,1280]{2,1,0:T(8,128)(2,1)} %copy-done.12), calls=%async_computation.11 | async-start | bytes 1310720 | tf_op jit(solution)/shard_map/all_to_all | solution.py:100
  272.3 4.9 %convolution_convert_fusion = bf16[576,4096]{1,0:T(8,128)(2,1)} fusion(bf16[256,576]{1,0:T(8,128)(2,1)} %copy-done.45, bf16[256,4224]{1,0:T(8,128)(2,1)S(1)} %bitcast.30, f32[256]{0:T(256)S(1)} %get-tuple-element.45, f32[256]{0:T(256)S(1)} %get-tuple-element.44, s32[256]{0:T(256)} %copy-done.51), kind=kOutput, calls=%fused_computation | convolution fusion | flops 1216610304 | bytes 7113728 | tf_op jit(solution)/shard_map/dot_general | solution.py:20
  277.2 1.9 all-to-all-done.11
  279.1 1.1 copy-done.9
  280.2 1.1 copy-done.11
  281.3 1.5 shard_map.156
  282.9 8.6 %all-to-all-start.12 = ((bf16[32,8,640]{2,1,0:T(8,128)(2,1)}), bf16[32,8,640]{2,1,0:T(8,128)(2,1)S(1)}, u32[]{:S(2)}, u32[]{:S(2)}) async-start(bf16[32,8,640]{2,1,0:T(8,128)(2,1)} %bitcast.15), calls=%async_computation.12 | async-start | bytes 655360 | tf_op jit(solution)/shard_map/all_to_all | solution.py:100
  291.5 2.1 convolution_convert_fusion.2
  293.8 1.4 convolution_convert_fusion.3
  295.2 2.4 convolution_convert_fusion.1
  297.6 8.4 %all-to-all-done.12.refs_1_ = bf16[32,8,640]{2,1,0:T(8,128)(2,1)S(1)} async-done(((bf16[32,8,640]{2,1,0:T(8,128)(2,1)}), bf16[32,8,640]{2,1,0:T(8,128)(2,1)S(1)}, u32[]{:S(2)}, u32[]{:S(2)}) %all-to-all-start.12) | async-done | bytes 327712 | tf_op jit(solution)/shard_map/all_to_all | solution.py:100
  (111 shorter events, 19.6 us)
Async XLA Ops:
  0.6 36.8 %copy-start.50 = (s32[256]{0:T(256)S(1)}, s32[256]{0:T(256)}, u32[]{:S(2)}) copy-start(s32[256]{0:T(256)} %param.18) | copy-start | bytes 3076
  2.1 27.2 %all-to-all-start = ((bf16[32,8,576]{2,1,0:T(8,128)(2,1)}), bf16[32,8,576]{2,1,0:T(8,128)(2,1)S(1)}, u32[]{:S(2)}, u32[]{:S(2)}) async-start(bf16[32,8,576]{2,1,0:T(8,128)(2,1)} %broadcast_in_dim.48), calls=%async_computation | async-start | bytes 655360 | tf_op jit(solution)/shard_map/all_to_all | solution.py:100
  15.6 21.9 %copy-start.34 = (f32[1,576]{1,0:T(1,128)}, f32[1,576]{1,0:T(1,128)S(1)}, u32[]{:S(2)}) copy-start(f32[1,576]{1,0:T(1,128)S(1)} %broadcast_in_dim.49.pre_gain.refs_5_) | copy-start | bytes 6916
  29.3 91.4 %copy-start.6 = (bf16[32,8,576]{2,1,0:T(8,128)(2,1)}, bf16[32,8,576]{2,1,0:T(8,128)(2,1)S(1)}, u32[]{:S(2)}) copy-start(bf16[32,8,576]{2,1,0:T(8,128)(2,1)S(1)} %all-to-all-done) | copy-start | bytes 884740
  29.3 1.2 copy-start.8
  30.6 1.1 copy-start.10
  33.3 13.0 %all-to-all-start.1 = ((bf16[8,32,1280]{2,1,0:T(8,128)(2,1)}), bf16[8,32,1280]{2,1,0:T(8,128)(2,1)S(1)}, u32[]{:S(2)}, u32[]{:S(2)}) async-start(bf16[8,32,1280]{2,1,0:T(8,128)(2,1)} %bitcast.3), calls=%async_computation.1 | async-start | bytes 1310720 | tf_op jit(solution)/shard_map/all_to_all | solution.py:100
  37.5 95.8 %copy-start.51 = (s32[256]{0:T(256)}, s32[256]{0:T(256)S(1)}, u32[]{:S(2)}) copy-start(s32[256]{0:T(256)S(1)} %broadcast_subtract_fusion) | copy-start | bytes 3076
  49.7 11.1 %all-to-all-start.2 = ((bf16[8,32,640]{2,1,0:T(8,128)(2,1)}), bf16[8,32,640]{2,1,0:T(8,128)(2,1)S(1)}, u32[]{:S(2)}, u32[]{:S(2)}) async-start(bf16[8,32,640]{2,1,0:T(8,128)(2,1)} %get-tuple-element.25), calls=%async_computation.2 | async-start | bytes 655360 | tf_op jit(solution)/shard_map/all_to_all | solution.py:100
  54.7 6.1 %copy-start.2 = (bf16[576,576]{1,0:T(8,128)(2,1)S(1)}, bf16[576,576]{1,0:T(8,128)(2,1)}, u32[]{:S(2)}) copy-start(bf16[576,576]{1,0:T(8,128)(2,1)} %down_weight.5) | copy-start | bytes 1990660
  54.7 14.3 %copy-start.46 = (f32[576]{0:T(1024)S(1)}, f32[576]{0:T(1024)}, u32[]{:S(2)}) copy-start(f32[576]{0:T(1024)} %param.12) | copy-start | bytes 6916
  54.7 34.8 %copy-start.15 = (bf16[8,576]{1,0:T(8,128)(2,1)S(1)}, bf16[8,576]{1,0:T(8,128)(2,1)}, u32[]{:S(2)}) copy-start(bf16[8,576]{1,0:T(8,128)(2,1)} %refs_3_.3) | copy-start | bytes 27652
  58.7 47.4 %copy-start.47 = (f32[576]{0:T(1024)S(1)}, f32[576]{0:T(1024)}, u32[]{:S(2)}) copy-start(f32[576]{0:T(1024)} %param.13) | copy-start | bytes 6916
  62.1 27.4 %all-to-all-start.3 = ((bf16[32,8,1280]{2,1,0:T(8,128)(2,1)}), bf16[32,8,1280]{2,1,0:T(8,128)(2,1)S(1)}, u32[]{:S(2)}, u32[]{:S(2)}) async-start(bf16[32,8,1280]{2,1,0:T(8,128)(2,1)} %bitcast.5), calls=%async_computation.3 | async-start | bytes 1310720 | tf_op jit(solution)/shard_map/all_to_all | solution.py:100
  69.0 60.6 %copy-start.30 = (f32[1,576]{1,0:T(1,128)}, f32[1,576]{1,0:T(1,128)S(1)}, u32[]{:S(2)}) copy-start(f32[1,576]{1,0:T(1,128)S(1)} %broadcast_in_dim.50.post_gain.refs_7_) | copy-start | bytes 6916
  89.6 7.5 %copy-start.36 = (f32[8,576]{1,0:T(8,128)}, f32[8,576]{1,0:T(8,128)S(1)}, u32[]{:S(2)}) copy-start(f32[8,576]{1,0:T(8,128)S(1)} %get-tuple-element.31.refs_1_) | copy-start | bytes 55300
  89.6 8.3 %copy-start.28 = (f32[8,576]{1,0:T(8,128)}, f32[8,576]{1,0:T(8,128)S(1)}, u32[]{:S(2)}) copy-start(f32[8,576]{1,0:T(8,128)S(1)} %get-tuple-element.27.refs_3_.refs_2_) | copy-start | bytes 55300
  99.1 21.6 %all-to-all-start.5 = ((bf16[32,8,640]{2,1,0:T(8,128)(2,1)}), bf16[32,8,640]{2,1,0:T(8,128)(2,1)S(1)}, u32[]{:S(2)}, u32[]{:S(2)}) async-start(bf16[32,8,640]{2,1,0:T(8,128)(2,1)} %get-tuple-element.28), calls=%async_computation.5 | async-start | bytes 655360 | tf_op jit(solution)/shard_map/all_to_all | solution.py:100
  106.1 23.5 %copy-start.32 = (f32[1,576]{1,0:T(1,128)}, f32[1,576]{1,0:T(1,128)S(1)}, u32[]{:S(2)}) copy-start(f32[1,576]{1,0:T(1,128)S(1)} %broadcast_in_dim.51.final_gain.refs_8_) | copy-start | bytes 6916
  120.7 8.9 %copy-start.3 = (bf16[32,8,640]{2,1,0:T(8,128)(2,1)}, bf16[32,8,640]{2,1,0:T(8,128)(2,1)S(1)}, u32[]{:S(2)}) copy-start(bf16[32,8,640]{2,1,0:T(8,128)(2,1)S(1)} %all-to-all-done.5) | copy-start | bytes 983044
  120.7 2.5 copy-start
  127.4 1.4 copy-start.14
  129.6 37.8 %all-to-all-start.6 = ((bf16[8,32,4672]{2,1,0:T(8,128)(2,1)}), bf16[8,32,4672]{2,1,0:T(8,128)(2,1)S(1)}, u32[]{:S(2)}, u32[]{:S(2)}) async-start(bf16[8,32,4672]{2,1,0:T(8,128)(2,1)} %bitcast.49), calls=%async_computation.6 | async-start | bytes 4849664 | tf_op jit(solution)/shard_map/all_to_all | solution.py:100
  168.0 27.8 %copy-start.26 = (f32[32,576]{1,0:T(8,128)}, f32[32,576]{1,0:T(8,128)S(1)}, u32[]{:S(2)}) copy-start(f32[32,576]{1,0:T(8,128)S(1)} %get-tuple-element.36.refs_2_) | copy-start | bytes 221188
  195.9 2.3 copy-start.1
  203.0 23.5 %all-to-all-start.8 = ((bf16[32,8,640]{2,1,0:T(8,128)(2,1)}), bf16[32,8,640]{2,1,0:T(8,128)(2,1)S(1)}, u32[]{:S(2)}, u32[]{:S(2)}) async-start(bf16[32,8,640]{2,1,0:T(8,128)(2,1)} %bitcast.10), calls=%async_computation.8 | async-start | bytes 655360 | tf_op jit(solution)/shard_map/all_to_all | solution.py:100
  227.3 0.7 copy-start.29
  229.3 0.7 copy-start.37
  232.4 28.8 %copy-start.38 = (f32[8,576]{1,0:T(8,128)}, f32[8,576]{1,0:T(8,128)S(1)}, u32[]{:S(2)}) copy-start(f32[8,576]{1,0:T(8,128)S(1)} %get-tuple-element.41.refs_2_) | copy-start | bytes 55300
  251.5 20.8 %copy-start.13 = (bf16[32,8,640]{2,1,0:T(8,128)(2,1)}, bf16[32,8,640]{2,1,0:T(8,128)(2,1)S(1)}, u32[]{:S(2)}) copy-start(bf16[32,8,640]{2,1,0:T(8,128)(2,1)S(1)} %all_to_all.67) | copy-start | bytes 983044
  261.3 1.0 copy-start.4
  262.2 0.9 copy-start.19
  263.1 0.9 copy-start.21
  264.0 0.9 copy-start.23
  264.9 0.9 copy-start.25
  265.8 0.9 copy-start.27
  266.9 0.8 copy-start.12
  267.7 11.3 %all-to-all-start.11 = ((bf16[8,32,1280]{2,1,0:T(8,128)(2,1)}), bf16[8,32,1280]{2,1,0:T(8,128)(2,1)S(1)}, u32[]{:S(2)}, u32[]{:S(2)}) async-start(bf16[8,32,1280]{2,1,0:T(8,128)(2,1)} %copy-done.12), calls=%async_computation.11 | async-start | bytes 1310720 | tf_op jit(solution)/shard_map/all_to_all | solution.py:100
  272.3 19.2 %copy-start.7 = (bf16[32,8,576]{2,1,0:T(8,128)(2,1)S(1)}, bf16[32,8,576]{2,1,0:T(8,128)(2,1)}, u32[]{:S(2)}) copy-start(bf16[32,8,576]{2,1,0:T(8,128)(2,1)} %copy-done.6) | copy-start | bytes 884740
  277.2 16.4 %copy-start.5 = (bf16[32,8,640]{2,1,0:T(8,128)(2,1)S(1)}, bf16[32,8,640]{2,1,0:T(8,128)(2,1)}, u32[]{:S(2)}) copy-start(bf16[32,8,640]{2,1,0:T(8,128)(2,1)} %copy-done.3) | copy-start | bytes 983044
  279.1 1.1 copy-start.9
  280.2 1.1 copy-start.11
  281.3 12.5 %copy-start.48 = (f32[576]{0:T(1024)S(1)}, f32[576]{0:T(1024)}, u32[]{:S(2)}) copy-start(f32[576]{0:T(1024)} %param.11) | copy-start | bytes 6916
  281.3 12.5 %copy-start.49 = (f32[256]{0:T(256)S(1)}, f32[256]{0:T(256)}, u32[]{:S(2)}) copy-start(f32[256]{0:T(256)} %rsqrt_reduce_fusion) | copy-start | bytes 3076
  281.3 24.6 %copy-start.17 = (bf16[8,576]{1,0:T(8,128)(2,1)S(1)}, bf16[8,576]{1,0:T(8,128)(2,1)}, u32[]{:S(2)}) copy-start(bf16[8,576]{1,0:T(8,128)(2,1)} %refs_3_.3) | copy-start | bytes 27652
  281.3 24.6 %copy-start.35 = (f32[1,576]{1,0:T(1,128)S(1)}, f32[1,576]{1,0:T(1,128)}, u32[]{:S(2)}) copy-start(f32[1,576]{1,0:T(1,128)} %copy-done.34) | copy-start | bytes 6916
  281.3 24.6 %copy-start.39 = (f32[8,576]{1,0:T(8,128)S(1)}, f32[8,576]{1,0:T(8,128)}, u32[]{:S(2)}) copy-start(f32[8,576]{1,0:T(8,128)} %copy-done.38) | copy-start | bytes 55300
  282.9 23.1 %all-to-all-start.12 = ((bf16[32,8,640]{2,1,0:T(8,128)(2,1)}), bf16[32,8,640]{2,1,0:T(8,128)(2,1)S(1)}, u32[]{:S(2)}, u32[]{:S(2)}) async-start(bf16[32,8,640]{2,1,0:T(8,128)(2,1)} %bitcast.15), calls=%async_computation.12 | async-start | bytes 655360 | tf_op jit(solution)/shard_map/all_to_all | solution.py:100
  (13 other events, 8.5 us)

commit v4 on v3

v4 whole, which is shorter than its diff:
```python
import math

import jax
import jax.numpy as jnp
from jax import lax
from jax.experimental import pallas as pl
from jax.experimental.pallas import tpu as pltpu
from jax.sharding import PartitionSpec as P

CAP = 30.0
EPS = 1e-06
ROOT_TWO_PI = math.sqrt(2.0 / math.pi)
BF16 = jnp.bfloat16
F32 = jnp.float32
LANES = 128
CHUNK = 512


def contract(left, right, left_dim, right_dim):
    return lax.dot_general(
        left, right, (((left_dim,), (right_dim,)), ((), ())), preferred_element_type=F32
    )


def gelu_parts(value):
    square = value * value
    bent = jnp.tanh(ROOT_TWO_PI * value * (1.0 + 0.044715 * square))
    half = 0.5 * (1.0 + bent)
    slope = half + 0.5 * value * (1.0 - bent * bent) * ROOT_TWO_PI * (1.0 + 3.0 * 0.044715 * square)
    return value * half, slope


def padded(width):
    return width // LANES * LANES + LANES


def pick(tile, at):
    lane = lax.broadcasted_iota(jnp.int32, tile.shape, 1)
    return jnp.sum(jnp.where((lane == at) | (lane == at + 1), tile, 0.0), axis=1, keepdims=True)


def read_stats(tile, width, count):
    return [pick(tile, width % LANES + 2 * i) for i in range(count)]


def tail_of(width):
    return slice(width // LANES * LANES, padded(width))


def with_stats(tile, width, stats):
    lane = lax.broadcasted_iota(jnp.int32, tile.shape, 1)
    at = width % LANES
    tile = jnp.where(lane < at, tile, 0.0)
    for i, stat in enumerate(stats):
        high = stat.astype(BF16).astype(F32)
        tile = jnp.where(lane == at + 2 * i, high, tile)
        tile = jnp.where(lane == at + 2 * i + 1, stat - high, tile)
    return tile.astype(BF16)


def put(ref, block, stats):
    width = block.shape[1]
    ref[:, :width] = block
    tail = tail_of(width)
    ref[:, tail] = with_stats(ref[:, tail].astype(F32), width, stats)


def put_copies(ref, block, stats):
    put(ref.at[0], block, stats)
    whole = ref[0]
    for i in range(1, ref.shape[0]):
        ref[i] = whole


def summed(ref, columns):
    total = ref[0, :, columns].astype(F32)
    for i in range(1, ref.shape[0]):
        total = total + ref[i, :, columns].astype(F32)
    return total


def local(body, outs, *args):
    return pl.pallas_call(
        body,
        out_shape=tuple(jax.ShapeDtypeStruct(s, d) for s, d in outs),
        in_specs=[pl.BlockSpec(memory_space=pltpu.VMEM) for _ in args],
        out_specs=tuple(pl.BlockSpec(memory_space=pltpu.VMEM) for _ in outs),
        compiler_params=pltpu.CompilerParams(vmem_limit_bytes=16 << 20),
    )(*args)


def exchange(parts, axis):
    size = lax.axis_size(axis)
    if parts.ndim == 2:
        parts = parts.reshape(size, parts.shape[0] // size, parts.shape[1])
    return lax.all_to_all(parts, axis, 0, 0, tiled=True)


def flat(message):
    return message.reshape(message.shape[0] * message.shape[1], message.shape[2])


def gate_step(
    inputs, gains, gate_weight, up_weight, target_rows, ids, weights, out, *kept
):
    for source, copy in zip((target_rows, ids, weights, gains), kept):
        copy[...] = source[...]
    width = gate_weight.shape[1]
    values = inputs[...].astype(F32)
    scaled = (values * gains[0:1]).astype(BF16)
    squares = jnp.sum(values * values, axis=1, keepdims=True)
    put(out, contract(scaled, gate_weight[...], 1, 0).astype(BF16), [squares])
    out[:, padded(width) : padded(width) + width] = contract(
        scaled, up_weight[...], 1, 0
    ).astype(BF16)


def active_step(model, width, message, gate, upward, gelu_gate, gelu_slope, out):
    (squares,) = read_stats(summed(message, tail_of(width)), width, 1)
    scale = lax.rsqrt(squares / model + EPS)
    gate_value = summed(message, slice(0, width)) * scale
    up_value = summed(message, slice(padded(width), padded(width) + width)) * scale
    value, slope = gelu_parts(gate_value)
    gate[...] = gate_value
    upward[...] = up_value
    gelu_gate[...] = value
    gelu_slope[...] = slope
    put_copies(out, (value * up_value).astype(BF16), [squares])


def branch_step(message, down_weight, target_rows, out):
    width = down_weight.shape[0]
    depth = down_weight.shape[1]
    out[:, :depth] = contract(message[:, :width], down_weight[...], 1, 0).astype(BF16)
    out[:, padded(depth) : padded(depth) + depth] = target_rows[...]


def norm_step(message, inputs, gains, branch, target, out):
    width = branch.shape[1]
    value = summed(message, slice(0, width))
    branch[...] = value
    target[...] = summed(message, slice(padded(width), padded(width) + width))
    bent = value * gains[1:2]
    own = inputs[...].astype(F32)
    stats = [
        jnp.sum(x, axis=1, keepdims=True) for x in (value * value, own * bent, bent * bent, own * own)
    ]
    lane = lax.broadcasted_iota(jnp.int32, out.shape[1:], 1)
    tile = jnp.zeros(out.shape[1:], F32)
    for i, stat in enumerate(stats):
        tile = jnp.where(lane == i, stat, tile)
    for i in range(out.shape[0]):
        out[i] = tile


def scale_step(model, message, branch, scales, out):
    tile = message[0]
    for i in range(1, message.shape[0]):
        tile = tile + message[i]
    lane = lax.broadcasted_iota(jnp.int32, tile.shape, 1)
    square, cross, bent, own = [
        jnp.sum(jnp.where(lane == i, tile, 0.0), axis=1, keepdims=True) for i in range(4)
    ]
    post = lax.rsqrt(square / model + EPS)
    final_squares = own + post * (2.0 * cross + post * bent)
    final = lax.rsqrt(jnp.maximum(final_squares, 0.0) / model + EPS)
    pre = lax.rsqrt(own / model + EPS)
    scales[...] = jnp.where(lane == 0, post, jnp.where(lane == 1, final, pre))
    put_copies(out, branch[...].astype(BF16), [post, final])


def logit_step(copies_n, message, inputs, gains, down_weight, head, out, final):
    width = final.shape[1]
    branch = message[:, :width]
    post, scale = read_stats(message[:, tail_of(width)].astype(F32), width, 2)
    resid = inputs[...].astype(F32) + branch.astype(F32) * post * gains[1:2]
    final[...] = (resid * scale * gains[2:3]).astype(BF16)
    vocab = head.shape[1]
    hidden = down_weight.shape[0]
    out[:, vocab : vocab + hidden] = contract(branch, down_weight[...], 1, 1).astype(BF16)
    tail = tail_of(vocab + hidden)
    out[:, tail] = with_stats(out[:, tail].astype(F32), vocab + hidden, [post / copies_n])
    for i in range(0, vocab, CHUNK):
        columns = slice(i, i + CHUNK)
        out[:, columns] = contract(final[...], head[:, columns], 1, 0).astype(BF16)


def soft_step(vocab, hidden, message, ids, out, branch_down):
    rows = message.shape[1]
    step = 256
    others = jnp.zeros((rows, step), F32)
    cross = jnp.zeros((rows, step), F32)
    target = jnp.zeros((rows, step), F32)
    lane = lax.broadcasted_iota(jnp.int32, (rows, step), 1)
    for i in range(vocab // step):
        columns = slice(i * step, (i + 1) * step)
        logits = summed(message, columns)
        hits = lane == ids[...] - i * step
        bent = jnp.tanh(logits / CAP)
        raised = jnp.where(hits, 0.0, jnp.exp(CAP * bent - CAP))
        sloped = raised * (1.0 - bent * bent)
        others = others + raised
        cross = cross + sloped * logits
        target = target + jnp.where(hits, logits, 0.0)
        part = sloped.astype(BF16)
        for j in range(out.shape[0]):
            out[j, :, columns] = part
    stats = [jnp.sum(x, axis=1, keepdims=True) for x in (others, cross, target)]
    tile = with_stats(jnp.zeros((rows, LANES), F32), vocab, stats)
    for j in range(out.shape[0]):
        out[j, :, vocab : vocab + LANES] = tile
    branch_down[...] = summed(message, slice(vocab, vocab + padded(hidden)))


def row_step(message, head, out):
    vocab = head.shape[1]
    total = contract(message[:, :vocab], head[...], 1, 1)
    put(
        out,
        total.astype(BF16),
        read_stats(message[:, vocab : vocab + LANES].astype(F32), vocab, 3),
    )


def resid_step(
    model, message, target_rows, branch, inputs, scales, weights, gains, grad_resid, out
):
    width = branch.shape[1]
    others, cross, logit = read_stats(summed(message, tail_of(width)), width, 3)
    bent = jnp.tanh(logit / CAP)
    target = CAP * bent
    total = others + jnp.exp(target - CAP)
    logprob = target - CAP - jnp.log(total)
    spread = weights[...] / total
    pull = -spread * others * (1.0 - bent * bent)
    post = scales[:, 0:1]
    final = scales[:, 1:2]
    post_gain = gains[1:2]
    final_gain = gains[2:3]
    grad_final = spread * summed(message, slice(0, width)) + pull * target_rows[...]
    back_final = (spread * cross + pull * logit) / final
    value = branch[...]
    resid = inputs[...].astype(F32) + post * value * post_gain
    grad = final * grad_final * final_gain - resid * (
        final * final * final * back_final / model
    )
    grad_resid[...] = grad
    weighted = grad * post_gain
    back_post = jnp.sum(weighted * value, axis=1, keepdims=True)
    put_copies(
        out,
        (post * weighted).astype(BF16),
        [spread, pull, weights[...] * logprob, back_post],
    )


def down_step(message, down_weight, out, loss):
    width = down_weight.shape[1]
    _, _, score, back_post = read_stats(message[:, tail_of(width)].astype(F32), width, 4)
    put(
        out,
        contract(message[:, :width], down_weight[...], 1, 1).astype(BF16),
        [back_post],
    )
    loss[...] = -jnp.sum(score, axis=0, keepdims=True) / message.shape[0]


def hidden_step(model, message, branch_down, gate, upward, gelu_gate, gelu_slope, out):
    rows, width = gate.shape
    (back_post,) = read_stats(summed(message, tail_of(width)), width, 1)
    (post,) = read_stats(branch_down[:, tail_of(width)], width, 1)
    grad = summed(message, slice(0, width)) - branch_down[:, :width] * (
        post * post * post * back_post / model
    )
    gate_in = (grad * upward[...] * gelu_slope[...]).astype(BF16)
    up_in = (grad * gelu_gate[...]).astype(BF16)
    back = jnp.sum(
        gate_in.astype(F32) * gate[...] + up_in.astype(F32) * upward[...], axis=1, keepdims=True
    )
    start = padded(width)
    put(out.at[0], gate_in, [back, back_post])
    out[0, :, start : start + width] = up_in
    whole = out[0]
    for i in range(1, out.shape[0]):
        out[i] = whole


def normed_step(model, message, gate_weight, up_weight, active, branch, weighted, out, rates):
    width, hidden = gate_weight.shape
    start = padded(hidden)
    total = contract(message[:, :hidden], gate_weight[...], 1, 1) + contract(
        message[:, start : start + hidden], up_weight[...], 1, 1
    )
    back, back_post = read_stats(message[:, tail_of(hidden)].astype(F32), hidden, 2)
    put(out, total.astype(BF16), [back])
    (squares,) = read_stats(active[:, tail_of(hidden)].astype(F32), hidden, 1)
    (post,) = read_stats(branch[:, tail_of(width)].astype(F32), width, 1)
    spread, pull = read_stats(weighted[:, tail_of(width)].astype(F32), width, 2)
    lane = lax.broadcasted_iota(jnp.int32, rates.shape, 1)
    tile = jnp.where(lane == 0, spread, pull)
    tile = jnp.where(lane == 2, post * post * post * back_post / model, tile)
    rates[...] = jnp.where(lane == 3, lax.rsqrt(squares / model + EPS), tile)


def last_step(model, message, grad_resid, inputs, scales, gains, out):
    width = out.shape[1]
    scale = scales[:, 2:3]
    (back,) = read_stats(summed(message, tail_of(width)), width, 1)
    weighted = summed(message, slice(0, width)) * gains[0:1]
    out[...] = (
        grad_resid[...] + scale * weighted - inputs[...].astype(F32) * (scale * scale * back / model)
    ).astype(BF16)


def shards(
    hidden,
    pre_gain,
    post_gain,
    final_gain,
    gate_weight,
    up_weight,
    down_weight,
    head_weight,
    token_ids,
    rewards,
):
    tok_dev, width = hidden.shape
    tokens = token_ids.shape[0]
    rows_n = lax.axis_size("vocab")
    cols_n = lax.axis_size("width")
    model = width * cols_n
    ff = gate_weight.shape[1]
    vocab = head_weight.shape[1]
    sub = tokens // cols_n
    vocab_index = lax.axis_index("vocab")
    width_index = lax.axis_index("width")
    gains = jnp.stack([pre_gain, post_gain, final_gain])

    weights = jnp.repeat(rewards, tokens // rewards.shape[0])
    own_weights = lax.dynamic_slice_in_dim(weights, vocab_index * tok_dev, tok_dev, 0)[:, None]
    ids = token_ids - vocab_index * vocab
    hits = jnp.arange(vocab, dtype=jnp.int32)[None, :] == ids[:, None]
    sub_ids = lax.dynamic_slice_in_dim(ids, width_index * sub, sub, 0)[:, None]
    target_part = contract(hits.astype(BF16), head_weight, 1, 1).astype(BF16)
    inputs = flat(exchange(jnp.broadcast_to(hidden[None], (rows_n, tok_dev, width)), "vocab"))
    message, target_part, sub_ids, own_weights, gains = local(
        gate_step,
        [
            ((tokens, padded(ff) * 2), BF16),
            ((tokens, width), BF16),
            ((sub, 1), jnp.int32),
            ((tok_dev, 1), F32),
            ((3, width), F32),
        ],
        inputs,
        gains,
        gate_weight,
        up_weight,
        target_part,
        sub_ids,
        own_weights,
    )
    gate, upward, gelu_gate, gelu_slope, message = local(
        lambda *refs: active_step(model, ff, *refs),
        [((sub, ff), F32)] * 4 + [((cols_n, sub, padded(ff)), BF16)],
        exchange(message, "width"),
    )
    active = flat(exchange(message, "width"))
    (message,) = local(
        branch_step, [((tokens, padded(width) * 2), BF16)], active, down_weight, target_part
    )
    branch, target_rows, message = local(
        norm_step,
        [((tok_dev, width), F32)] * 2 + [((cols_n, tok_dev, LANES), F32)],
        exchange(message, "vocab"),
        hidden,
        gains,
    )
    scales, message = local(
        lambda *refs: scale_step(model, *refs),
        [((tok_dev, LANES), F32), ((rows_n, tok_dev, padded(width)), BF16)],
        exchange(message, "width"),
        branch,
    )
    branch_all = flat(exchange(message, "vocab"))
    message, final = local(
        lambda *refs: logit_step(cols_n, *refs),
        [((tokens, vocab + padded(ff)), BF16), ((tokens, width), BF16)],
        branch_all,
        inputs,
        gains,
        down_weight,
        head_weight,
    )
    message, branch_down = local(
        lambda *refs: soft_step(vocab, ff, *refs),
        [((cols_n, sub, vocab + LANES), BF16), ((sub, padded(ff)), F32)],
        exchange(message, "width"),
        sub_ids,
    )
    sloped = flat(exchange(message, "width"))
    (message,) = local(
        row_step,
        [((tokens, padded(width)), BF16)],
        sloped,
        head_weight,
    )
    grad_resid, message = local(
        lambda *refs: resid_step(model, *refs),
        [((tok_dev, width), F32), ((rows_n, tok_dev, padded(width)), BF16)],
        exchange(message, "vocab"),
        target_rows,
        branch,
        hidden,
        scales,
        own_weights,
        gains,
    )
    weighted = flat(exchange(message, "vocab"))
    message, loss = local(
        down_step,
        [((tokens, padded(ff)), BF16), ((1, 1), F32)],
        weighted,
        down_weight,
    )
    (message,) = local(
        lambda *refs: hidden_step(model, *refs),
        [((cols_n, sub, padded(ff) * 2), BF16)],
        exchange(message, "width"),
        branch_down,
        gate,
        upward,
        gelu_gate,
        gelu_slope,
    )
    grads_in = flat(exchange(message, "width"))
    message, rates = local(
        lambda *refs: normed_step(model, *refs),
        [((tokens, padded(width)), BF16), ((tokens, LANES), F32)],
        grads_in,
        gate_weight,
        up_weight,
        active,
        branch_all,
        weighted,
    )
    (grad_hidden,) = local(
        lambda *refs: last_step(model, *refs),
        [((tok_dev, width), BF16)],
        exchange(message, "vocab"),
        grad_resid,
        hidden,
        scales,
        gains,
    )

    spread, pull, along, scale_pre = [rates[:, i : i + 1] for i in range(4)]
    delta = (spread * sloped[:, :vocab].astype(F32) + jnp.where(hits, pull, 0.0)).astype(BF16)
    grad_head = contract(final, delta, 0, 0).astype(BF16)
    grad_branch = (
        weighted[:, :width].astype(F32) - branch_all[:, :width].astype(F32) * along
    ).astype(BF16)
    grad_down = contract(active[:, :ff], grad_branch, 0, 0).astype(BF16)
    normed = (inputs.astype(F32) * scale_pre * pre_gain).astype(BF16)
    grad_gate = contract(normed, grads_in[:, :ff], 0, 0).astype(BF16)
    grad_up = contract(normed, grads_in[:, padded(ff) : padded(ff) + ff], 0, 0).astype(BF16)
    return (grad_hidden, grad_gate, grad_up, grad_down, grad_head, loss[0, 0])


def solution(mesh):
    return jax.shard_map(
        shards,
        mesh=mesh,
        in_specs=(
            P("vocab", "width"),
            P("width"),
            P("width"),
            P("width"),
            P("width", "vocab"),
            P("width", "vocab"),
            P("vocab", "width"),
            P("width", "vocab"),
            P(),
            P(),
        ),
        out_specs=(
            P("vocab", "width"),
            P("width", "vocab"),
            P("width", "vocab"),
            P("vocab", "width"),
            P("width", "vocab"),
            P(),
        ),
        check_vma=False,
    )
```

time: 309 us -> 267 us (0.86)
  blocking collectives: 63.2 us -> 201 us
  waiting for transfers between devices: 113 us -> 11.4 us
  starting transfers between devices: 60.6 us -> 21.4 us
  local copies, waits for them, and re-layouts: 34.9 us -> 6.28 us
  Pallas kernels: 18.2 us -> 10.4 us
    all_to_all x4 -> x11, blocking collectives: 63.2 us -> 201 us  [exchange(): return lax.all_to_all(parts, axis, 0, 0, tiled=True)]
    all_to_all x9 -> x2, waiting for transfers between devices: 113 us -> 11.4 us  [exchange(): return lax.all_to_all(parts, axis, 0, 0, tiled=True)]
    all_to_all x9 -> x2, starting transfers between devices: 60.6 us -> 21.4 us  [exchange(): return lax.all_to_all(parts, axis, 0, 0, tiled=True)]
    unnamed x104 -> x26, local copies, waits for them, and re-layouts: 27.1 us -> 0.06 us
    pallas_call x13, Pallas kernels: 18.2 us -> 10.4 us  [local(): pl.pallas_call(body, out_shape=tuple((jax.ShapeDtypeStruct(s, d) for s, d...]
  transfers between devices with their start and end apart: 9 -> 2, of which waited for: 9 -> 2; matrix products, arithmetic and copies ran while one was open for 7% -> 7% of each run, Pallas kernels for 0% -> 0%
where the time goes in v4:
time: 267 us; the launch traced here: 266 us
  blocking collectives  201 us (75%)
  starting transfers between devices  21.4 us (8%)
  matrix products  13.8 us (5%)
  waiting for transfers between devices  11.4 us (4%)
  Pallas kernels  10.4 us (4%)
  local copies, waits for them, and re-layouts  6.28 us (2%)
    all_to_all x11, blocking collectives, exchange(): return lax.all_to_all(parts, axis, 0, 0, tiled=True)  201 us
    all_to_all x2, starting transfers between devices, exchange(): return lax.all_to_all(parts, axis, 0, 0, tiled=True)  21.4 us
    dot_general x5, matrix products, contract(): lax.dot_general(left, right, (((left_dim,), (right_dim,)), ((), ())), pre...  13.8 us
    all_to_all x2, waiting for transfers between devices, exchange(): return lax.all_to_all(parts, axis, 0, 0, tiled=True)  11.4 us
    pallas_call x13, Pallas kernels, local(): pl.pallas_call(body, out_shape=tuple((jax.ShapeDtypeStruct(s, d) for s, d...  10.4 us
  transfers between devices with their start and end apart: 2, of which 2 were waited for; matrix products, arithmetic and copies ran while one was open for 7% of the time, Pallas kernels for 0%

profile of v4, /device:TPU:1, one launch (start us, length us, event | category | flops | bytes accessed | tf_op | source)
XLA Modules:
  0.0 265.9 jit_solution(4074649627258697283)
XLA Ops:
  0.6 1.5 broadcast_in_dim.32
  2.1 12.8 %all-to-all-start = ((bf16[32,8,576]{2,1,0:T(8,128)(2,1)}), bf16[32,8,576]{2,1,0:T(8,128)(2,1)S(1)}, u32[]{:S(2)}, u32[]{:S(2)}) async-start(bf16[32,8,576]{2,1,0:T(8,128)(2,1)} %broadcast_in_dim.32), calls=%async_computation | async-start | bytes 655360 | tf_op jit(solution)/shard_map/all_to_all | solution.py:96
  14.9 0.7 broadcast_in_dim.34
  15.6 0.1 reshape.55
  15.7 0.7 broadcast_subtract_fusion
  16.4 0.1 dynamic-slice_bitcast_fusion.1
  16.4 0.1 dynamic-slice_bitcast_fusion
  16.5 0.7 stack.13
  17.2 0.7 stack.14
  17.9 0.7 stack.12
  18.6 0.1 copy.23.ids
  18.7 0.1 copy.24.weights
  18.7 4.8 %fusion.7 = bf16[256,576]{0,1:T(8,128)(2,1)} fusion(bf16[576,4096]{1,0:T(8,128)(2,1)} %head.1, s32[256]{0:T(256)S(1)} %broadcast_subtract_fusion), kind=kOutput, calls=%fused_computation.13 | convolution fusion | flops 1209155584 | bytes 5014528 | tf_op jit(solution)/shard_map/dot_general | solution.py:20
  23.5 1.2 copy.22.target_rows
  24.8 0.0 copy-start.8
  24.8 4.5 %all-to-all-done = bf16[32,8,576]{2,1,0:T(8,128)(2,1)S(1)} async-done(((bf16[32,8,576]{2,1,0:T(8,128)(2,1)}), bf16[32,8,576]{2,1,0:T(8,128)(2,1)S(1)}, u32[]{:S(2)}, u32[]{:S(2)}) %all-to-all-start) | async-done | bytes 294944 | tf_op jit(solution)/shard_map/all_to_all | solution.py:96
  29.3 0.8 shard_map.145
  30.1 12.7 %all_to_all.65.refs_0_ = bf16[8,32,1280]{2,1,0:T(8,128)(2,1)S(1)} all-to-all(bf16[8,32,1280]{2,1,0:T(8,128)(2,1)S(1)} %bitcast.48), channel_id=1, replica_groups=mesh['vocab'=32,'width'=8] {'width'}, dimensions={0} | all-to-all | bytes 1310720 | tf_op jit(solution)/shard_map/all_to_all | solution.py:96
  42.8 0.2 shard_map.146
  43.0 9.7 %all_to_all.66 = bf16[8,32,640]{2,1,0:T(8,128)(2,1)S(1)} all-to-all(bf16[8,32,640]{2,1,0:T(8,128)(2,1)S(1)} %get-tuple-element.32), channel_id=1, replica_groups=mesh['vocab'=32,'width'=8] {'width'}, dimensions={0} | all-to-all | bytes 655360 | tf_op jit(solution)/shard_map/all_to_all | solution.py:96
  52.7 0.5 shard_map.147
  53.2 30.2 %all_to_all.67.message = bf16[32,8,1280]{2,1,0:T(8,128)(2,1)S(1)} all-to-all(bf16[32,8,1280]{2,1,0:T(8,128)(2,1)S(1)} %bitcast.42), channel_id=1, replica_groups=mesh['vocab'=32,'width'=8] {'vocab'}, dimensions={0} | all-to-all | bytes 1310720 | tf_op jit(solution)/shard_map/all_to_all | solution.py:96
  83.4 0.1 shard_map.148
  83.5 7.4 %all_to_all.68.refs_0_ = f32[8,8,128]{2,1,0:T(8,128)S(1)} all-to-all(f32[8,8,128]{2,1,0:T(8,128)S(1)} %get-tuple-element.35), channel_id=1, replica_groups=mesh['vocab'=32,'width'=8] {'width'}, dimensions={0} | all-to-all | bytes 65536 | tf_op jit(solution)/shard_map/all_to_all | solution.py:96
  90.9 0.1 shard_map.149
  91.1 20.5 %all_to_all.69 = bf16[32,8,640]{2,1,0:T(8,128)(2,1)S(1)} all-to-all(bf16[32,8,640]{2,1,0:T(8,128)(2,1)S(1)} %get-tuple-element.37), channel_id=1, replica_groups=mesh['vocab'=32,'width'=8] {'vocab'}, dimensions={0} | all-to-all | bytes 655360 | tf_op jit(solution)/shard_map/all_to_all | solution.py:96
  111.6 2.2 shard_map.150
  113.8 30.8 %all_to_all.70.refs_0_ = bf16[8,32,4736]{2,1,0:T(8,128)(2,1)S(1)} all-to-all(bf16[8,32,4736]{2,1,0:T(8,128)(2,1)S(1)} %bitcast.46), channel_id=1, replica_groups=mesh['vocab'=32,'width'=8] {'width'}, dimensions={0} | all-to-all | bytes 4849664 | tf_op jit(solution)/shard_map/all_to_all | solution.py:96
  144.6 0.7 shard_map.151
  145.3 26.8 %all_to_all.71 = bf16[8,32,4224]{2,1,0:T(8,128)(2,1)S(1)} all-to-all(bf16[8,32,4224]{2,1,0:T(8,128)(2,1)S(1)} %get-tuple-element.40), channel_id=1, replica_groups=mesh['vocab'=32,'width'=8] {'width'}, dimensions={0} | all-to-all | bytes 4325376 | tf_op jit(solution)/shard_map/all_to_all | solution.py:96
  172.1 1.9 shard_map.152
  174.0 0.0 copy-start.6
  174.0 24.1 %all_to_all.72.refs_0_ = bf16[32,8,640]{2,1,0:T(8,128)(2,1)S(1)} all-to-all(bf16[32,8,640]{2,1,0:T(8,128)(2,1)S(1)} %bitcast.47), channel_id=1, replica_groups=mesh['vocab'=32,'width'=8] {'vocab'}, dimensions={0} | all-to-all | bytes 655360 | tf_op jit(solution)/shard_map/all_to_all | solution.py:96
  198.1 0.4 shard_map.153
  198.4 19.1 %all_to_all.73 = bf16[32,8,640]{2,1,0:T(8,128)(2,1)S(1)} all-to-all(bf16[32,8,640]{2,1,0:T(8,128)(2,1)S(1)} %get-tuple-element.44), channel_id=1, replica_groups=mesh['vocab'=32,'width'=8] {'vocab'}, dimensions={0} | all-to-all | bytes 655360 | tf_op jit(solution)/shard_map/all_to_all | solution.py:96
  217.5 0.9 shard_map.154
  218.4 8.9 %all_to_all.74.refs_0_ = bf16[8,32,640]{2,1,0:T(8,128)(2,1)S(1)} all-to-all(bf16[8,32,640]{2,1,0:T(8,128)(2,1)S(1)} %bitcast.50), channel_id=1, replica_groups=mesh['vocab'=32,'width'=8] {'width'}, dimensions={0} | all-to-all | bytes 655360 | tf_op jit(solution)/shard_map/all_to_all | solution.py:96
  227.3 0.2 shard_map.155
  227.5 10.8 %all_to_all.75 = bf16[8,32,1280]{2,1,0:T(8,128)(2,1)S(1)} all-to-all(bf16[8,32,1280]{2,1,0:T(8,128)(2,1)S(1)} %shard_map.155), channel_id=1, replica_groups=mesh['vocab'=32,'width'=8] {'width'}, dimensions={0} | all-to-all | bytes 1310720 | tf_op jit(solution)/shard_map/all_to_all | solution.py:96
  238.3 0.8 shard_map.156
  239.2 0.3 slice_reduce_fusion.1
  239.5 1.4 convolution_convert_fusion.1
  240.9 8.7 %all-to-all-start.12 = ((bf16[32,8,640]{2,1,0:T(8,128)(2,1)}), bf16[32,8,640]{2,1,0:T(8,128)(2,1)}, u32[]{:S(2)}, u32[]{:S(2)}) async-start(bf16[32,8,640]{2,1,0:T(8,128)(2,1)} %bitcast.49), calls=%async_computation.12 | async-start | bytes 655360 | tf_op jit(solution)/shard_map/all_to_all | solution.py:96
  249.6 1.4 convolution_convert_fusion.2
  251.0 1.4 convolution_convert_fusion.3
  252.4 4.8 %convolution_convert_fusion = bf16[576,4096]{1,0:T(8,128)(2,1)} fusion(bf16[256,576]{1,0:T(8,128)(2,1)} %copy-done.9, bf16[256,4224]{1,0:T(8,128)(2,1)S(1)} %bitcast.30, f32[256]{0:T(256)S(1)} %get-tuple-element.57, f32[256]{0:T(256)S(1)} %get-tuple-element.56, s32[256]{0:T(256)S(1)} %broadcast_subtract_fusion), kind=kOutput, calls=%fused_computation | convolution fusion | flops 1216610304 | bytes 7113728 | tf_op jit(solution)/shard_map/dot_general | solution.py:20
  257.2 6.9 %all-to-all-done.12.refs_0_ = bf16[32,8,640]{2,1,0:T(8,128)(2,1)} async-done(((bf16[32,8,640]{2,1,0:T(8,128)(2,1)}), bf16[32,8,640]{2,1,0:T(8,128)(2,1)}, u32[]{:S(2)}, u32[]{:S(2)}) %all-to-all-start.12) | async-done | bytes 327712 | tf_op jit(solution)/shard_map/all_to_all | solution.py:96
  264.1 1.8 shard_map.157
  (26 shorter events, 0.1 us)
Async XLA Ops:
  2.1 27.2 %all-to-all-start = ((bf16[32,8,576]{2,1,0:T(8,128)(2,1)}), bf16[32,8,576]{2,1,0:T(8,128)(2,1)S(1)}, u32[]{:S(2)}, u32[]{:S(2)}) async-start(bf16[32,8,576]{2,1,0:T(8,128)(2,1)} %broadcast_in_dim.32), calls=%async_computation | async-start | bytes 655360 | tf_op jit(solution)/shard_map/all_to_all | solution.py:96
  18.7 10.6 %copy-start.3 = (bf16[576,576]{1,0:T(8,128)(2,1)S(1)}, bf16[576,576]{1,0:T(8,128)(2,1)}, u32[]{:S(2)}) copy-start(bf16[576,576]{1,0:T(8,128)(2,1)} %refs_1_.1) | copy-start | bytes 1990660
  18.7 10.6 %copy-start.5 = (bf16[576,576]{1,0:T(8,128)(2,1)S(1)}, bf16[576,576]{1,0:T(8,128)(2,1)}, u32[]{:S(2)}) copy-start(bf16[576,576]{1,0:T(8,128)(2,1)} %refs_2_.2) | copy-start | bytes 1990660
  18.7 92.9 %slice-start = ((s8[4718592]{0:T(1024)(128)(4,1)}), s8[524288]{0:T(1024)(128)(4,1)S(1)}, s32[]{:S(2)}) async-start(s8[4718592]{0:T(1024)(128)(4,1)} %bitcast.27), calls=%async_computation.13 | async-start | bytes 1048576
  23.5 29.2 %copy-start = (bf16[576,576]{1,0:T(8,128)(2,1)S(1)}, bf16[576,576]{1,0:T(8,128)(2,1)}, u32[]{:S(2)}) copy-start(bf16[576,576]{1,0:T(8,128)(2,1)} %down_weight.3) | copy-start | bytes 1990660
  24.8 58.6 %copy-start.8 = (bf16[8,576]{1,0:T(8,128)(2,1)S(1)}, bf16[8,576]{1,0:T(8,128)(2,1)}, u32[]{:S(2)}) copy-start(bf16[8,576]{1,0:T(8,128)(2,1)} %refs_2_.3) | copy-start | bytes 27652
  29.3 82.3 %copy-start.1 = (bf16[32,8,576]{2,1,0:T(8,128)(2,1)}, bf16[32,8,576]{2,1,0:T(8,128)(2,1)S(1)}, u32[]{:S(2)}) copy-start(bf16[32,8,576]{2,1,0:T(8,128)(2,1)S(1)} %all-to-all-done) | copy-start | bytes 884740
  29.3 82.3 %slice-start.1 = ((s8[4718592]{0:T(1024)(128)(4,1)}), s8[4194304]{0:T(1024)(128)(4,1)S(1)}, s32[]{:S(2)}) async-start(s8[4718592]{0:T(1024)(128)(4,1)} %bitcast.27), calls=%async_computation.14 | async-start | bytes 8388608
  113.8 31.5 %copy-start.9 = (bf16[256,576]{1,0:T(8,128)(2,1)}, bf16[256,576]{1,0:T(8,128)(2,1)S(1)}, u32[]{:S(2)}) copy-start(bf16[256,576]{1,0:T(8,128)(2,1)S(1)} %get-tuple-element.54) | copy-start | bytes 884740
  174.0 64.3 %copy-start.4 = (bf16[576,576]{1,0:T(8,128)(2,1)S(1)}, bf16[576,576]{1,0:T(8,128)(2,1)}, u32[]{:S(2)}) copy-start(bf16[576,576]{1,0:T(8,128)(2,1)} %refs_1_.1) | copy-start | bytes 1990660
  174.0 64.3 %copy-start.6 = (bf16[576,576]{1,0:T(8,128)(2,1)S(1)}, bf16[576,576]{1,0:T(8,128)(2,1)}, u32[]{:S(2)}) copy-start(bf16[576,576]{1,0:T(8,128)(2,1)} %refs_2_.2) | copy-start | bytes 1990660
  227.3 22.3 %copy-start.2 = (bf16[32,8,576]{2,1,0:T(8,128)(2,1)S(1)}, bf16[32,8,576]{2,1,0:T(8,128)(2,1)}, u32[]{:S(2)}) copy-start(bf16[32,8,576]{2,1,0:T(8,128)(2,1)} %copy-done.1) | copy-start | bytes 884740
  227.3 22.3 %copy-start.10 = (f32[576]{0:T(1024)S(1)}, f32[576]{0:T(1024)}, u32[]{:S(2)}) copy-start(f32[576]{0:T(1024)} %param.11) | copy-start | bytes 6916
  239.1 1.7 copy-start.7
  240.9 23.2 %all-to-all-start.12 = ((bf16[32,8,640]{2,1,0:T(8,128)(2,1)}), bf16[32,8,640]{2,1,0:T(8,128)(2,1)}, u32[]{:S(2)}, u32[]{:S(2)}) async-start(bf16[32,8,640]{2,1,0:T(8,128)(2,1)} %bitcast.49), calls=%async_computation.12 | async-start | bytes 655360 | tf_op jit(solution)/shard_map/all_to_all | solution.py:96

commit v5 on v4

--- a/solution.py
+++ b/solution.py
@@ -5,6 +5,7 @@
 from jax import lax
 from jax.experimental import pallas as pl
 from jax.experimental.pallas import tpu as pltpu
+from jax.sharding import Mesh
 from jax.sharding import PartitionSpec as P
 
 CAP = 30.0
@@ -55,14 +56,20 @@
         high = stat.astype(BF16).astype(F32)
         tile = jnp.where(lane == at + 2 * i, high, tile)
         tile = jnp.where(lane == at + 2 * i + 1, stat - high, tile)
-    return tile.astype(BF16)
+    return tile
 
 
 def put(ref, block, stats):
     width = block.shape[1]
     ref[:, :width] = block
     tail = tail_of(width)
-    ref[:, tail] = with_stats(ref[:, tail].astype(F32), width, stats)
+    ref[:, tail] = with_stats(ref[:, tail].astype(F32), width, stats).astype(ref.dtype)
+
+
+def put_halves(mine, theirs, block, stats):
+    half = mine.shape[0]
+    put(mine, block[:half], [stat[:half] for stat in stats])
+    put(theirs, block[half:].astype(BF16), [stat[half:] for stat in stats])
 
 
 def put_copies(ref, block, stats):
@@ -79,12 +86,16 @@
     return total
 
 
-def local(body, outs, *args):
+def local(body, outs, *args, hbm=(), scratch=()):
     return pl.pallas_call(
         body,
         out_shape=tuple(jax.ShapeDtypeStruct(s, d) for s, d in outs),
-        in_specs=[pl.BlockSpec(memory_space=pltpu.VMEM) for _ in args],
+        in_specs=[
+            pl.BlockSpec(memory_space=pltpu.HBM if i in hbm else pltpu.VMEM)
+            for i in range(len(args))
+        ],
         out_specs=tuple(pl.BlockSpec(memory_space=pltpu.VMEM) for _ in outs),
+        scratch_shapes=scratch,
         compiler_params=pltpu.CompilerParams(vmem_limit_bytes=16 << 20),
     )(*args)
 
@@ -100,9 +111,47 @@
     return message.reshape(message.shape[0] * message.shape[1], message.shape[2])
 
 
+def rejoin(near, far, whole):
+    half = near.shape[0]
+    whole[:half] = near[...]
+    whole[half:] = far[...]
+
+
+def pair_step(width, count, mine, theirs, *rest):
+    *held, out = rest
+    for source, copy in zip(held[: len(held) // 2], held[len(held) // 2 :]):
+        copy[...] = source[...]
+    out[...] = (mine[...] + theirs[...].astype(F32)).astype(BF16)
+    if count:
+        tail = tail_of(width)
+        tile = mine[:, tail] + theirs[:, tail].astype(F32)
+        out[:, tail] = with_stats(tile, width, read_stats(tile, width, count)).astype(BF16)
+
+
+def swap(values):
+    return lax.ppermute(values, "core", [(0, 1), (1, 0)])
+
+
+def gathered(copies):
+    near = flat(exchange(copies, "rows"))
+    return near, swap(near)
+
+
+def reduced(mine, theirs, width, count, *held):
+    *held, message = local(
+        lambda *refs: pair_step(width, count, *refs),
+        [*((x.shape, x.dtype) for x in held), (mine.shape, BF16)],
+        mine,
+        swap(theirs),
+        *held,
+    )
+    return (exchange(message, "rows"), *held)
+
+
 def gate_step(
-    inputs, gains, gate_weight, up_weight, target_rows, ids, weights, out, *kept
+    near, far, gains, gate_weight, up_weight, target_rows, ids, weights, out, inputs, *kept
 ):
+    rejoin(near, far, inputs)
     for source, copy in zip((target_rows, ids, weights, gains), kept):
         copy[...] = source[...]
     width = gate_weight.shape[1]
@@ -128,18 +177,22 @@
     put_copies(out, (value * up_value).astype(BF16), [squares])
 
 
-def branch_step(message, down_weight, target_rows, out):
-    width = down_weight.shape[0]
-    depth = down_weight.shape[1]
-    out[:, :depth] = contract(message[:, :width], down_weight[...], 1, 0).astype(BF16)
-    out[:, padded(depth) : padded(depth) + depth] = target_rows[...]
+def branch_step(message, down_weight, target_rows, mine, theirs):
+    hidden, width = down_weight.shape
+    half = mine.shape[0]
+    block = contract(message[:, :hidden], down_weight[...], 1, 0)
+    mine[:, :width] = block[:half]
+    theirs[:, :width] = block[half:].astype(BF16)
+    mine[:, width : 2 * width] = target_rows[:half].astype(F32)
+    theirs[:, width : 2 * width] = target_rows[half:]
 
 
 def norm_step(message, inputs, gains, branch, target, out):
     width = branch.shape[1]
-    value = summed(message, slice(0, width))
+    both = summed(message, slice(0, 2 * width))
+    value = both[:, :width]
     branch[...] = value
-    target[...] = summed(message, slice(padded(width), padded(width) + width))
+    target[...] = both[:, width:]
     bent = value * gains[1:2]
     own = inputs[...].astype(F32)
     stats = [
@@ -169,20 +222,31 @@
     put_copies(out, branch[...].astype(BF16), [post, final])
 
 
-def logit_step(copies_n, message, inputs, gains, down_weight, head, out, final):
+def logit_step(
+    copies_n, near, far, inputs, gains, down_weight, head, out, final, message, buffer, sems
+):
+    vocab = head.shape[1]
+    copies = [
+        pltpu.make_async_copy(head.at[:, pl.ds(i * CHUNK, CHUNK)], buffer.at[i], sems.at[i])
+        for i in range(vocab // CHUNK)
+    ]
+    for copy in copies:
+        copy.start()
+    rejoin(near, far, message)
     width = final.shape[1]
     branch = message[:, :width]
     post, scale = read_stats(message[:, tail_of(width)].astype(F32), width, 2)
     resid = inputs[...].astype(F32) + branch.astype(F32) * post * gains[1:2]
     final[...] = (resid * scale * gains[2:3]).astype(BF16)
-    vocab = head.shape[1]
     hidden = down_weight.shape[0]
     out[:, vocab : vocab + hidden] = contract(branch, down_weight[...], 1, 1).astype(BF16)
     tail = tail_of(vocab + hidden)
-    out[:, tail] = with_stats(out[:, tail].astype(F32), vocab + hidden, [post / copies_n])
-    for i in range(0, vocab, CHUNK):
-        columns = slice(i, i + CHUNK)
-        out[:, columns] = contract(final[...], head[:, columns], 1, 0).astype(BF16)
+    tile = with_stats(out[:, tail].astype(F32), vocab + hidden, [post / copies_n])
+    out[:, tail] = tile.astype(BF16)
+    for i, copy in enumerate(copies):
+        copy.wait()
+        columns = slice(i * CHUNK, (i + 1) * CHUNK)
+        out[:, columns] = contract(final[...], buffer[i], 1, 0).astype(BF16)
 
 
 def soft_step(vocab, hidden, message, ids, out, branch_down):
@@ -206,20 +270,17 @@
         for j in range(out.shape[0]):
             out[j, :, columns] = part
     stats = [jnp.sum(x, axis=1, keepdims=True) for x in (others, cross, target)]
-    tile = with_stats(jnp.zeros((rows, LANES), F32), vocab, stats)
+    tile = with_stats(jnp.zeros((rows, LANES), F32), vocab, stats).astype(BF16)
     for j in range(out.shape[0]):
         out[j, :, vocab : vocab + LANES] = tile
     branch_down[...] = summed(message, slice(vocab, vocab + padded(hidden)))
 
 
-def row_step(message, head, out):
+def row_step(message, head, mine, theirs):
     vocab = head.shape[1]
     total = contract(message[:, :vocab], head[...], 1, 1)
-    put(
-        out,
-        total.astype(BF16),
-        read_stats(message[:, vocab : vocab + LANES].astype(F32), vocab, 3),
-    )
+    stats = read_stats(message[:, vocab : vocab + LANES].astype(F32), vocab, 3)
+    put_halves(mine, theirs, total, stats)
 
 
 def resid_step(
@@ -254,7 +315,8 @@
     )
 
 
-def down_step(message, down_weight, out, loss):
+def down_step(near, far, down_weight, out, message, loss):
+    rejoin(near, far, message)
     width = down_weight.shape[1]
     _, _, score, back_post = read_stats(message[:, tail_of(width)].astype(F32), width, 4)
     put(
@@ -285,14 +347,16 @@
         out[i] = whole
 
 
-def normed_step(model, message, gate_weight, up_weight, active, branch, weighted, out, rates):
+def normed_step(
+    model, message, gate_weight, up_weight, active, branch, weighted, mine, theirs, rates
+):
     width, hidden = gate_weight.shape
     start = padded(hidden)
     total = contract(message[:, :hidden], gate_weight[...], 1, 1) + contract(
         message[:, start : start + hidden], up_weight[...], 1, 1
     )
     back, back_post = read_stats(message[:, tail_of(hidden)].astype(F32), hidden, 2)
-    put(out, total.astype(BF16), [back])
+    put_halves(mine, theirs, total, [back])
     (squares,) = read_stats(active[:, tail_of(hidden)].astype(F32), hidden, 1)
     (post,) = read_stats(branch[:, tail_of(width)].astype(F32), width, 1)
     spread, pull = read_stats(weighted[:, tail_of(width)].astype(F32), width, 2)
@@ -326,33 +390,39 @@
 ):
     tok_dev, width = hidden.shape
     tokens = token_ids.shape[0]
-    rows_n = lax.axis_size("vocab")
+    rows_n = lax.axis_size("rows")
     cols_n = lax.axis_size("width")
     model = width * cols_n
     ff = gate_weight.shape[1]
     vocab = head_weight.shape[1]
     sub = tokens // cols_n
-    vocab_index = lax.axis_index("vocab")
+    half = tokens // 2
+    core = lax.axis_index("core")
+    vocab_index = lax.axis_index("rows") * 2 + core
     width_index = lax.axis_index("width")
     gains = jnp.stack([pre_gain, post_gain, final_gain])
 
     weights = jnp.repeat(rewards, tokens // rewards.shape[0])
     own_weights = lax.dynamic_slice_in_dim(weights, vocab_index * tok_dev, tok_dev, 0)[:, None]
-    ids = token_ids - vocab_index * vocab
+    ids = token_ids.reshape(rows_n, 2, tok_dev)
+    ids = jnp.where(core == 0, jnp.swapaxes(ids, 0, 1), jnp.swapaxes(ids[:, ::-1], 0, 1))
+    ids = ids.reshape(tokens) - vocab_index * vocab
     hits = jnp.arange(vocab, dtype=jnp.int32)[None, :] == ids[:, None]
     sub_ids = lax.dynamic_slice_in_dim(ids, width_index * sub, sub, 0)[:, None]
     target_part = contract(hits.astype(BF16), head_weight, 1, 1).astype(BF16)
-    inputs = flat(exchange(jnp.broadcast_to(hidden[None], (rows_n, tok_dev, width)), "vocab"))
-    message, target_part, sub_ids, own_weights, gains = local(
+    near, far = gathered(jnp.broadcast_to(hidden[None], (rows_n, tok_dev, width)))
+    message, inputs, target_part, sub_ids, own_weights, gains = local(
         gate_step,
         [
             ((tokens, padded(ff) * 2), BF16),
+            ((tokens, width), BF16),
             ((tokens, width), BF16),
             ((sub, 1), jnp.int32),
             ((tok_dev, 1), F32),
             ((3, width), F32),
         ],
-        inputs,
+        near,
+        far,
         gains,
         gate_weight,
         up_weight,
@@ -366,13 +436,17 @@
         exchange(message, "width"),
     )
     active = flat(exchange(message, "width"))
-    (message,) = local(
-        branch_step, [((tokens, padded(width) * 2), BF16)], active, down_weight, target_part
+    mine, theirs = local(
+        branch_step,
+        [((half, width * 2), F32), ((half, width * 2), BF16)],
+        active,
+        down_weight,
+        target_part,
     )
     branch, target_rows, message = local(
         norm_step,
         [((tok_dev, width), F32)] * 2 + [((cols_n, tok_dev, LANES), F32)],
-        exchange(message, "vocab"),
+        *reduced(mine, theirs, width * 2, 0),
         hidden,
         gains,
     )
@@ -382,15 +456,25 @@
         exchange(message, "width"),
         branch,
     )
-    branch_all = flat(exchange(message, "vocab"))
-    message, final = local(
+    near, far = gathered(message)
+    message, final, branch_all = local(
         lambda *refs: logit_step(cols_n, *refs),
-        [((tokens, vocab + padded(ff)), BF16), ((tokens, width), BF16)],
-        branch_all,
+        [
+            ((tokens, vocab + padded(ff)), BF16),
+            ((tokens, width), BF16),
+            ((tokens, padded(width)), BF16),
+        ],
+        near,
+        far,
         inputs,
         gains,
         down_weight,
-        head_weight,
+        pltpu.with_memory_space_constraint(head_weight, pltpu.HBM),
+        hbm=(5,),
+        scratch=(
+            pltpu.VMEM((vocab // CHUNK, width, CHUNK), BF16),
+            pltpu.SemaphoreType.DMA((vocab // CHUNK,)),
+        ),
     )
     message, branch_down = local(
         lambda *refs: soft_step(vocab, ff, *refs),
@@ -399,16 +483,12 @@
         sub_ids,
     )
     sloped = flat(exchange(message, "width"))
-    (message,) = local(
-        row_step,
-        [((tokens, padded(width)), BF16)],
-        sloped,
-        head_weight,
-    )
+    halves = [((half, padded(width)), F32), ((half, padded(width)), BF16)]
+    mine, theirs = local(row_step, halves, sloped, head_weight)
     grad_resid, message = local(
         lambda *refs: resid_step(model, *refs),
         [((tok_dev, width), F32), ((rows_n, tok_dev, padded(width)), BF16)],
-        exchange(message, "vocab"),
+        *reduced(mine, theirs, width, 3),
         target_rows,
         branch,
         hidden,
@@ -416,11 +496,12 @@
         own_weights,
         gains,
     )
-    weighted = flat(exchange(message, "vocab"))
-    message, loss = local(
+    near, far = gathered(message)
+    message, weighted, loss = local(
         down_step,
-        [((tokens, padded(ff)), BF16), ((1, 1), F32)],
-        weighted,
+        [((tokens, padded(ff)), BF16), ((tokens, padded(width)), BF16), ((1, 1), F32)],
+        near,
+        far,
         down_weight,
     )
     (message,) = local(
@@ -434,9 +515,9 @@
         gelu_slope,
     )
     grads_in = flat(exchange(message, "width"))
-    message, rates = local(
+    mine, theirs, rates = local(
         lambda *refs: normed_step(model, *refs),
-        [((tokens, padded(width)), BF16), ((tokens, LANES), F32)],
+        [*halves, ((tokens, LANES), F32)],
         grads_in,
         gate_weight,
         up_weight,
@@ -444,10 +525,11 @@
         branch_all,
         weighted,
     )
+    message, rates = reduced(mine, theirs, width, 1, rates)
     (grad_hidden,) = local(
         lambda *refs: last_step(model, *refs),
         [((tok_dev, width), BF16)],
-        exchange(message, "vocab"),
+        message,
         grad_resid,
         hidden,
         scales,
@@ -468,27 +550,31 @@
 
 
 def solution(mesh):
+    devices = mesh.devices
+    vocab = ("rows", "core")
     return jax.shard_map(
         shards,
-        mesh=mesh,
+        mesh=Mesh(
+            devices.reshape(devices.shape[0] // 2, 2, devices.shape[1]), (*vocab, "width")
+        ),
         in_specs=(
-            P("vocab", "width"),
+            P(vocab, "width"),
             P("width"),
             P("width"),
             P("width"),
-            P("width", "vocab"),
-            P("width", "vocab"),
-            P("vocab", "width"),
-            P("width", "vocab"),
+            P("width", vocab),
+            P("width", vocab),
+            P(vocab, "width"),
+            P("width", vocab),
             P(),
             P(),
         ),
         out_specs=(
-            P("vocab", "width"),
-            P("width", "vocab"),
-            P("width", "vocab"),
-            P("vocab", "width"),
-            P("width", "vocab"),
+            P(vocab, "width"),
+            P("width", vocab),
+            P("width", vocab),
+            P(vocab, "width"),
+            P("width", vocab),
             P(),
         ),
         check_vma=False,

time: 267 us -> 244 us (0.914)
  blocking collectives: 201 us -> 169 us
  starting transfers between devices: 21.4 us -> 32.7 us
    all_to_all x11, blocking collectives: 201 us -> 169 us  [exchange(): return lax.all_to_all(parts, axis, 0, 0, tiled=True)]
    ppermute x0 -> x6, starting transfers between devices: none -> 17.3 us  [swap(): return lax.ppermute(values, 'core', [(0, 1), (1, 0)])]
    all_to_all x2, waiting for transfers between devices: 11.4 us -> 4.81 us  [exchange(): return lax.all_to_all(parts, axis, 0, 0, tiled=True)]
    all_to_all x2, starting transfers between devices: 21.4 us -> 15.4 us  [exchange(): return lax.all_to_all(parts, axis, 0, 0, tiled=True)]
    ppermute x0 -> x6, waiting for transfers between devices: none -> 5.82 us  [swap(): return lax.ppermute(values, 'core', [(0, 1), (1, 0)])]
    pallas_call x13 -> x16, Pallas kernels: 10.4 us -> 12.1 us  [local(): pl.pallas_call(body, out_shape=tuple((jax.ShapeDtypeStruct(s, d) for s, d...]
  transfers between devices with their start and end apart: 2 -> 8, of which waited for: 2 -> 8; matrix products, arithmetic and copies ran while one was open for 7% -> 6% of each run, Pallas kernels for 0% -> 0%
where the time goes in v5:
time: 244 us; the launch traced here: 243 us
  blocking collectives  169 us (69%)
  starting transfers between devices  32.7 us (13%)
  matrix products  13.2 us (5%)
  Pallas kernels  12.1 us (5%)
  waiting for transfers between devices  10.6 us (4%)
  local copies, waits for them, and re-layouts  4.14 us (2%)
    all_to_all x11, blocking collectives, exchange(): return lax.all_to_all(parts, axis, 0, 0, tiled=True)  169 us
    ppermute x6, starting transfers between devices, swap(): return lax.ppermute(values, 'core', [(0, 1), (1, 0)])  17.3 us
    all_to_all x2, starting transfers between devices, exchange(): return lax.all_to_all(parts, axis, 0, 0, tiled=True)  15.4 us
    dot_general x5, matrix products, contract(): lax.dot_general(left, right, (((left_dim,), (right_dim,)), ((), ())), pre...  13.2 us
    pallas_call x16, Pallas kernels, local(): pl.pallas_call(body, out_shape=tuple((jax.ShapeDtypeStruct(s, d) for s, d...  12.1 us
    ppermute x6, waiting for transfers between devices, swap(): return lax.ppermute(values, 'core', [(0, 1), (1, 0)])  5.82 us
  transfers between devices with their start and end apart: 8, of which 8 were waited for; matrix products, arithmetic and copies ran while one was open for 6% of the time, Pallas kernels for 0%

profile of v5, /device:TPU:1, one launch (start us, length us, event | category | flops | bytes accessed | tf_op | source)
XLA Modules:
  0.0 242.9 jit_solution(8657529810935322379)
XLA Ops:
  0.6 1.4 broadcast_in_dim.32
  2.0 11.7 %all-to-all-start = ((bf16[16,8,576]{2,1,0:T(8,128)(2,1)}), bf16[16,8,576]{2,1,0:T(8,128)(2,1)S(1)}, u32[]{:S(2)}, u32[]{:S(2)}) async-start(bf16[16,8,576]{2,1,0:T(8,128)(2,1)} %broadcast_in_dim.32), calls=%async_computation | async-start | bytes 327680 | tf_op jit(solution)/shard_map/all_to_all | solution.py:107
  13.8 0.8 reshape.65
  14.8 4.0 %fusion.7 = bf16[256,576]{0,1:T(8,128)(2,1)S(1)} fusion(bf16[576,4096]{1,0:T(8,128)(2,1)} %head.1, s32[256]{0:T(256)S(1)} %sub.22), kind=kOutput, calls=%fused_computation.13 | convolution fusion | flops 1209155584 | bytes 5014528 | tf_op jit(solution)/shard_map/dot_general | solution.py:21
  19.1 3.6 %all-to-all-done = bf16[16,8,576]{2,1,0:T(8,128)(2,1)S(1)} async-done(((bf16[16,8,576]{2,1,0:T(8,128)(2,1)}), bf16[16,8,576]{2,1,0:T(8,128)(2,1)S(1)}, u32[]{:S(2)}, u32[]{:S(2)}) %all-to-all-start) | async-done | bytes 147488 | tf_op jit(solution)/shard_map/all_to_all | solution.py:107
  22.7 2.3 collective-permute-start
  25.3 0.2 copy.24.target_rows
  25.6 0.5 collective-permute-done.far
  26.1 0.8 shard_map.145
  26.9 14.3 %all_to_all.65.refs_0_ = bf16[8,32,1280]{2,1,0:T(8,128)(2,1)S(1)} all-to-all(bf16[8,32,1280]{2,1,0:T(8,128)(2,1)S(1)} %bitcast.38), channel_id=1, replica_groups=mesh['rows'=16,'core'=2,'width'=8] {'width'}, dimensions={0} | all-to-all | bytes 1310720 | tf_op jit(solution)/shard_map/all_to_all | solution.py:107
  41.3 0.2 shard_map.146
  41.5 9.3 %all_to_all.66 = bf16[8,32,640]{2,1,0:T(8,128)(2,1)S(1)} all-to-all(bf16[8,32,640]{2,1,0:T(8,128)(2,1)S(1)} %get-tuple-element.42), channel_id=1, replica_groups=mesh['rows'=16,'core'=2,'width'=8] {'width'}, dimensions={0} | all-to-all | bytes 655360 | tf_op jit(solution)/shard_map/all_to_all | solution.py:107
  50.8 0.5 shard_map.147
  51.3 3.0 %collective-permute-start.1 = (bf16[128,1152]{1,0:T(8,128)(2,1)S(1)}, bf16[128,1152]{1,0:T(8,128)(2,1)S(1)}, u32[]{:S(2)}, u32[]{:S(2)}) collective-permute-start(bf16[128,1152]{1,0:T(8,128)(2,1)S(1)} %get-tuple-element.45), channel_id=1, source_target_pairs={{0,8},{8,0},{1,9},{9,1},{2,10},{10,2},{3,11},{11,3},{4,12},{12,4},... | collective-permute-start | bytes 884744 | tf_op jit(solution)/shard_map/ppermute | solution.py:132
  54.3 1.2 collective-permute-done.1.refs_1_
  55.5 15.8 %all_to_all.67.message = bf16[16,8,1152]{2,1,0:T(8,128)(2,1)S(1)} all-to-all(bf16[16,8,1152]{2,1,0:T(8,128)(2,1)S(1)} %bitcast.32), channel_id=1, replica_groups=mesh['rows'=16,'core'=2,'width'=8] {'rows'}, dimensions={0} | all-to-all | bytes 589824 | tf_op jit(solution)/shard_map/all_to_all | solution.py:107
  71.5 7.5 %all_to_all.68.refs_0_ = f32[8,8,128]{2,1,0:T(8,128)S(1)} all-to-all(f32[8,8,128]{2,1,0:T(8,128)S(1)} %get-tuple-element.47), channel_id=1, replica_groups=mesh['rows'=16,'core'=2,'width'=8] {'width'}, dimensions={0} | all-to-all | bytes 65536 | tf_op jit(solution)/shard_map/all_to_all | solution.py:107
  79.0 14.3 %all_to_all.69 = bf16[16,8,640]{2,1,0:T(8,128)(2,1)S(1)} all-to-all(bf16[16,8,640]{2,1,0:T(8,128)(2,1)S(1)} %get-tuple-element.49), channel_id=1, replica_groups=mesh['rows'=16,'core'=2,'width'=8] {'rows'}, dimensions={0} | all-to-all | bytes 327680 | tf_op jit(solution)/shard_map/all_to_all | solution.py:107
  93.4 3.6 %collective-permute-start.2 = (bf16[128,640]{1,0:T(8,128)(2,1)S(1)}, bf16[128,640]{1,0:T(8,128)(2,1)S(1)}, u32[]{:S(2)}, u32[]{:S(2)}) collective-permute-start(bf16[128,640]{1,0:T(8,128)(2,1)S(1)} %bitcast.35), channel_id=1, source_target_pairs={{0,8},{8,0},{1,9},{9,1},{2,10},{10,2},{3,11},{11,3},{4,12},{12,4},... | collective-permute-start | bytes 491528 | tf_op jit(solution)/shard_map/ppermute | solution.py:132
  97.0 1.0 collective-permute-done.2.refs_1_
  98.0 4.5 %shard_map.151 = (bf16[256,4736]{1,0:T(8,128)(2,1)S(1)}, bf16[256,576]{1,0:T(8,128)(2,1)S(1)}, bf16[256,640]{1,0:T(8,128)(2,1)S(1)}) custom-call(bf16[128,640]{1,0:T(8,128)(2,1)S(1)} %bitcast.36, bf16[128,640]{1,0:T(8,128)(2,1)S(1)} %collective-permute-done.2.refs_1_, bf16[256,576]{1,0:T(8,128)(2,1)S(1)} %get-tuple-element.50.refs_2_, ...), custom_call_target="tpu_custom_call" | custom-call | tf_op jit(solution)/shard_map/pallas_call | solution.py:90
  102.6 0.7 copy-done.13
  103.3 32.5 %all_to_all.70.refs_0_ = bf16[8,32,4736]{2,1,0:T(8,128)(2,1)S(1)} all-to-all(bf16[8,32,4736]{2,1,0:T(8,128)(2,1)S(1)} %bitcast.31), channel_id=1, replica_groups=mesh['rows'=16,'core'=2,'width'=8] {'width'}, dimensions={0} | all-to-all | bytes 4849664 | tf_op jit(solution)/shard_map/all_to_all | solution.py:107
  135.7 0.7 shard_map.152
  136.4 28.2 %all_to_all.71 = bf16[8,32,4224]{2,1,0:T(8,128)(2,1)S(1)} all-to-all(bf16[8,32,4224]{2,1,0:T(8,128)(2,1)S(1)} %get-tuple-element.53), channel_id=1, replica_groups=mesh['rows'=16,'core'=2,'width'=8] {'width'}, dimensions={0} | all-to-all | bytes 4325376 | tf_op jit(solution)/shard_map/all_to_all | solution.py:107
  164.6 1.9 shard_map.153
  166.5 3.0 %collective-permute-start.3 = (bf16[128,640]{1,0:T(8,128)(2,1)S(1)}, bf16[128,640]{1,0:T(8,128)(2,1)S(1)}, u32[]{:S(2)}, u32[]{:S(2)}) collective-permute-start(bf16[128,640]{1,0:T(8,128)(2,1)S(1)} %get-tuple-element.55), channel_id=1, source_target_pairs={{0,8},{8,0},{1,9},{9,1},{2,10},{10,2},{3,11},{11,3},{4,12},{12,4},... | collective-permute-start | bytes 491528 | tf_op jit(solution)/shard_map/ppermute | solution.py:132
  169.5 1.0 collective-permute-done.3.refs_1_
  170.7 11.9 %all_to_all.72.refs_0_ = bf16[16,8,640]{2,1,0:T(8,128)(2,1)S(1)} all-to-all(bf16[16,8,640]{2,1,0:T(8,128)(2,1)S(1)} %bitcast.37), channel_id=1, replica_groups=mesh['rows'=16,'core'=2,'width'=8] {'rows'}, dimensions={0} | all-to-all | bytes 327680 | tf_op jit(solution)/shard_map/all_to_all | solution.py:107
  182.6 0.4 shard_map.155
  183.0 13.7 %all_to_all.73 = bf16[16,8,640]{2,1,0:T(8,128)(2,1)S(1)} all-to-all(bf16[16,8,640]{2,1,0:T(8,128)(2,1)S(1)} %get-tuple-element.59), channel_id=1, replica_groups=mesh['rows'=16,'core'=2,'width'=8] {'rows'}, dimensions={0} | all-to-all | bytes 327680 | tf_op jit(solution)/shard_map/all_to_all | solution.py:107
  196.7 2.4 collective-permute-start.4
  199.1 1.0 collective-permute-done.4.far
  200.1 0.9 shard_map.156
  201.0 9.7 %all_to_all.74.refs_0_ = bf16[8,32,640]{2,1,0:T(8,128)(2,1)S(1)} all-to-all(bf16[8,32,640]{2,1,0:T(8,128)(2,1)S(1)} %bitcast.41), channel_id=1, replica_groups=mesh['rows'=16,'core'=2,'width'=8] {'width'}, dimensions={0} | all-to-all | bytes 655360 | tf_op jit(solution)/shard_map/all_to_all | solution.py:107
  210.7 0.2 shard_map.157
  210.9 11.9 %all_to_all.75 = bf16[8,32,1280]{2,1,0:T(8,128)(2,1)S(1)} all-to-all(bf16[8,32,1280]{2,1,0:T(8,128)(2,1)S(1)} %shard_map.157), channel_id=1, replica_groups=mesh['rows'=16,'core'=2,'width'=8] {'width'}, dimensions={0} | all-to-all | bytes 1310720 | tf_op jit(solution)/shard_map/all_to_all | solution.py:107
  222.8 0.8 shard_map.158
  223.7 3.0 %collective-permute-start.5 = (bf16[128,640]{1,0:T(8,128)(2,1)S(1)}, bf16[128,640]{1,0:T(8,128)(2,1)S(1)}, u32[]{:S(2)}, u32[]{:S(2)}) collective-permute-start(bf16[128,640]{1,0:T(8,128)(2,1)S(1)} %get-tuple-element.69), channel_id=1, source_target_pairs={{0,8},{8,0},{1,9},{9,1},{2,10},{10,2},{3,11},{11,3},{4,12},{12,4},... | collective-permute-start | bytes 491528 | tf_op jit(solution)/shard_map/ppermute | solution.py:132
  226.7 1.0 collective-permute-done.5.refs_1_
  227.8 0.3 slice_reduce_fusion.1
  228.2 1.4 convolution_convert_fusion.2
  229.6 3.6 %all-to-all-start.12 = ((bf16[16,8,640]{2,1,0:T(8,128)(2,1)}), bf16[16,8,640]{2,1,0:T(8,128)(2,1)S(1)}, u32[]{:S(2)}, u32[]{:S(2)}) async-start(bf16[16,8,640]{2,1,0:T(8,128)(2,1)} %bitcast.42), calls=%async_computation.12 | async-start | bytes 327680 | tf_op jit(solution)/shard_map/all_to_all | solution.py:107
  233.2 5.0 %convolution_convert_fusion = bf16[576,4096]{1,0:T(8,128)(2,1)} fusion(bf16[256,576]{1,0:T(8,128)(2,1)} %copy-done.13, bf16[256,4224]{1,0:T(8,128)(2,1)S(1)} %bitcast.24, f32[256]{0:T(256)S(1)} %get-tuple-element.77, f32[256]{0:T(256)S(1)} %get-tuple-element.76, s32[256]{0:T(256)S(1)} %sub.22), kind=kOutput, calls=%fused_computation | convolution fusion | flops 1216610304 | bytes 7113728 | tf_op jit(solution)/shard_map/dot_general | solution.py:21
  238.2 1.4 convolution_convert_fusion.3
  239.6 1.4 convolution_convert_fusion.1
  241.0 1.2 all-to-all-done.12.refs_0_
  242.2 0.8 shard_map.160
  (59 shorter events, 1.3 us)
Async XLA Ops:
  2.0 20.7 %all-to-all-start = ((bf16[16,8,576]{2,1,0:T(8,128)(2,1)}), bf16[16,8,576]{2,1,0:T(8,128)(2,1)S(1)}, u32[]{:S(2)}, u32[]{:S(2)}) async-start(bf16[16,8,576]{2,1,0:T(8,128)(2,1)} %broadcast_in_dim.32), calls=%async_computation | async-start | bytes 327680 | tf_op jit(solution)/shard_map/all_to_all | solution.py:107
  14.7 4.1 %copy-start.17 = (f32[32]{0:T(128)S(1)}, f32[32]{0:T(128)}, u32[]{:S(2)}) copy-start(f32[32]{0:T(128)} %param.19) | copy-start | bytes 388
  14.7 10.8 %copy-start.16 = (f32[576]{0:T(1024)S(1)}, f32[576]{0:T(1024)}, u32[]{:S(2)}) copy-start(f32[576]{0:T(1024)} %param.11) | copy-start | bytes 6916
  14.8 10.8 %copy-start.14 = (f32[576]{0:T(1024)S(1)}, f32[576]{0:T(1024)}, u32[]{:S(2)}) copy-start(f32[576]{0:T(1024)} %param.12) | copy-start | bytes 6916
  14.8 10.8 %copy-start.15 = (f32[576]{0:T(1024)S(1)}, f32[576]{0:T(1024)}, u32[]{:S(2)}) copy-start(f32[576]{0:T(1024)} %param.13) | copy-start | bytes 6916
  14.8 11.3 %copy-start.1 = (bf16[576,576]{1,0:T(8,128)(2,1)S(1)}, bf16[576,576]{1,0:T(8,128)(2,1)}, u32[]{:S(2)}) copy-start(bf16[576,576]{1,0:T(8,128)(2,1)} %refs_1_.1) | copy-start | bytes 1990660
  14.8 11.3 %copy-start.3 = (bf16[576,576]{1,0:T(8,128)(2,1)S(1)}, bf16[576,576]{1,0:T(8,128)(2,1)}, u32[]{:S(2)}) copy-start(bf16[576,576]{1,0:T(8,128)(2,1)} %refs_2_.2) | copy-start | bytes 1990660
  18.8 32.0 %copy-start = (bf16[576,576]{1,0:T(8,128)(2,1)S(1)}, bf16[576,576]{1,0:T(8,128)(2,1)}, u32[]{:S(2)}) copy-start(bf16[576,576]{1,0:T(8,128)(2,1)} %down_weight.3) | copy-start | bytes 1990660
  22.7 3.4 %collective-permute-start = (bf16[128,576]{1,0:T(8,128)(2,1)S(1)}, bf16[128,576]{1,0:T(8,128)(2,1)S(1)}, u32[]{:S(2)}, u32[]{:S(2)}) collective-permute-start(bf16[128,576]{1,0:T(8,128)(2,1)S(1)} %bitcast.33), channel_id=1, source_target_pairs={{0,8},{8,0},{1,9},{9,1},{2,10},{10,2},{3,11},{11,3},{4,12},{12,4},... | collective-permute-start | bytes 442376 | tf_op jit(solution)/shard_map/ppermute | solution.py:132
  25.3 46.1 %copy-start.11 = (bf16[8,576]{1,0:T(8,128)(2,1)S(1)}, bf16[8,576]{1,0:T(8,128)(2,1)}, u32[]{:S(2)}) copy-start(bf16[8,576]{1,0:T(8,128)(2,1)} %refs_2_.3) | copy-start | bytes 27652
  26.9 201.2 %copy-start.5 = (bf16[256,576]{1,0:T(8,128)(2,1)}, bf16[256,576]{1,0:T(8,128)(2,1)S(1)}, u32[]{:S(2)}) copy-start(bf16[256,576]{1,0:T(8,128)(2,1)S(1)} %get-tuple-element.50.refs_2_) | copy-start | bytes 884740
  51.3 4.2 %collective-permute-start.1 = (bf16[128,1152]{1,0:T(8,128)(2,1)S(1)}, bf16[128,1152]{1,0:T(8,128)(2,1)S(1)}, u32[]{:S(2)}, u32[]{:S(2)}) collective-permute-start(bf16[128,1152]{1,0:T(8,128)(2,1)S(1)} %get-tuple-element.45), channel_id=1, source_target_pairs={{0,8},{8,0},{1,9},{9,1},{2,10},{10,2},{3,11},{11,3},{4,12},{12,4},... | collective-permute-start | bytes 884744 | tf_op jit(solution)/shard_map/ppermute | solution.py:132
  93.4 4.6 %collective-permute-start.2 = (bf16[128,640]{1,0:T(8,128)(2,1)S(1)}, bf16[128,640]{1,0:T(8,128)(2,1)S(1)}, u32[]{:S(2)}, u32[]{:S(2)}) collective-permute-start(bf16[128,640]{1,0:T(8,128)(2,1)S(1)} %bitcast.35), channel_id=1, source_target_pairs={{0,8},{8,0},{1,9},{9,1},{2,10},{10,2},{3,11},{11,3},{4,12},{12,4},... | collective-permute-start | bytes 491528 | tf_op jit(solution)/shard_map/ppermute | solution.py:132
  98.0 66.6 %slice-start = ((s8[4718592]{0:T(1024)(128)(4,1)}), s8[4194304]{0:T(1024)(128)(4,1)S(1)}, s32[]{:S(2)}) async-start(s8[4718592]{0:T(1024)(128)(4,1)} %bitcast.21), calls=%async_computation.13 | async-start | bytes 8388608
  102.5 0.7 copy-start.13
  103.3 119.5 %copy-start.7 = (bf16[256,640]{1,0:T(8,128)(2,1)}, bf16[256,640]{1,0:T(8,128)(2,1)S(1)}, u32[]{:S(2)}) copy-start(bf16[256,640]{1,0:T(8,128)(2,1)S(1)} %get-tuple-element.66.refs_4_) | copy-start | bytes 983044
  103.3 61.4 %slice-start.1 = ((s8[4718592]{0:T(1024)(128)(4,1)}), s8[524288]{0:T(1024)(128)(4,1)S(1)}, s32[]{:S(2)}) async-start(s8[4718592]{0:T(1024)(128)(4,1)} %bitcast.21), calls=%async_computation.14 | async-start | bytes 1048576
  166.5 56.3 %copy-start.2 = (bf16[576,576]{1,0:T(8,128)(2,1)S(1)}, bf16[576,576]{1,0:T(8,128)(2,1)}, u32[]{:S(2)}) copy-start(bf16[576,576]{1,0:T(8,128)(2,1)} %refs_1_.1) | copy-start | bytes 1990660
  166.5 56.3 %copy-start.4 = (bf16[576,576]{1,0:T(8,128)(2,1)S(1)}, bf16[576,576]{1,0:T(8,128)(2,1)}, u32[]{:S(2)}) copy-start(bf16[576,576]{1,0:T(8,128)(2,1)} %refs_2_.2) | copy-start | bytes 1990660
  166.5 4.0 %collective-permute-start.3 = (bf16[128,640]{1,0:T(8,128)(2,1)S(1)}, bf16[128,640]{1,0:T(8,128)(2,1)S(1)}, u32[]{:S(2)}, u32[]{:S(2)}) collective-permute-start(bf16[128,640]{1,0:T(8,128)(2,1)S(1)} %get-tuple-element.55), channel_id=1, source_target_pairs={{0,8},{8,0},{1,9},{9,1},{2,10},{10,2},{3,11},{11,3},{4,12},{12,4},... | collective-permute-start | bytes 491528 | tf_op jit(solution)/shard_map/ppermute | solution.py:132
  196.7 3.4 %collective-permute-start.4 = (bf16[128,640]{1,0:T(8,128)(2,1)S(1)}, bf16[128,640]{1,0:T(8,128)(2,1)S(1)}, u32[]{:S(2)}, u32[]{:S(2)}) collective-permute-start(bf16[128,640]{1,0:T(8,128)(2,1)S(1)} %bitcast.39), channel_id=1, source_target_pairs={{0,8},{8,0},{1,9},{9,1},{2,10},{10,2},{3,11},{11,3},{4,12},{12,4},... | collective-permute-start | bytes 491528 | tf_op jit(solution)/shard_map/ppermute | solution.py:132
  201.0 28.5 %copy-start.9 = (bf16[256,640]{1,0:T(8,128)(2,1)}, bf16[256,640]{1,0:T(8,128)(2,1)S(1)}, u32[]{:S(2)}) copy-start(bf16[256,640]{1,0:T(8,128)(2,1)S(1)} %get-tuple-element.67.refs_5_) | copy-start | bytes 983044
  223.7 4.0 %collective-permute-start.5 = (bf16[128,640]{1,0:T(8,128)(2,1)S(1)}, bf16[128,640]{1,0:T(8,128)(2,1)S(1)}, u32[]{:S(2)}, u32[]{:S(2)}) collective-permute-start(bf16[128,640]{1,0:T(8,128)(2,1)S(1)} %get-tuple-element.69), channel_id=1, source_target_pairs={{0,8},{8,0},{1,9},{9,1},{2,10},{10,2},{3,11},{11,3},{4,12},{12,4},... | collective-permute-start | bytes 491528 | tf_op jit(solution)/shard_map/ppermute | solution.py:132
  227.8 1.8 copy-start.12
  229.6 12.6 %all-to-all-start.12 = ((bf16[16,8,640]{2,1,0:T(8,128)(2,1)}), bf16[16,8,640]{2,1,0:T(8,128)(2,1)S(1)}, u32[]{:S(2)}, u32[]{:S(2)}) async-start(bf16[16,8,640]{2,1,0:T(8,128)(2,1)} %bitcast.42), calls=%async_computation.12 | async-start | bytes 327680 | tf_op jit(solution)/shard_map/all_to_all | solution.py:107
  233.2 5.0 %copy-start.6 = (bf16[256,576]{1,0:T(8,128)(2,1)S(1)}, bf16[256,576]{1,0:T(8,128)(2,1)}, u32[]{:S(2)}) copy-start(bf16[256,576]{1,0:T(8,128)(2,1)} %copy-done.5) | copy-start | bytes 884740
  233.2 6.4 %copy-start.8 = (bf16[256,640]{1,0:T(8,128)(2,1)S(1)}, bf16[256,640]{1,0:T(8,128)(2,1)}, u32[]{:S(2)}) copy-start(bf16[256,640]{1,0:T(8,128)(2,1)} %copy-done.7) | copy-start | bytes 983044
  233.2 6.4 %copy-start.10 = (bf16[256,640]{1,0:T(8,128)(2,1)S(1)}, bf16[256,640]{1,0:T(8,128)(2,1)}, u32[]{:S(2)}) copy-start(bf16[256,640]{1,0:T(8,128)(2,1)} %copy-done.9) | copy-start | bytes 983044

commit v6 on v5

--- a/solution.py
+++ b/solution.py
@@ -86,15 +86,15 @@
     return total
 
 
-def local(body, outs, *args, hbm=(), scratch=()):
+def local(body, outs, *args, off_chip=(), scratch=()):
     return pl.pallas_call(
         body,
         out_shape=tuple(jax.ShapeDtypeStruct(s, d) for s, d in outs),
-        in_specs=[
-            pl.BlockSpec(memory_space=pltpu.HBM if i in hbm else pltpu.VMEM)
-            for i in range(len(args))
-        ],
-        out_specs=tuple(pl.BlockSpec(memory_space=pltpu.VMEM) for _ in outs),
+        in_specs=[pl.BlockSpec(memory_space=pltpu.VMEM) for _ in args],
+        out_specs=tuple(
+            pl.BlockSpec(memory_space=pltpu.HBM if i in off_chip else pltpu.VMEM)
+            for i in range(len(outs))
+        ),
         scratch_shapes=scratch,
         compiler_params=pltpu.CompilerParams(vmem_limit_bytes=16 << 20),
     )(*args)
@@ -187,7 +187,8 @@
     theirs[:, width : 2 * width] = target_rows[half:]
 
 
-def norm_step(message, inputs, gains, branch, target, out):
+def norm_step(message, inputs, gains, head, branch, target, out):
+    del head
     width = branch.shape[1]
     both = summed(message, slice(0, 2 * width))
     value = both[:, :width]
@@ -222,35 +223,22 @@
     put_copies(out, branch[...].astype(BF16), [post, final])
 
 
-def logit_step(
-    copies_n, near, far, inputs, gains, down_weight, head, out, final, message, buffer, sems
-):
-    vocab = head.shape[1]
-    copies = [
-        pltpu.make_async_copy(head.at[:, pl.ds(i * CHUNK, CHUNK)], buffer.at[i], sems.at[i])
-        for i in range(vocab // CHUNK)
-    ]
-    for copy in copies:
-        copy.start()
+def logit_step(near, far, inputs, gains, head, out, final_out, message, final, sem):
     rejoin(near, far, message)
     width = final.shape[1]
-    branch = message[:, :width]
     post, scale = read_stats(message[:, tail_of(width)].astype(F32), width, 2)
-    resid = inputs[...].astype(F32) + branch.astype(F32) * post * gains[1:2]
+    resid = inputs[...].astype(F32) + message[:, :width].astype(F32) * post * gains[1:2]
     final[...] = (resid * scale * gains[2:3]).astype(BF16)
-    hidden = down_weight.shape[0]
-    out[:, vocab : vocab + hidden] = contract(branch, down_weight[...], 1, 1).astype(BF16)
-    tail = tail_of(vocab + hidden)
-    tile = with_stats(out[:, tail].astype(F32), vocab + hidden, [post / copies_n])
-    out[:, tail] = tile.astype(BF16)
-    for i, copy in enumerate(copies):
-        copy.wait()
-        columns = slice(i * CHUNK, (i + 1) * CHUNK)
-        out[:, columns] = contract(final[...], buffer[i], 1, 0).astype(BF16)
-
-
-def soft_step(vocab, hidden, message, ids, out, branch_down):
-    rows = message.shape[1]
+    copy = pltpu.make_async_copy(final, final_out, sem)
+    copy.start()
+    for i in range(0, head.shape[1], CHUNK):
+        columns = slice(i, i + CHUNK)
+        out[:, columns] = contract(final[...], head[:, columns], 1, 0).astype(BF16)
+    copy.wait()
+
+
+def soft_step(message, ids, out):
+    rows, vocab = message.shape[1:]
     step = 256
     others = jnp.zeros((rows, step), F32)
     cross = jnp.zeros((rows, step), F32)
@@ -273,7 +261,6 @@
     tile = with_stats(jnp.zeros((rows, LANES), F32), vocab, stats).astype(BF16)
     for j in range(out.shape[0]):
         out[j, :, vocab : vocab + LANES] = tile
-    branch_down[...] = summed(message, slice(vocab, vocab + padded(hidden)))
 
 
 def row_step(message, head, mine, theirs):
@@ -315,23 +302,28 @@
     )
 
 
-def down_step(near, far, down_weight, out, message, loss):
+def down_step(copies_n, near, far, branch, down_weight, out, message, loss):
     rejoin(near, far, message)
-    width = down_weight.shape[1]
-    _, _, score, back_post = read_stats(message[:, tail_of(width)].astype(F32), width, 4)
+    hidden, width = down_weight.shape
+    tail = tail_of(width)
+    _, _, score, back_post = read_stats(message[:, tail].astype(F32), width, 4)
+    post, _ = read_stats(branch[:, tail].astype(F32), width, 2)
     put(
         out,
         contract(message[:, :width], down_weight[...], 1, 1).astype(BF16),
-        [back_post],
-    )
+        [back_post, post / copies_n],
+    )
+    out[:, padded(hidden) : padded(hidden) + hidden] = contract(
+        branch[:, :width], down_weight[...], 1, 1
+    ).astype(BF16)
     loss[...] = -jnp.sum(score, axis=0, keepdims=True) / message.shape[0]
 
 
-def hidden_step(model, message, branch_down, gate, upward, gelu_gate, gelu_slope, out):
-    rows, width = gate.shape
-    (back_post,) = read_stats(summed(message, tail_of(width)), width, 1)
-    (post,) = read_stats(branch_down[:, tail_of(width)], width, 1)
-    grad = summed(message, slice(0, width)) - branch_down[:, :width] * (
+def hidden_step(model, message, gate, upward, gelu_gate, gelu_slope, out):
+    width = gate.shape[1]
+    start = padded(width)
+    back_post, post = read_stats(summed(message, tail_of(width)), width, 2)
+    grad = summed(message, slice(0, width)) - summed(message, slice(start, start + width)) * (
         post * post * post * back_post / model
     )
     gate_in = (grad * upward[...] * gelu_slope[...]).astype(BF16)
@@ -339,7 +331,6 @@
     back = jnp.sum(
         gate_in.astype(F32) * gate[...] + up_in.astype(F32) * upward[...], axis=1, keepdims=True
     )
-    start = padded(width)
     put(out.at[0], gate_in, [back, back_post])
     out[0, :, start : start + width] = up_in
     whole = out[0]
@@ -449,6 +440,7 @@
         *reduced(mine, theirs, width * 2, 0),
         hidden,
         gains,
+        head_weight,
     )
     scales, message = local(
         lambda *refs: scale_step(model, *refs),
@@ -458,9 +450,9 @@
     )
     near, far = gathered(message)
     message, final, branch_all = local(
-        lambda *refs: logit_step(cols_n, *refs),
+        logit_step,
         [
-            ((tokens, vocab + padded(ff)), BF16),
+            ((tokens, vocab), BF16),
             ((tokens, width), BF16),
             ((tokens, padded(width)), BF16),
         ],
@@ -468,17 +460,13 @@
         far,
         inputs,
         gains,
-        down_weight,
-        pltpu.with_memory_space_constraint(head_weight, pltpu.HBM),
-        hbm=(5,),
-        scratch=(
-            pltpu.VMEM((vocab // CHUNK, width, CHUNK), BF16),
-            pltpu.SemaphoreType.DMA((vocab // CHUNK,)),
-        ),
-    )
-    message, branch_down = local(
-        lambda *refs: soft_step(vocab, ff, *refs),
-        [((cols_n, sub, vocab + LANES), BF16), ((sub, padded(ff)), F32)],
+        head_weight,
+        off_chip=(1,),
+        scratch=(pltpu.VMEM((tokens, width), BF16), pltpu.SemaphoreType.DMA),
+    )
+    (message,) = local(
+        soft_step,
+        [((cols_n, sub, vocab + LANES), BF16)],
         exchange(message, "width"),
         sub_ids,
     )
@@ -498,17 +486,17 @@
     )
     near, far = gathered(message)
     message, weighted, loss = local(
-        down_step,
-        [((tokens, padded(ff)), BF16), ((tokens, padded(width)), BF16), ((1, 1), F32)],
+        lambda *refs: down_step(cols_n, *refs),
+        [((tokens, padded(ff) * 2), BF16), ((tokens, padded(width)), BF16), ((1, 1), F32)],
         near,
         far,
+        branch_all,
         down_weight,
     )
     (message,) = local(
         lambda *refs: hidden_step(model, *refs),
         [((cols_n, sub, padded(ff) * 2), BF16)],
         exchange(message, "width"),
-        branch_down,
         gate,
         upward,
         gelu_gate,

time: 244 us -> 245 us (level)
  transfers between devices with their start and end apart: 8 -> 8, of which waited for: 8 -> 8; matrix products, arithmetic and copies ran while one was open for 6% -> 5% of each run, Pallas kernels for 0% -> 0%
where the time goes in v6:
time: 245 us; the launch traced here: 244 us
  blocking collectives  170 us (69%)
  starting transfers between devices  33 us (13%)
  matrix products  13.1 us (5%)
  Pallas kernels  11.6 us (5%)
  waiting for transfers between devices  10.7 us (4%)
  local copies, waits for them, and re-layouts  4.19 us (2%)
    all_to_all x11, blocking collectives, exchange(): return lax.all_to_all(parts, axis, 0, 0, tiled=True)  170 us
    ppermute x6, starting transfers between devices, swap(): return lax.ppermute(values, 'core', [(0, 1), (1, 0)])  17.1 us
    all_to_all x2, starting transfers between devices, exchange(): return lax.all_to_all(parts, axis, 0, 0, tiled=True)  15.9 us
    dot_general x5, matrix products, contract(): lax.dot_general(left, right, (((left_dim,), (right_dim,)), ((), ())), pre...  13.1 us
    pallas_call x16, Pallas kernels, local(): pl.pallas_call(body, out_shape=tuple((jax.ShapeDtypeStruct(s, d) for s, d...  11.6 us
    ppermute x6, waiting for transfers between devices, swap(): return lax.ppermute(values, 'core', [(0, 1), (1, 0)])  5.8 us
  transfers between devices with their start and end apart: 8, of which 8 were waited for; matrix products, arithmetic and copies ran while one was open for 5% of the time, Pallas kernels for 0%

profile of v6, /device:TPU:1, one launch (start us, length us, event | category | flops | bytes accessed | tf_op | source)
XLA Modules:
  0.0 243.5 jit_solution(2629853389990898075)
XLA Ops:
  0.6 1.4 broadcast_in_dim.32
  2.0 11.7 %all-to-all-start = ((bf16[16,8,576]{2,1,0:T(8,128)(2,1)}), bf16[16,8,576]{2,1,0:T(8,128)(2,1)S(1)}, u32[]{:S(2)}, u32[]{:S(2)}) async-start(bf16[16,8,576]{2,1,0:T(8,128)(2,1)} %broadcast_in_dim.32), calls=%async_computation | async-start | bytes 327680 | tf_op jit(solution)/shard_map/all_to_all | solution.py:107
  13.8 0.8 reshape.65
  14.8 4.0 %fusion.7 = bf16[256,576]{0,1:T(8,128)(2,1)S(1)} fusion(bf16[576,4096]{1,0:T(8,128)(2,1)} %head.5, s32[256]{0:T(256)S(1)} %sub.22), kind=kOutput, calls=%fused_computation.13 | convolution fusion | flops 1209155584 | bytes 5014528 | tf_op jit(solution)/shard_map/dot_general | solution.py:21
  19.1 3.6 %all-to-all-done = bf16[16,8,576]{2,1,0:T(8,128)(2,1)S(1)} async-done(((bf16[16,8,576]{2,1,0:T(8,128)(2,1)}), bf16[16,8,576]{2,1,0:T(8,128)(2,1)S(1)}, u32[]{:S(2)}, u32[]{:S(2)}) %all-to-all-start) | async-done | bytes 147488 | tf_op jit(solution)/shard_map/all_to_all | solution.py:107
  22.7 2.3 collective-permute-start
  25.6 0.5 collective-permute-done.far
  26.1 0.8 shard_map.145
  26.9 14.6 %all_to_all.65.refs_0_ = bf16[8,32,1280]{2,1,0:T(8,128)(2,1)S(1)} all-to-all(bf16[8,32,1280]{2,1,0:T(8,128)(2,1)S(1)} %bitcast.36), channel_id=1, replica_groups=mesh['rows'=16,'core'=2,'width'=8] {'width'}, dimensions={0} | all-to-all | bytes 1310720 | tf_op jit(solution)/shard_map/all_to_all | solution.py:107
  41.5 0.2 shard_map.146
  41.7 9.4 %all_to_all.66 = bf16[8,32,640]{2,1,0:T(8,128)(2,1)S(1)} all-to-all(bf16[8,32,640]{2,1,0:T(8,128)(2,1)S(1)} %get-tuple-element.40), channel_id=1, replica_groups=mesh['rows'=16,'core'=2,'width'=8] {'width'}, dimensions={0} | all-to-all | bytes 655360 | tf_op jit(solution)/shard_map/all_to_all | solution.py:107
  51.1 0.5 shard_map.147
  51.6 2.8 %collective-permute-start.1 = (bf16[128,1152]{1,0:T(8,128)(2,1)S(1)}, bf16[128,1152]{1,0:T(8,128)(2,1)S(1)}, u32[]{:S(2)}, u32[]{:S(2)}) collective-permute-start(bf16[128,1152]{1,0:T(8,128)(2,1)S(1)} %get-tuple-element.43), channel_id=1, source_target_pairs={{0,8},{8,0},{1,9},{9,1},{2,10},{10,2},{3,11},{11,3},{4,12},{12,4},... | collective-permute-start | bytes 884744 | tf_op jit(solution)/shard_map/ppermute | solution.py:132
  54.4 1.2 collective-permute-done.1.refs_1_
  55.7 15.9 %all_to_all.67.message = bf16[16,8,1152]{2,1,0:T(8,128)(2,1)S(1)} all-to-all(bf16[16,8,1152]{2,1,0:T(8,128)(2,1)S(1)} %bitcast.30), channel_id=1, replica_groups=mesh['rows'=16,'core'=2,'width'=8] {'rows'}, dimensions={0} | all-to-all | bytes 589824 | tf_op jit(solution)/shard_map/all_to_all | solution.py:107
  71.6 7.5 %all_to_all.68.refs_0_ = f32[8,8,128]{2,1,0:T(8,128)S(1)} all-to-all(f32[8,8,128]{2,1,0:T(8,128)S(1)} %get-tuple-element.45), channel_id=1, replica_groups=mesh['rows'=16,'core'=2,'width'=8] {'width'}, dimensions={0} | all-to-all | bytes 65536 | tf_op jit(solution)/shard_map/all_to_all | solution.py:107
  79.2 14.3 %all_to_all.69 = bf16[16,8,640]{2,1,0:T(8,128)(2,1)S(1)} all-to-all(bf16[16,8,640]{2,1,0:T(8,128)(2,1)S(1)} %get-tuple-element.47), channel_id=1, replica_groups=mesh['rows'=16,'core'=2,'width'=8] {'rows'}, dimensions={0} | all-to-all | bytes 327680 | tf_op jit(solution)/shard_map/all_to_all | solution.py:107
  93.5 3.6 %collective-permute-start.2 = (bf16[128,640]{1,0:T(8,128)(2,1)S(1)}, bf16[128,640]{1,0:T(8,128)(2,1)S(1)}, u32[]{:S(2)}, u32[]{:S(2)}) collective-permute-start(bf16[128,640]{1,0:T(8,128)(2,1)S(1)} %bitcast.33), channel_id=1, source_target_pairs={{0,8},{8,0},{1,9},{9,1},{2,10},{10,2},{3,11},{11,3},{4,12},{12,4},... | collective-permute-start | bytes 491528 | tf_op jit(solution)/shard_map/ppermute | solution.py:132
  97.1 1.0 collective-permute-done.2.far
  98.2 2.2 shard_map.151
  100.3 0.7 copy-done.21
  101.0 28.6 %all_to_all.70.message = bf16[8,32,4096]{2,1,0:T(8,128)(2,1)S(1)} all-to-all(bf16[8,32,4096]{2,1,0:T(8,128)(2,1)S(1)} %bitcast.29), channel_id=1, replica_groups=mesh['rows'=16,'core'=2,'width'=8] {'width'}, dimensions={0} | all-to-all | bytes 4194304 | tf_op jit(solution)/shard_map/all_to_all | solution.py:107
  129.7 0.7 shard_map.152
  130.3 28.4 %all_to_all.71 = bf16[8,32,4224]{2,1,0:T(8,128)(2,1)S(1)} all-to-all(bf16[8,32,4224]{2,1,0:T(8,128)(2,1)S(1)} %shard_map.152), channel_id=1, replica_groups=mesh['rows'=16,'core'=2,'width'=8] {'width'}, dimensions={0} | all-to-all | bytes 4325376 | tf_op jit(solution)/shard_map/all_to_all | solution.py:107
  158.8 1.9 shard_map.153
  160.6 3.0 %collective-permute-start.3 = (bf16[128,640]{1,0:T(8,128)(2,1)S(1)}, bf16[128,640]{1,0:T(8,128)(2,1)S(1)}, u32[]{:S(2)}, u32[]{:S(2)}) collective-permute-start(bf16[128,640]{1,0:T(8,128)(2,1)S(1)} %get-tuple-element.52), channel_id=1, source_target_pairs={{0,8},{8,0},{1,9},{9,1},{2,10},{10,2},{3,11},{11,3},{4,12},{12,4},... | collective-permute-start | bytes 491528 | tf_op jit(solution)/shard_map/ppermute | solution.py:132
  163.7 1.0 collective-permute-done.3.refs_1_
  164.8 12.0 %all_to_all.72.refs_0_ = bf16[16,8,640]{2,1,0:T(8,128)(2,1)S(1)} all-to-all(bf16[16,8,640]{2,1,0:T(8,128)(2,1)S(1)} %bitcast.35), channel_id=1, replica_groups=mesh['rows'=16,'core'=2,'width'=8] {'rows'}, dimensions={0} | all-to-all | bytes 327680 | tf_op jit(solution)/shard_map/all_to_all | solution.py:107
  176.9 0.4 shard_map.155
  177.2 13.7 %all_to_all.73 = bf16[16,8,640]{2,1,0:T(8,128)(2,1)S(1)} all-to-all(bf16[16,8,640]{2,1,0:T(8,128)(2,1)S(1)} %get-tuple-element.56), channel_id=1, replica_groups=mesh['rows'=16,'core'=2,'width'=8] {'rows'}, dimensions={0} | all-to-all | bytes 327680 | tf_op jit(solution)/shard_map/all_to_all | solution.py:107
  191.0 2.4 collective-permute-start.4
  193.4 1.0 collective-permute-done.4.refs_1_
  194.4 1.2 shard_map.156
  195.6 13.2 %all_to_all.74.refs_0_ = bf16[8,32,1280]{2,1,0:T(8,128)(2,1)S(1)} all-to-all(bf16[8,32,1280]{2,1,0:T(8,128)(2,1)S(1)} %bitcast.37), channel_id=1, replica_groups=mesh['rows'=16,'core'=2,'width'=8] {'width'}, dimensions={0} | all-to-all | bytes 1310720 | tf_op jit(solution)/shard_map/all_to_all | solution.py:107
  208.8 0.2 shard_map.157
  209.1 12.2 %all_to_all.75 = bf16[8,32,1280]{2,1,0:T(8,128)(2,1)S(1)} all-to-all(bf16[8,32,1280]{2,1,0:T(8,128)(2,1)S(1)} %shard_map.157), channel_id=1, replica_groups=mesh['rows'=16,'core'=2,'width'=8] {'width'}, dimensions={0} | all-to-all | bytes 1310720 | tf_op jit(solution)/shard_map/all_to_all | solution.py:107
  221.2 0.8 shard_map.158
  222.0 3.0 %collective-permute-start.5 = (bf16[128,640]{1,0:T(8,128)(2,1)S(1)}, bf16[128,640]{1,0:T(8,128)(2,1)S(1)}, u32[]{:S(2)}, u32[]{:S(2)}) collective-permute-start(bf16[128,640]{1,0:T(8,128)(2,1)S(1)} %get-tuple-element.65), channel_id=1, source_target_pairs={{0,8},{8,0},{1,9},{9,1},{2,10},{10,2},{3,11},{11,3},{4,12},{12,4},... | collective-permute-start | bytes 491528 | tf_op jit(solution)/shard_map/ppermute | solution.py:132
  225.0 1.0 collective-permute-done.5.refs_1_
  226.0 0.8 shard_map.159
  226.8 0.3 slice_reduce_fusion.1
  227.2 1.4 convolution_convert_fusion.2
  228.6 4.2 %all-to-all-start.12 = ((bf16[16,8,640]{2,1,0:T(8,128)(2,1)}), bf16[16,8,640]{2,1,0:T(8,128)(2,1)}, u32[]{:S(2)}, u32[]{:S(2)}) async-start(bf16[16,8,640]{2,1,0:T(8,128)(2,1)} %bitcast.14), calls=%async_computation.12 | async-start | bytes 327680 | tf_op jit(solution)/shard_map/all_to_all | solution.py:107
  232.8 4.9 %convolution_convert_fusion = bf16[576,4096]{1,0:T(8,128)(2,1)} fusion(bf16[256,576]{1,0:T(8,128)(2,1)} %copy-done.21, bf16[256,4224]{1,0:T(8,128)(2,1)S(1)} %bitcast.22, f32[256]{0:T(256)S(1)} %get-tuple-element.73, f32[256]{0:T(256)S(1)} %get-tuple-element.72, s32[256]{0:T(256)} %copy-done.27), kind=kOutput, calls=%fused_computation | convolution fusion | flops 1216610304 | bytes 7113728 | tf_op jit(solution)/shard_map/dot_general | solution.py:21
  237.8 1.4 convolution_convert_fusion.3
  239.2 1.4 convolution_convert_fusion.1
  240.5 1.3 all-to-all-done.12.refs_0_
  241.8 1.7 shard_map.160
  (76 shorter events, 1.4 us)
Async XLA Ops:
  2.0 20.7 %all-to-all-start = ((bf16[16,8,576]{2,1,0:T(8,128)(2,1)}), bf16[16,8,576]{2,1,0:T(8,128)(2,1)S(1)}, u32[]{:S(2)}, u32[]{:S(2)}) async-start(bf16[16,8,576]{2,1,0:T(8,128)(2,1)} %broadcast_in_dim.32), calls=%async_computation | async-start | bytes 327680 | tf_op jit(solution)/shard_map/all_to_all | solution.py:107
  14.7 4.3 %copy-start.27 = (s32[256]{0:T(256)}, s32[256]{0:T(256)S(1)}, u32[]{:S(2)}) copy-start(s32[256]{0:T(256)S(1)} %sub.22) | copy-start | bytes 3076
  14.7 4.1 %copy-start.28 = (f32[32]{0:T(128)S(1)}, f32[32]{0:T(128)}, u32[]{:S(2)}) copy-start(f32[32]{0:T(128)} %param.19) | copy-start | bytes 388
  14.8 10.8 %copy-start.24 = (f32[576]{0:T(1024)S(1)}, f32[576]{0:T(1024)}, u32[]{:S(2)}) copy-start(f32[576]{0:T(1024)} %param.11) | copy-start | bytes 6916
  14.8 10.8 %copy-start.22 = (f32[576]{0:T(1024)S(1)}, f32[576]{0:T(1024)}, u32[]{:S(2)}) copy-start(f32[576]{0:T(1024)} %param.12) | copy-start | bytes 6916
  14.8 10.8 %copy-start.23 = (f32[576]{0:T(1024)S(1)}, f32[576]{0:T(1024)}, u32[]{:S(2)}) copy-start(f32[576]{0:T(1024)} %param.13) | copy-start | bytes 6916
  14.8 11.3 %copy-start.1 = (bf16[576,576]{1,0:T(8,128)(2,1)S(1)}, bf16[576,576]{1,0:T(8,128)(2,1)}, u32[]{:S(2)}) copy-start(bf16[576,576]{1,0:T(8,128)(2,1)} %refs_1_.1) | copy-start | bytes 1990660
  14.8 11.3 %copy-start.2 = (bf16[576,576]{1,0:T(8,128)(2,1)S(1)}, bf16[576,576]{1,0:T(8,128)(2,1)}, u32[]{:S(2)}) copy-start(bf16[576,576]{1,0:T(8,128)(2,1)} %refs_2_.2) | copy-start | bytes 1990660
  18.9 32.3 %copy-start.4 = (bf16[576,576]{1,0:T(8,128)(2,1)S(1)}, bf16[576,576]{1,0:T(8,128)(2,1)}, u32[]{:S(2)}) copy-start(bf16[576,576]{1,0:T(8,128)(2,1)} %refs_3_.3) | copy-start | bytes 1990660
  22.7 3.4 %collective-permute-start = (bf16[128,576]{1,0:T(8,128)(2,1)S(1)}, bf16[128,576]{1,0:T(8,128)(2,1)S(1)}, u32[]{:S(2)}, u32[]{:S(2)}) collective-permute-start(bf16[128,576]{1,0:T(8,128)(2,1)S(1)} %bitcast.31), channel_id=1, source_target_pairs={{0,8},{8,0},{1,9},{9,1},{2,10},{10,2},{3,11},{11,3},{4,12},{12,4},... | collective-permute-start | bytes 442376 | tf_op jit(solution)/shard_map/ppermute | solution.py:132
  25.3 46.2 %copy-start.14 = (bf16[8,576]{1,0:T(8,128)(2,1)S(1)}, bf16[8,576]{1,0:T(8,128)(2,1)}, u32[]{:S(2)}) copy-start(bf16[8,576]{1,0:T(8,128)(2,1)} %refs_2_.3) | copy-start | bytes 27652
  25.5 46.0 %copy-start = (bf16[576,4096]{1,0:T(8,128)(2,1)S(1)}, bf16[576,4096]{1,0:T(8,128)(2,1)}, u32[]{:S(2)}) copy-start(bf16[576,4096]{1,0:T(8,128)(2,1)} %head.5) | copy-start | bytes 14155780
  26.9 150.0 %copy-start.12 = (f32[3,576]{1,0:T(4,128)}, f32[3,576]{1,0:T(4,128)S(1)}, u32[]{:S(2)}) copy-start(f32[3,576]{1,0:T(4,128)S(1)} %get-tuple-element.44.gains.refs_6_.refs_4_) | copy-start | bytes 20740
  26.9 200.2 %copy-start.8 = (bf16[256,576]{1,0:T(8,128)(2,1)}, bf16[256,576]{1,0:T(8,128)(2,1)S(1)}, u32[]{:S(2)}) copy-start(bf16[256,576]{1,0:T(8,128)(2,1)S(1)} %get-tuple-element.48.inputs) | copy-start | bytes 884740
  51.6 4.0 %collective-permute-start.1 = (bf16[128,1152]{1,0:T(8,128)(2,1)S(1)}, bf16[128,1152]{1,0:T(8,128)(2,1)S(1)}, u32[]{:S(2)}, u32[]{:S(2)}) collective-permute-start(bf16[128,1152]{1,0:T(8,128)(2,1)S(1)} %get-tuple-element.43), channel_id=1, source_target_pairs={{0,8},{8,0},{1,9},{9,1},{2,10},{10,2},{3,11},{11,3},{4,12},{12,4},... | collective-permute-start | bytes 884744 | tf_op jit(solution)/shard_map/ppermute | solution.py:132
  79.2 97.7 %copy-start.19 = (f32[8,128]{1,0:T(8,128)}, f32[8,128]{1,0:T(8,128)S(1)}, u32[]{:S(2)}) copy-start(f32[8,128]{1,0:T(8,128)S(1)} %get-tuple-element.54.refs_4_.refs_3_) | copy-start | bytes 12292
  93.5 4.6 %collective-permute-start.2 = (bf16[128,640]{1,0:T(8,128)(2,1)S(1)}, bf16[128,640]{1,0:T(8,128)(2,1)S(1)}, u32[]{:S(2)}, u32[]{:S(2)}) collective-permute-start(bf16[128,640]{1,0:T(8,128)(2,1)S(1)} %bitcast.33), channel_id=1, source_target_pairs={{0,8},{8,0},{1,9},{9,1},{2,10},{10,2},{3,11},{11,3},{4,12},{12,4},... | collective-permute-start | bytes 491528 | tf_op jit(solution)/shard_map/ppermute | solution.py:132
  100.3 0.7 copy-start.21
  158.8 18.1 %copy-start.15 = (bf16[8,576]{1,0:T(8,128)(2,1)S(1)}, bf16[8,576]{1,0:T(8,128)(2,1)}, u32[]{:S(2)}) copy-start(bf16[8,576]{1,0:T(8,128)(2,1)} %refs_2_.3) | copy-start | bytes 27652
  158.8 35.6 %copy-start.5 = (bf16[576,576]{1,0:T(8,128)(2,1)S(1)}, bf16[576,576]{1,0:T(8,128)(2,1)}, u32[]{:S(2)}) copy-start(bf16[576,576]{1,0:T(8,128)(2,1)} %refs_3_.3) | copy-start | bytes 1990660
  160.6 60.6 %copy-start.3 = (bf16[576,576]{1,0:T(8,128)(2,1)S(1)}, bf16[576,576]{1,0:T(8,128)(2,1)}, u32[]{:S(2)}) copy-start(bf16[576,576]{1,0:T(8,128)(2,1)} %refs_2_.2) | copy-start | bytes 1990660
  160.6 4.0 %collective-permute-start.3 = (bf16[128,640]{1,0:T(8,128)(2,1)S(1)}, bf16[128,640]{1,0:T(8,128)(2,1)S(1)}, u32[]{:S(2)}, u32[]{:S(2)}) collective-permute-start(bf16[128,640]{1,0:T(8,128)(2,1)S(1)} %get-tuple-element.52), channel_id=1, source_target_pairs={{0,8},{8,0},{1,9},{9,1},{2,10},{10,2},{3,11},{11,3},{4,12},{12,4},... | collective-permute-start | bytes 491528 | tf_op jit(solution)/shard_map/ppermute | solution.py:132
  177.2 18.4 %copy-start.17 = (f32[8,576]{1,0:T(8,128)}, f32[8,576]{1,0:T(8,128)S(1)}, u32[]{:S(2)}) copy-start(f32[8,576]{1,0:T(8,128)S(1)} %get-tuple-element.68.refs_1_) | copy-start | bytes 55300
  191.0 3.4 %collective-permute-start.4 = (bf16[128,640]{1,0:T(8,128)(2,1)S(1)}, bf16[128,640]{1,0:T(8,128)(2,1)S(1)}, u32[]{:S(2)}, u32[]{:S(2)}) collective-permute-start(bf16[128,640]{1,0:T(8,128)(2,1)S(1)} %bitcast.38), channel_id=1, source_target_pairs={{0,8},{8,0},{1,9},{9,1},{2,10},{10,2},{3,11},{11,3},{4,12},{12,4},... | collective-permute-start | bytes 491528 | tf_op jit(solution)/shard_map/ppermute | solution.py:132
  195.6 31.5 %copy-start.10 = (bf16[256,640]{1,0:T(8,128)(2,1)}, bf16[256,640]{1,0:T(8,128)(2,1)S(1)}, u32[]{:S(2)}) copy-start(bf16[256,640]{1,0:T(8,128)(2,1)S(1)} %get-tuple-element.63.refs_5_) | copy-start | bytes 983044
  195.6 31.5 %copy-start.25 = (f32[576]{0:T(1024)S(1)}, f32[576]{0:T(1024)}, u32[]{:S(2)}) copy-start(f32[576]{0:T(1024)} %param.11) | copy-start | bytes 6916
  221.2 5.9 %copy-start.6 = (bf16[8,32,1280]{2,1,0:T(8,128)(2,1)}, bf16[8,32,1280]{2,1,0:T(8,128)(2,1)S(1)}, u32[]{:S(2)}) copy-start(bf16[8,32,1280]{2,1,0:T(8,128)(2,1)S(1)} %all_to_all.75) | copy-start | bytes 1966084
  222.0 4.0 %collective-permute-start.5 = (bf16[128,640]{1,0:T(8,128)(2,1)S(1)}, bf16[128,640]{1,0:T(8,128)(2,1)S(1)}, u32[]{:S(2)}, u32[]{:S(2)}) collective-permute-start(bf16[128,640]{1,0:T(8,128)(2,1)S(1)} %get-tuple-element.65), channel_id=1, source_target_pairs={{0,8},{8,0},{1,9},{9,1},{2,10},{10,2},{3,11},{11,3},{4,12},{12,4},... | collective-permute-start | bytes 491528 | tf_op jit(solution)/shard_map/ppermute | solution.py:132
  228.6 13.2 %all-to-all-start.12 = ((bf16[16,8,640]{2,1,0:T(8,128)(2,1)}), bf16[16,8,640]{2,1,0:T(8,128)(2,1)}, u32[]{:S(2)}, u32[]{:S(2)}) async-start(bf16[16,8,640]{2,1,0:T(8,128)(2,1)} %bitcast.14), calls=%async_computation.12 | async-start | bytes 327680 | tf_op jit(solution)/shard_map/all_to_all | solution.py:107
  232.7 5.0 %copy-start.7 = (bf16[8,32,1280]{2,1,0:T(8,128)(2,1)S(1)}, bf16[8,32,1280]{2,1,0:T(8,128)(2,1)}, u32[]{:S(2)}) copy-start(bf16[8,32,1280]{2,1,0:T(8,128)(2,1)} %copy-done.6) | copy-start | bytes 1966084
  232.8 5.0 %copy-start.9 = (bf16[256,576]{1,0:T(8,128)(2,1)S(1)}, bf16[256,576]{1,0:T(8,128)(2,1)}, u32[]{:S(2)}) copy-start(bf16[256,576]{1,0:T(8,128)(2,1)} %copy-done.8) | copy-start | bytes 884740
  232.8 5.0 %copy-start.26 = (f32[576]{0:T(1024)S(1)}, f32[576]{0:T(1024)}, u32[]{:S(2)}) copy-start(f32[576]{0:T(1024)} %param.11) | copy-start | bytes 6916
  232.8 6.4 %copy-start.11 = (bf16[256,640]{1,0:T(8,128)(2,1)S(1)}, bf16[256,640]{1,0:T(8,128)(2,1)}, u32[]{:S(2)}) copy-start(bf16[256,640]{1,0:T(8,128)(2,1)} %copy-done.10) | copy-start | bytes 983044
  232.8 9.0 %copy-start.13 = (f32[3,576]{1,0:T(4,128)S(1)}, f32[3,576]{1,0:T(4,128)}, u32[]{:S(2)}) copy-start(f32[3,576]{1,0:T(4,128)} %copy-done.12) | copy-start | bytes 20740
  232.8 9.0 %copy-start.16 = (bf16[8,576]{1,0:T(8,128)(2,1)S(1)}, bf16[8,576]{1,0:T(8,128)(2,1)}, u32[]{:S(2)}) copy-start(bf16[8,576]{1,0:T(8,128)(2,1)} %refs_2_.3) | copy-start | bytes 27652
  232.8 9.0 %copy-start.18 = (f32[8,576]{1,0:T(8,128)S(1)}, f32[8,576]{1,0:T(8,128)}, u32[]{:S(2)}) copy-start(f32[8,576]{1,0:T(8,128)} %copy-done.17) | copy-start | bytes 55300
  232.8 9.0 %copy-start.20 = (f32[8,128]{1,0:T(8,128)S(1)}, f32[8,128]{1,0:T(8,128)}, u32[]{:S(2)}) copy-start(f32[8,128]{1,0:T(8,128)} %copy-done.19) | copy-start | bytes 12292

commit v7 on v6

--- a/solution.py
+++ b/solution.py
@@ -86,16 +86,12 @@
     return total
 
 
-def local(body, outs, *args, off_chip=(), scratch=()):
+def local(body, outs, *args):
     return pl.pallas_call(
         body,
         out_shape=tuple(jax.ShapeDtypeStruct(s, d) for s, d in outs),
         in_specs=[pl.BlockSpec(memory_space=pltpu.VMEM) for _ in args],
-        out_specs=tuple(
-            pl.BlockSpec(memory_space=pltpu.HBM if i in off_chip else pltpu.VMEM)
-            for i in range(len(outs))
-        ),
-        scratch_shapes=scratch,
+        out_specs=tuple(pl.BlockSpec(memory_space=pltpu.VMEM) for _ in outs),
         compiler_params=pltpu.CompilerParams(vmem_limit_bytes=16 << 20),
     )(*args)
 
@@ -218,23 +214,19 @@
     post = lax.rsqrt(square / model + EPS)
     final_squares = own + post * (2.0 * cross + post * bent)
     final = lax.rsqrt(jnp.maximum(final_squares, 0.0) / model + EPS)
-    pre = lax.rsqrt(own / model + EPS)
-    scales[...] = jnp.where(lane == 0, post, jnp.where(lane == 1, final, pre))
+    scales[...] = jnp.where(lane == 0, post, final)
     put_copies(out, branch[...].astype(BF16), [post, final])
 
 
-def logit_step(near, far, inputs, gains, head, out, final_out, message, final, sem):
+def logit_step(near, far, inputs, gains, head, out, final, message):
     rejoin(near, far, message)
     width = final.shape[1]
     post, scale = read_stats(message[:, tail_of(width)].astype(F32), width, 2)
     resid = inputs[...].astype(F32) + message[:, :width].astype(F32) * post * gains[1:2]
     final[...] = (resid * scale * gains[2:3]).astype(BF16)
-    copy = pltpu.make_async_copy(final, final_out, sem)
-    copy.start()
     for i in range(0, head.shape[1], CHUNK):
         columns = slice(i, i + CHUNK)
         out[:, columns] = contract(final[...], head[:, columns], 1, 0).astype(BF16)
-    copy.wait()
 
 
 def soft_step(message, ids, out):
@@ -339,32 +331,43 @@
 
 
 def normed_step(
-    model, message, gate_weight, up_weight, active, branch, weighted, mine, theirs, rates
+    model,
+    message,
+    gate_weight,
+    up_weight,
+    active,
+    branch,
+    weighted,
+    gains,
+    final,
+    mine,
+    theirs,
+    rates,
+    final_copy,
 ):
+    final_copy[...] = final[...]
     width, hidden = gate_weight.shape
     start = padded(hidden)
     total = contract(message[:, :hidden], gate_weight[...], 1, 1) + contract(
         message[:, start : start + hidden], up_weight[...], 1, 1
     )
     back, back_post = read_stats(message[:, tail_of(hidden)].astype(F32), hidden, 2)
-    put_halves(mine, theirs, total, [back])
     (squares,) = read_stats(active[:, tail_of(hidden)].astype(F32), hidden, 1)
+    scale = lax.rsqrt(squares / model + EPS)
+    put_halves(mine, theirs, total * scale * gains[0:1], [scale * scale * back / model])
     (post,) = read_stats(branch[:, tail_of(width)].astype(F32), width, 1)
     spread, pull = read_stats(weighted[:, tail_of(width)].astype(F32), width, 2)
     lane = lax.broadcasted_iota(jnp.int32, rates.shape, 1)
     tile = jnp.where(lane == 0, spread, pull)
     tile = jnp.where(lane == 2, post * post * post * back_post / model, tile)
-    rates[...] = jnp.where(lane == 3, lax.rsqrt(squares / model + EPS), tile)
-
-
-def last_step(model, message, grad_resid, inputs, scales, gains, out):
+    rates[...] = jnp.where(lane == 3, scale, tile)
+
+
+def last_step(message, grad_resid, inputs, out):
     width = out.shape[1]
-    scale = scales[:, 2:3]
     (back,) = read_stats(summed(message, tail_of(width)), width, 1)
-    weighted = summed(message, slice(0, width)) * gains[0:1]
-    out[...] = (
-        grad_resid[...] + scale * weighted - inputs[...].astype(F32) * (scale * scale * back / model)
-    ).astype(BF16)
+    total = grad_resid[...] + summed(message, slice(0, width))
+    out[...] = (total - inputs[...].astype(F32) * back).astype(BF16)
 
 
 def shards(
@@ -461,8 +464,6 @@
         inputs,
         gains,
         head_weight,
-        off_chip=(1,),
-        scratch=(pltpu.VMEM((tokens, width), BF16), pltpu.SemaphoreType.DMA),
     )
     (message,) = local(
         soft_step,
@@ -503,28 +504,29 @@
         gelu_slope,
     )
     grads_in = flat(exchange(message, "width"))
-    mine, theirs, rates = local(
+    mine, theirs, rates, final = local(
         lambda *refs: normed_step(model, *refs),
-        [*halves, ((tokens, LANES), F32)],
+        [*halves, ((tokens, LANES), F32), ((tokens, width), BF16)],
         grads_in,
         gate_weight,
         up_weight,
         active,
         branch_all,
         weighted,
-    )
+        gains,
+        final,
+    )
+    scale_pre = rates[:, 3:4]
     message, rates = reduced(mine, theirs, width, 1, rates)
     (grad_hidden,) = local(
-        lambda *refs: last_step(model, *refs),
+        last_step,
         [((tok_dev, width), BF16)],
         message,
         grad_resid,
         hidden,
-        scales,
-        gains,
-    )
-
-    spread, pull, along, scale_pre = [rates[:, i : i + 1] for i in range(4)]
+    )
+
+    spread, pull, along, late_scale = [rates[:, i : i + 1] for i in range(4)]
     delta = (spread * sloped[:, :vocab].astype(F32) + jnp.where(hits, pull, 0.0)).astype(BF16)
     grad_head = contract(final, delta, 0, 0).astype(BF16)
     grad_branch = (
@@ -533,6 +535,7 @@
     grad_down = contract(active[:, :ff], grad_branch, 0, 0).astype(BF16)
     normed = (inputs.astype(F32) * scale_pre * pre_gain).astype(BF16)
     grad_gate = contract(normed, grads_in[:, :ff], 0, 0).astype(BF16)
+    normed = (inputs.astype(F32) * late_scale * pre_gain).astype(BF16)
     grad_up = contract(normed, grads_in[:, padded(ff) : padded(ff) + ff], 0, 0).astype(BF16)
     return (grad_hidden, grad_gate, grad_up, grad_down, grad_head, loss[0, 0])
 

time: 245 us -> 243 us (level)
  transfers between devices with their start and end apart: 8 -> 8, of which waited for: 8 -> 7; matrix products, arithmetic and copies ran while one was open for 5% -> 6% of each run, Pallas kernels for 0% -> 0%
where the time goes in v7:
time: 243 us; the launch traced here: 242 us
  blocking collectives  170 us (70%)
  starting transfers between devices  33 us (14%)
  matrix products  13.1 us (5%)
  Pallas kernels  11.4 us (5%)
  waiting for transfers between devices  10.1 us (4%)
  local copies, waits for them, and re-layouts  3.63 us (1%)
    all_to_all x11, blocking collectives, exchange(): return lax.all_to_all(parts, axis, 0, 0, tiled=True)  170 us
    ppermute x6, starting transfers between devices, swap(): return lax.ppermute(values, 'core', [(0, 1), (1, 0)])  17.1 us
    all_to_all x2, starting transfers between devices, exchange(): return lax.all_to_all(parts, axis, 0, 0, tiled=True)  15.9 us
    dot_general x5, matrix products, contract(): lax.dot_general(left, right, (((left_dim,), (right_dim,)), ((), ())), pre...  13.1 us
    pallas_call x16, Pallas kernels, local(): pl.pallas_call(body, out_shape=tuple((jax.ShapeDtypeStruct(s, d) for s, d...  11.4 us
    all_to_all x2, waiting for transfers between devices, exchange(): return lax.all_to_all(parts, axis, 0, 0, tiled=True)  5.26 us
  transfers between devices with their start and end apart: 8, of which 7 were waited for; matrix products, arithmetic and copies ran while one was open for 6% of the time, Pallas kernels for 0%

profile of v7, /device:TPU:1, one launch (start us, length us, event | category | flops | bytes accessed | tf_op | source)
XLA Modules:
  0.0 242.1 jit_solution(2947976334774709092)
XLA Ops:
  0.6 1.4 broadcast_in_dim.33
  2.0 11.7 %all-to-all-start = ((bf16[16,8,576]{2,1,0:T(8,128)(2,1)}), bf16[16,8,576]{2,1,0:T(8,128)(2,1)S(1)}, u32[]{:S(2)}, u32[]{:S(2)}) async-start(bf16[16,8,576]{2,1,0:T(8,128)(2,1)} %broadcast_in_dim.33), calls=%async_computation | async-start | bytes 327680 | tf_op jit(solution)/shard_map/all_to_all | solution.py:103
  13.8 0.8 reshape.65
  14.8 4.0 %fusion.7 = bf16[256,576]{0,1:T(8,128)(2,1)S(1)} fusion(bf16[576,4096]{1,0:T(8,128)(2,1)} %head.5, s32[256]{0:T(256)S(1)} %sub.22), kind=kOutput, calls=%fused_computation.13 | convolution fusion | flops 1209155584 | bytes 5014528 | tf_op jit(solution)/shard_map/dot_general | solution.py:21
  19.1 3.6 %all-to-all-done = bf16[16,8,576]{2,1,0:T(8,128)(2,1)S(1)} async-done(((bf16[16,8,576]{2,1,0:T(8,128)(2,1)}), bf16[16,8,576]{2,1,0:T(8,128)(2,1)S(1)}, u32[]{:S(2)}, u32[]{:S(2)}) %all-to-all-start) | async-done | bytes 147488 | tf_op jit(solution)/shard_map/all_to_all | solution.py:103
  22.7 2.3 collective-permute-start
  25.4 0.2 copy.24.target_rows
  25.6 0.5 collective-permute-done.far
  26.1 0.8 shard_map.145
  26.9 14.6 %all_to_all.65.refs_0_ = bf16[8,32,1280]{2,1,0:T(8,128)(2,1)S(1)} all-to-all(bf16[8,32,1280]{2,1,0:T(8,128)(2,1)S(1)} %bitcast.36), channel_id=1, replica_groups=mesh['rows'=16,'core'=2,'width'=8] {'width'}, dimensions={0} | all-to-all | bytes 1310720 | tf_op jit(solution)/shard_map/all_to_all | solution.py:103
  41.5 0.2 shard_map.146
  41.7 9.4 %all_to_all.66 = bf16[8,32,640]{2,1,0:T(8,128)(2,1)S(1)} all-to-all(bf16[8,32,640]{2,1,0:T(8,128)(2,1)S(1)} %get-tuple-element.41), channel_id=1, replica_groups=mesh['rows'=16,'core'=2,'width'=8] {'width'}, dimensions={0} | all-to-all | bytes 655360 | tf_op jit(solution)/shard_map/all_to_all | solution.py:103
  51.1 0.5 shard_map.147
  51.6 2.8 %collective-permute-start.1 = (bf16[128,1152]{1,0:T(8,128)(2,1)S(1)}, bf16[128,1152]{1,0:T(8,128)(2,1)S(1)}, u32[]{:S(2)}, u32[]{:S(2)}) collective-permute-start(bf16[128,1152]{1,0:T(8,128)(2,1)S(1)} %get-tuple-element.44), channel_id=1, source_target_pairs={{0,8},{8,0},{1,9},{9,1},{2,10},{10,2},{3,11},{11,3},{4,12},{12,4},... | collective-permute-start | bytes 884744 | tf_op jit(solution)/shard_map/ppermute | solution.py:128
  54.4 1.2 collective-permute-done.1.refs_1_
  55.6 15.8 %all_to_all.67.message = bf16[16,8,1152]{2,1,0:T(8,128)(2,1)S(1)} all-to-all(bf16[16,8,1152]{2,1,0:T(8,128)(2,1)S(1)} %bitcast.30), channel_id=1, replica_groups=mesh['rows'=16,'core'=2,'width'=8] {'rows'}, dimensions={0} | all-to-all | bytes 589824 | tf_op jit(solution)/shard_map/all_to_all | solution.py:103
  71.6 7.5 %all_to_all.68.refs_0_ = f32[8,8,128]{2,1,0:T(8,128)S(1)} all-to-all(f32[8,8,128]{2,1,0:T(8,128)S(1)} %get-tuple-element.46), channel_id=1, replica_groups=mesh['rows'=16,'core'=2,'width'=8] {'width'}, dimensions={0} | all-to-all | bytes 65536 | tf_op jit(solution)/shard_map/all_to_all | solution.py:103
  79.2 14.3 %all_to_all.69 = bf16[16,8,640]{2,1,0:T(8,128)(2,1)S(1)} all-to-all(bf16[16,8,640]{2,1,0:T(8,128)(2,1)S(1)} %get-tuple-element.48), channel_id=1, replica_groups=mesh['rows'=16,'core'=2,'width'=8] {'rows'}, dimensions={0} | all-to-all | bytes 327680 | tf_op jit(solution)/shard_map/all_to_all | solution.py:103
  93.5 3.6 %collective-permute-start.2 = (bf16[128,640]{1,0:T(8,128)(2,1)S(1)}, bf16[128,640]{1,0:T(8,128)(2,1)S(1)}, u32[]{:S(2)}, u32[]{:S(2)}) collective-permute-start(bf16[128,640]{1,0:T(8,128)(2,1)S(1)} %bitcast.33), channel_id=1, source_target_pairs={{0,8},{8,0},{1,9},{9,1},{2,10},{10,2},{3,11},{11,3},{4,12},{12,4},... | collective-permute-start | bytes 491528 | tf_op jit(solution)/shard_map/ppermute | solution.py:128
  97.1 1.0 collective-permute-done.2.far
  98.1 1.9 shard_map.151
  100.1 28.7 %all_to_all.70.message = bf16[8,32,4096]{2,1,0:T(8,128)(2,1)S(1)} all-to-all(bf16[8,32,4096]{2,1,0:T(8,128)(2,1)S(1)} %bitcast.29), channel_id=1, replica_groups=mesh['rows'=16,'core'=2,'width'=8] {'width'}, dimensions={0} | all-to-all | bytes 4194304 | tf_op jit(solution)/shard_map/all_to_all | solution.py:103
  128.7 0.7 shard_map.152
  129.4 28.4 %all_to_all.71 = bf16[8,32,4224]{2,1,0:T(8,128)(2,1)S(1)} all-to-all(bf16[8,32,4224]{2,1,0:T(8,128)(2,1)S(1)} %shard_map.152), channel_id=1, replica_groups=mesh['rows'=16,'core'=2,'width'=8] {'width'}, dimensions={0} | all-to-all | bytes 4325376 | tf_op jit(solution)/shard_map/all_to_all | solution.py:103
  157.8 1.9 shard_map.153
  159.7 3.0 %collective-permute-start.3 = (bf16[128,640]{1,0:T(8,128)(2,1)S(1)}, bf16[128,640]{1,0:T(8,128)(2,1)S(1)}, u32[]{:S(2)}, u32[]{:S(2)}) collective-permute-start(bf16[128,640]{1,0:T(8,128)(2,1)S(1)} %get-tuple-element.53), channel_id=1, source_target_pairs={{0,8},{8,0},{1,9},{9,1},{2,10},{10,2},{3,11},{11,3},{4,12},{12,4},... | collective-permute-start | bytes 491528 | tf_op jit(solution)/shard_map/ppermute | solution.py:128
  162.7 1.0 collective-permute-done.3.refs_1_
  163.9 12.0 %all_to_all.72.refs_0_ = bf16[16,8,640]{2,1,0:T(8,128)(2,1)S(1)} all-to-all(bf16[16,8,640]{2,1,0:T(8,128)(2,1)S(1)} %bitcast.35), channel_id=1, replica_groups=mesh['rows'=16,'core'=2,'width'=8] {'rows'}, dimensions={0} | all-to-all | bytes 327680 | tf_op jit(solution)/shard_map/all_to_all | solution.py:103
  175.9 0.4 shard_map.155
  176.3 13.7 %all_to_all.73 = bf16[16,8,640]{2,1,0:T(8,128)(2,1)S(1)} all-to-all(bf16[16,8,640]{2,1,0:T(8,128)(2,1)S(1)} %get-tuple-element.57), channel_id=1, replica_groups=mesh['rows'=16,'core'=2,'width'=8] {'rows'}, dimensions={0} | all-to-all | bytes 327680 | tf_op jit(solution)/shard_map/all_to_all | solution.py:103
  190.0 2.4 collective-permute-start.4
  192.4 1.0 collective-permute-done.4.refs_1_
  193.4 1.2 shard_map.156
  194.7 13.2 %all_to_all.74.refs_0_ = bf16[8,32,1280]{2,1,0:T(8,128)(2,1)S(1)} all-to-all(bf16[8,32,1280]{2,1,0:T(8,128)(2,1)S(1)} %bitcast.37), channel_id=1, replica_groups=mesh['rows'=16,'core'=2,'width'=8] {'width'}, dimensions={0} | all-to-all | bytes 1310720 | tf_op jit(solution)/shard_map/all_to_all | solution.py:103
  207.9 0.2 shard_map.157
  208.1 12.2 %all_to_all.75 = bf16[8,32,1280]{2,1,0:T(8,128)(2,1)S(1)} all-to-all(bf16[8,32,1280]{2,1,0:T(8,128)(2,1)S(1)} %shard_map.157), channel_id=1, replica_groups=mesh['rows'=16,'core'=2,'width'=8] {'width'}, dimensions={0} | all-to-all | bytes 1310720 | tf_op jit(solution)/shard_map/all_to_all | solution.py:103
  220.3 0.8 shard_map.158
  221.1 0.2 slice_reduce_fusion.4
  221.3 3.0 %collective-permute-start.5 = (bf16[128,640]{1,0:T(8,128)(2,1)S(1)}, bf16[128,640]{1,0:T(8,128)(2,1)S(1)}, u32[]{:S(2)}, u32[]{:S(2)}) collective-permute-start(bf16[128,640]{1,0:T(8,128)(2,1)S(1)} %get-tuple-element.67), channel_id=1, source_target_pairs={{0,8},{8,0},{1,9},{9,1},{2,10},{10,2},{3,11},{11,3},{4,12},{12,4},... | collective-permute-start | bytes 491528 | tf_op jit(solution)/shard_map/ppermute | solution.py:128
  224.3 1.4 convolution_convert_fusion.3
  225.7 0.8 shard_map.159
  226.5 0.3 slice_reduce_fusion.1
  226.8 4.2 %all-to-all-start.12 = ((bf16[16,8,640]{2,1,0:T(8,128)(2,1)}), bf16[16,8,640]{2,1,0:T(8,128)(2,1)}, u32[]{:S(2)}, u32[]{:S(2)}) async-start(bf16[16,8,640]{2,1,0:T(8,128)(2,1)} %bitcast.14), calls=%async_computation.12 | async-start | bytes 327680 | tf_op jit(solution)/shard_map/all_to_all | solution.py:103
  231.1 4.9 %convolution_convert_fusion = bf16[576,4096]{1,0:T(8,128)(2,1)} fusion(bf16[256,576]{1,0:T(8,128)(2,1)} %copy-done.17, bf16[256,4224]{1,0:T(8,128)(2,1)S(1)} %bitcast.22, f32[256]{0:T(256)S(1)} %get-tuple-element.75, f32[256]{0:T(256)S(1)} %get-tuple-element.74, s32[256]{0:T(256)} %copy-done.23), kind=kOutput, calls=%fused_computation | convolution fusion | flops 1216610304 | bytes 7113728 | tf_op jit(solution)/shard_map/dot_general | solution.py:21
  236.0 1.4 convolution_convert_fusion.2
  237.4 1.4 convolution_convert_fusion.1
  238.8 1.7 all-to-all-done.12.message
  240.4 1.6 shard_map.160
  (69 shorter events, 1.2 us)
Async XLA Ops:
  2.0 20.7 %all-to-all-start = ((bf16[16,8,576]{2,1,0:T(8,128)(2,1)}), bf16[16,8,576]{2,1,0:T(8,128)(2,1)S(1)}, u32[]{:S(2)}, u32[]{:S(2)}) async-start(bf16[16,8,576]{2,1,0:T(8,128)(2,1)} %broadcast_in_dim.33), calls=%async_computation | async-start | bytes 327680 | tf_op jit(solution)/shard_map/all_to_all | solution.py:103
  14.7 4.3 %copy-start.23 = (s32[256]{0:T(256)}, s32[256]{0:T(256)S(1)}, u32[]{:S(2)}) copy-start(s32[256]{0:T(256)S(1)} %sub.22) | copy-start | bytes 3076
  14.7 4.1 %copy-start.24 = (f32[32]{0:T(128)S(1)}, f32[32]{0:T(128)}, u32[]{:S(2)}) copy-start(f32[32]{0:T(128)} %param.19) | copy-start | bytes 388
  14.8 10.4 %copy-start.18 = (f32[576]{0:T(1024)S(1)}, f32[576]{0:T(1024)}, u32[]{:S(2)}) copy-start(f32[576]{0:T(1024)} %param.12) | copy-start | bytes 6916
  14.8 10.4 %copy-start.19 = (f32[576]{0:T(1024)S(1)}, f32[576]{0:T(1024)}, u32[]{:S(2)}) copy-start(f32[576]{0:T(1024)} %param.13) | copy-start | bytes 6916
  14.8 10.4 %copy-start.20 = (f32[576]{0:T(1024)S(1)}, f32[576]{0:T(1024)}, u32[]{:S(2)}) copy-start(f32[576]{0:T(1024)} %param.11) | copy-start | bytes 6916
  14.8 11.3 %copy-start.1 = (bf16[576,576]{1,0:T(8,128)(2,1)S(1)}, bf16[576,576]{1,0:T(8,128)(2,1)}, u32[]{:S(2)}) copy-start(bf16[576,576]{1,0:T(8,128)(2,1)} %refs_1_.1) | copy-start | bytes 1990660
  14.8 11.3 %copy-start.2 = (bf16[576,576]{1,0:T(8,128)(2,1)S(1)}, bf16[576,576]{1,0:T(8,128)(2,1)}, u32[]{:S(2)}) copy-start(bf16[576,576]{1,0:T(8,128)(2,1)} %refs_2_.1) | copy-start | bytes 1990660
  18.9 32.3 %copy-start.4 = (bf16[576,576]{1,0:T(8,128)(2,1)S(1)}, bf16[576,576]{1,0:T(8,128)(2,1)}, u32[]{:S(2)}) copy-start(bf16[576,576]{1,0:T(8,128)(2,1)} %refs_3_.3) | copy-start | bytes 1990660
  22.7 3.4 %collective-permute-start = (bf16[128,576]{1,0:T(8,128)(2,1)S(1)}, bf16[128,576]{1,0:T(8,128)(2,1)S(1)}, u32[]{:S(2)}, u32[]{:S(2)}) collective-permute-start(bf16[128,576]{1,0:T(8,128)(2,1)S(1)} %bitcast.31), channel_id=1, source_target_pairs={{0,8},{8,0},{1,9},{9,1},{2,10},{10,2},{3,11},{11,3},{4,12},{12,4},... | collective-permute-start | bytes 442376 | tf_op jit(solution)/shard_map/ppermute | solution.py:128
  25.4 46.1 %copy-start.12 = (bf16[8,576]{1,0:T(8,128)(2,1)S(1)}, bf16[8,576]{1,0:T(8,128)(2,1)}, u32[]{:S(2)}) copy-start(bf16[8,576]{1,0:T(8,128)(2,1)} %inputs.3) | copy-start | bytes 27652
  25.6 45.9 %copy-start = (bf16[576,4096]{1,0:T(8,128)(2,1)S(1)}, bf16[576,4096]{1,0:T(8,128)(2,1)}, u32[]{:S(2)}) copy-start(bf16[576,4096]{1,0:T(8,128)(2,1)} %head.5) | copy-start | bytes 14155780
  26.9 197.4 %copy-start.8 = (bf16[256,576]{1,0:T(8,128)(2,1)}, bf16[256,576]{1,0:T(8,128)(2,1)S(1)}, u32[]{:S(2)}) copy-start(bf16[256,576]{1,0:T(8,128)(2,1)S(1)} %get-tuple-element.49.inputs) | copy-start | bytes 884740
  51.6 4.0 %collective-permute-start.1 = (bf16[128,1152]{1,0:T(8,128)(2,1)S(1)}, bf16[128,1152]{1,0:T(8,128)(2,1)S(1)}, u32[]{:S(2)}, u32[]{:S(2)}) collective-permute-start(bf16[128,1152]{1,0:T(8,128)(2,1)S(1)} %get-tuple-element.44), channel_id=1, source_target_pairs={{0,8},{8,0},{1,9},{9,1},{2,10},{10,2},{3,11},{11,3},{4,12},{12,4},... | collective-permute-start | bytes 884744 | tf_op jit(solution)/shard_map/ppermute | solution.py:128
  93.5 4.6 %collective-permute-start.2 = (bf16[128,640]{1,0:T(8,128)(2,1)S(1)}, bf16[128,640]{1,0:T(8,128)(2,1)S(1)}, u32[]{:S(2)}, u32[]{:S(2)}) collective-permute-start(bf16[128,640]{1,0:T(8,128)(2,1)S(1)} %bitcast.33), channel_id=1, source_target_pairs={{0,8},{8,0},{1,9},{9,1},{2,10},{10,2},{3,11},{11,3},{4,12},{12,4},... | collective-permute-start | bytes 491528 | tf_op jit(solution)/shard_map/ppermute | solution.py:128
  157.8 18.1 %copy-start.13 = (bf16[8,576]{1,0:T(8,128)(2,1)S(1)}, bf16[8,576]{1,0:T(8,128)(2,1)}, u32[]{:S(2)}) copy-start(bf16[8,576]{1,0:T(8,128)(2,1)} %inputs.3) | copy-start | bytes 27652
  157.8 35.6 %copy-start.5 = (bf16[576,576]{1,0:T(8,128)(2,1)S(1)}, bf16[576,576]{1,0:T(8,128)(2,1)}, u32[]{:S(2)}) copy-start(bf16[576,576]{1,0:T(8,128)(2,1)} %refs_3_.3) | copy-start | bytes 1990660
  159.7 60.6 %copy-start.3 = (bf16[576,576]{1,0:T(8,128)(2,1)S(1)}, bf16[576,576]{1,0:T(8,128)(2,1)}, u32[]{:S(2)}) copy-start(bf16[576,576]{1,0:T(8,128)(2,1)} %refs_2_.1) | copy-start | bytes 1990660
  159.7 4.0 %collective-permute-start.3 = (bf16[128,640]{1,0:T(8,128)(2,1)S(1)}, bf16[128,640]{1,0:T(8,128)(2,1)S(1)}, u32[]{:S(2)}, u32[]{:S(2)}) collective-permute-start(bf16[128,640]{1,0:T(8,128)(2,1)S(1)} %get-tuple-element.53), channel_id=1, source_target_pairs={{0,8},{8,0},{1,9},{9,1},{2,10},{10,2},{3,11},{11,3},{4,12},{12,4},... | collective-permute-start | bytes 491528 | tf_op jit(solution)/shard_map/ppermute | solution.py:128
  176.3 44.8 %copy-start.15 = (f32[8,576]{1,0:T(8,128)}, f32[8,576]{1,0:T(8,128)S(1)}, u32[]{:S(2)}) copy-start(f32[8,576]{1,0:T(8,128)S(1)} %get-tuple-element.70.grad_resid) | copy-start | bytes 55300
  190.0 3.4 %collective-permute-start.4 = (bf16[128,640]{1,0:T(8,128)(2,1)S(1)}, bf16[128,640]{1,0:T(8,128)(2,1)S(1)}, u32[]{:S(2)}, u32[]{:S(2)}) collective-permute-start(bf16[128,640]{1,0:T(8,128)(2,1)S(1)} %bitcast.38), channel_id=1, source_target_pairs={{0,8},{8,0},{1,9},{9,1},{2,10},{10,2},{3,11},{11,3},{4,12},{12,4},... | collective-permute-start | bytes 491528 | tf_op jit(solution)/shard_map/ppermute | solution.py:128
  194.7 31.0 %copy-start.10 = (bf16[256,640]{1,0:T(8,128)(2,1)}, bf16[256,640]{1,0:T(8,128)(2,1)S(1)}, u32[]{:S(2)}) copy-start(bf16[256,640]{1,0:T(8,128)(2,1)S(1)} %get-tuple-element.64.refs_5_) | copy-start | bytes 983044
  194.7 29.6 %copy-start.21 = (f32[576]{0:T(1024)S(1)}, f32[576]{0:T(1024)}, u32[]{:S(2)}) copy-start(f32[576]{0:T(1024)} %param.11) | copy-start | bytes 6916
  220.2 4.0 %copy-start.6 = (bf16[8,32,1280]{2,1,0:T(8,128)(2,1)}, bf16[8,32,1280]{2,1,0:T(8,128)(2,1)S(1)}, u32[]{:S(2)}) copy-start(bf16[8,32,1280]{2,1,0:T(8,128)(2,1)S(1)} %all_to_all.75) | copy-start | bytes 1966084
  221.1 5.7 %copy-start.17 = (bf16[256,576]{1,0:T(8,128)(2,1)}, bf16[256,576]{1,0:T(8,128)(2,1)S(1)}, u32[]{:S(2)}) copy-start(bf16[256,576]{1,0:T(8,128)(2,1)S(1)} %get-tuple-element.72) | copy-start | bytes 884740
  221.3 4.4 %collective-permute-start.5 = (bf16[128,640]{1,0:T(8,128)(2,1)S(1)}, bf16[128,640]{1,0:T(8,128)(2,1)S(1)}, u32[]{:S(2)}, u32[]{:S(2)}) collective-permute-start(bf16[128,640]{1,0:T(8,128)(2,1)S(1)} %get-tuple-element.67), channel_id=1, source_target_pairs={{0,8},{8,0},{1,9},{9,1},{2,10},{10,2},{3,11},{11,3},{4,12},{12,4},... | collective-permute-start | bytes 491528 | tf_op jit(solution)/shard_map/ppermute | solution.py:128
  226.8 13.6 %all-to-all-start.12 = ((bf16[16,8,640]{2,1,0:T(8,128)(2,1)}), bf16[16,8,640]{2,1,0:T(8,128)(2,1)}, u32[]{:S(2)}, u32[]{:S(2)}) async-start(bf16[16,8,640]{2,1,0:T(8,128)(2,1)} %bitcast.14), calls=%async_computation.12 | async-start | bytes 327680 | tf_op jit(solution)/shard_map/all_to_all | solution.py:103
  231.0 5.0 %copy-start.7 = (bf16[8,32,1280]{2,1,0:T(8,128)(2,1)S(1)}, bf16[8,32,1280]{2,1,0:T(8,128)(2,1)}, u32[]{:S(2)}) copy-start(bf16[8,32,1280]{2,1,0:T(8,128)(2,1)} %copy-done.6) | copy-start | bytes 1966084
  231.0 5.0 %copy-start.9 = (bf16[256,576]{1,0:T(8,128)(2,1)S(1)}, bf16[256,576]{1,0:T(8,128)(2,1)}, u32[]{:S(2)}) copy-start(bf16[256,576]{1,0:T(8,128)(2,1)} %copy-done.8) | copy-start | bytes 884740
  231.0 5.0 %copy-start.22 = (f32[576]{0:T(1024)S(1)}, f32[576]{0:T(1024)}, u32[]{:S(2)}) copy-start(f32[576]{0:T(1024)} %param.11) | copy-start | bytes 6916
  231.0 6.4 %copy-start.11 = (bf16[256,640]{1,0:T(8,128)(2,1)S(1)}, bf16[256,640]{1,0:T(8,128)(2,1)}, u32[]{:S(2)}) copy-start(bf16[256,640]{1,0:T(8,128)(2,1)} %copy-done.10) | copy-start | bytes 983044
  231.0 9.4 %copy-start.14 = (bf16[8,576]{1,0:T(8,128)(2,1)S(1)}, bf16[8,576]{1,0:T(8,128)(2,1)}, u32[]{:S(2)}) copy-start(bf16[8,576]{1,0:T(8,128)(2,1)} %inputs.3) | copy-start | bytes 27652
  231.1 9.4 %copy-start.16 = (f32[8,576]{1,0:T(8,128)S(1)}, f32[8,576]{1,0:T(8,128)}, u32[]{:S(2)}) copy-start(f32[8,576]{1,0:T(8,128)} %copy-done.15) | copy-start | bytes 55300

commit v8 on v7

--- a/solution.py
+++ b/solution.py
@@ -86,12 +86,13 @@
     return total
 
 
-def local(body, outs, *args):
+def local(body, outs, *args, reuse=None):
     return pl.pallas_call(
         body,
         out_shape=tuple(jax.ShapeDtypeStruct(s, d) for s, d in outs),
         in_specs=[pl.BlockSpec(memory_space=pltpu.VMEM) for _ in args],
         out_specs=tuple(pl.BlockSpec(memory_space=pltpu.VMEM) for _ in outs),
+        input_output_aliases=reuse or {},
         compiler_params=pltpu.CompilerParams(vmem_limit_bytes=16 << 20),
     )(*args)
 
@@ -218,15 +219,18 @@
     put_copies(out, branch[...].astype(BF16), [post, final])
 
 
-def logit_step(near, far, inputs, gains, head, out, final, message):
-    rejoin(near, far, message)
-    width = final.shape[1]
-    post, scale = read_stats(message[:, tail_of(width)].astype(F32), width, 2)
-    resid = inputs[...].astype(F32) + message[:, :width].astype(F32) * post * gains[1:2]
-    final[...] = (resid * scale * gains[2:3]).astype(BF16)
+def logit_step(part, piece, inputs, gains, head, *rest):
+    out, final, message = rest[-3:]
+    half, width = piece.shape[0], final.shape[1]
+    rows = slice(part * half, (part + 1) * half)
+    message[rows] = piece[...]
+    post, scale = read_stats(piece[:, tail_of(width)].astype(F32), width, 2)
+    resid = inputs[rows].astype(F32) + piece[:, :width].astype(F32) * post * gains[1:2]
+    value = (resid * scale * gains[2:3]).astype(BF16)
+    final[rows] = value
     for i in range(0, head.shape[1], CHUNK):
         columns = slice(i, i + CHUNK)
-        out[:, columns] = contract(final[...], head[:, columns], 1, 0).astype(BF16)
+        out[rows, columns] = contract(value, head[:, columns], 1, 0).astype(BF16)
 
 
 def soft_step(message, ids, out):
@@ -255,11 +259,11 @@
         out[j, :, vocab : vocab + LANES] = tile
 
 
-def row_step(message, head, mine, theirs):
+def row_step(start, message, head, out):
     vocab = head.shape[1]
-    total = contract(message[:, :vocab], head[...], 1, 1)
-    stats = read_stats(message[:, vocab : vocab + LANES].astype(F32), vocab, 3)
-    put_halves(mine, theirs, total, stats)
+    rows = slice(start, start + out.shape[0])
+    stats = read_stats(message[rows, vocab : vocab + LANES].astype(F32), vocab, 3)
+    put(out, contract(message[rows, :vocab], head[...], 1, 1).astype(out.dtype), stats)
 
 
 def resid_step(
@@ -294,21 +298,25 @@
     )
 
 
-def down_step(copies_n, near, far, branch, down_weight, out, message, loss):
-    rejoin(near, far, message)
+def down_step(copies_n, part, piece, branch, down_weight, *rest):
+    out, message, loss = rest[-3:]
     hidden, width = down_weight.shape
+    half = piece.shape[0]
+    rows = slice(part * half, (part + 1) * half)
     tail = tail_of(width)
-    _, _, score, back_post = read_stats(message[:, tail].astype(F32), width, 4)
-    post, _ = read_stats(branch[:, tail].astype(F32), width, 2)
+    message[rows] = piece[...]
+    _, _, score, back_post = read_stats(piece[:, tail].astype(F32), width, 4)
+    post, _ = read_stats(branch[rows, tail].astype(F32), width, 2)
     put(
-        out,
-        contract(message[:, :width], down_weight[...], 1, 1).astype(BF16),
+        out.at[rows],
+        contract(piece[:, :width], down_weight[...], 1, 1).astype(BF16),
         [back_post, post / copies_n],
     )
-    out[:, padded(hidden) : padded(hidden) + hidden] = contract(
-        branch[:, :width], down_weight[...], 1, 1
+    out[rows, padded(hidden) : padded(hidden) + hidden] = contract(
+        branch[rows, :width], down_weight[...], 1, 1
     ).astype(BF16)
-    loss[...] = -jnp.sum(score, axis=0, keepdims=True) / message.shape[0]
+    score = -jnp.sum(score, axis=0, keepdims=True) / out.shape[0]
+    loss[...] = loss[...] + score if part else score
 
 
 def hidden_step(model, message, gate, upward, gelu_gate, gelu_slope, out):
@@ -452,19 +460,23 @@
         branch,
     )
     near, far = gathered(message)
-    message, final, branch_all = local(
-        logit_step,
-        [
-            ((tokens, vocab), BF16),
-            ((tokens, width), BF16),
-            ((tokens, padded(width)), BF16),
-        ],
-        near,
-        far,
-        inputs,
-        gains,
-        head_weight,
-    )
+    filled = ()
+    for part, piece in enumerate((near, far)):
+        filled = local(
+            lambda *refs, part=part: logit_step(part, *refs),
+            [
+                ((tokens, vocab), BF16),
+                ((tokens, width), BF16),
+                ((tokens, padded(width)), BF16),
+            ],
+            piece,
+            inputs,
+            gains,
+            head_weight,
+            *filled,
+            reuse={4 + i: i for i in range(len(filled))},
+        )
+    message, final, branch_all = filled
     (message,) = local(
         soft_step,
         [((cols_n, sub, vocab + LANES), BF16)],
@@ -473,7 +485,8 @@
     )
     sloped = flat(exchange(message, "width"))
     halves = [((half, padded(width)), F32), ((half, padded(width)), BF16)]
-    mine, theirs = local(row_step, halves, sloped, head_weight)
+    (theirs,) = local(lambda *refs: row_step(half, *refs), halves[1:], sloped, head_weight)
+    (mine,) = local(lambda *refs: row_step(0, *refs), halves[:1], sloped, head_weight)
     grad_resid, message = local(
         lambda *refs: resid_step(model, *refs),
         [((tok_dev, width), F32), ((rows_n, tok_dev, padded(width)), BF16)],
@@ -486,14 +499,18 @@
         gains,
     )
     near, far = gathered(message)
-    message, weighted, loss = local(
-        lambda *refs: down_step(cols_n, *refs),
-        [((tokens, padded(ff) * 2), BF16), ((tokens, padded(width)), BF16), ((1, 1), F32)],
-        near,
-        far,
-        branch_all,
-        down_weight,
-    )
+    filled = ()
+    for part, piece in enumerate((near, far)):
+        filled = local(
+            lambda *refs, part=part: down_step(cols_n, part, *refs),
+            [((tokens, padded(ff) * 2), BF16), ((tokens, padded(width)), BF16), ((1, 1), F32)],
+            piece,
+            branch_all,
+            down_weight,
+            *filled,
+            reuse={3 + i: i for i in range(len(filled))},
+        )
+    message, weighted, loss = filled
     (message,) = local(
         lambda *refs: hidden_step(model, *refs),
         [((cols_n, sub, padded(ff) * 2), BF16)],

time: 243 us -> 243 us (level)
  waiting for transfers between devices: 10.1 us -> 7.08 us
  Pallas kernels: 11.4 us -> 13.9 us
    ppermute x6, waiting for transfers between devices: 4.81 us -> 1.78 us  [swap(): return lax.ppermute(values, 'core', [(0, 1), (1, 0)])]
    pallas_call x16 -> x19, Pallas kernels: 11.4 us -> 13.9 us  [local(): pl.pallas_call(body, out_shape=tuple((jax.ShapeDtypeStruct(s, d) for s, d...]
  transfers between devices with their start and end apart: 8 -> 8, of which waited for: 7 -> 5; matrix products, arithmetic and copies ran while one was open for 6% -> 6% of each run, Pallas kernels for 0% -> 2%
where the time goes in v8:
time: 243 us; the launch traced here: 242 us
  blocking collectives  170 us (70%)
  starting transfers between devices  33 us (14%)
  Pallas kernels  13.9 us (6%)
  matrix products  13.1 us (5%)
  waiting for transfers between devices  7.08 us (3%)
  local copies, waits for them, and re-layouts  3.93 us (2%)
    all_to_all x11, blocking collectives, exchange(): return lax.all_to_all(parts, axis, 0, 0, tiled=True)  170 us
    ppermute x6, starting transfers between devices, swap(): return lax.ppermute(values, 'core', [(0, 1), (1, 0)])  17.1 us
    all_to_all x2, starting transfers between devices, exchange(): return lax.all_to_all(parts, axis, 0, 0, tiled=True)  15.9 us
    pallas_call x19, Pallas kernels, local(): pl.pallas_call(body, out_shape=tuple((jax.ShapeDtypeStruct(s, d) for s, d...  13.9 us
    dot_general x5, matrix products, contract(): lax.dot_general(left, right, (((left_dim,), (right_dim,)), ((), ())), pre...  13.1 us
    all_to_all x2, waiting for transfers between devices, exchange(): return lax.all_to_all(parts, axis, 0, 0, tiled=True)  5.3 us
  transfers between devices with their start and end apart: 8, of which 5 were waited for; matrix products, arithmetic and copies ran while one was open for 6% of the time, Pallas kernels for 2%

profile of v8, /device:TPU:1, one launch (start us, length us, event | category | flops | bytes accessed | tf_op | source)
XLA Modules:
  0.0 242.2 jit_solution(2086748385844362089)
XLA Ops:
  0.6 1.4 broadcast_in_dim.33
  2.0 11.7 %all-to-all-start = ((bf16[16,8,576]{2,1,0:T(8,128)(2,1)}), bf16[16,8,576]{2,1,0:T(8,128)(2,1)S(1)}, u32[]{:S(2)}, u32[]{:S(2)}) async-start(bf16[16,8,576]{2,1,0:T(8,128)(2,1)} %broadcast_in_dim.33), calls=%async_computation | async-start | bytes 327680 | tf_op jit(solution)/shard_map/all_to_all | solution.py:104
  13.8 0.8 reshape.65
  14.8 4.0 %fusion.7 = bf16[256,576]{0,1:T(8,128)(2,1)S(1)} fusion(bf16[576,4096]{1,0:T(8,128)(2,1)} %refs_1_.4, s32[256]{0:T(256)S(1)} %sub.22), kind=kOutput, calls=%fused_computation.13 | convolution fusion | flops 1209155584 | bytes 5014528 | tf_op jit(solution)/shard_map/dot_general | solution.py:21
  19.1 3.6 %all-to-all-done = bf16[16,8,576]{2,1,0:T(8,128)(2,1)S(1)} async-done(((bf16[16,8,576]{2,1,0:T(8,128)(2,1)}), bf16[16,8,576]{2,1,0:T(8,128)(2,1)S(1)}, u32[]{:S(2)}, u32[]{:S(2)}) %all-to-all-start) | async-done | bytes 147488 | tf_op jit(solution)/shard_map/all_to_all | solution.py:104
  22.7 2.3 collective-permute-start
  25.4 0.2 copy.30.target_rows
  25.6 0.5 collective-permute-done.far
  26.1 0.8 shard_map.145
  26.9 14.6 %all_to_all.65.refs_0_ = bf16[8,32,1280]{2,1,0:T(8,128)(2,1)S(1)} all-to-all(bf16[8,32,1280]{2,1,0:T(8,128)(2,1)S(1)} %bitcast.40), channel_id=1, replica_groups=mesh['rows'=16,'core'=2,'width'=8] {'width'}, dimensions={0} | all-to-all | bytes 1310720 | tf_op jit(solution)/shard_map/all_to_all | solution.py:104
  41.5 0.2 shard_map.146
  41.7 9.4 %all_to_all.66 = bf16[8,32,640]{2,1,0:T(8,128)(2,1)S(1)} all-to-all(bf16[8,32,640]{2,1,0:T(8,128)(2,1)S(1)} %get-tuple-element.45), channel_id=1, replica_groups=mesh['rows'=16,'core'=2,'width'=8] {'width'}, dimensions={0} | all-to-all | bytes 655360 | tf_op jit(solution)/shard_map/all_to_all | solution.py:104
  51.1 0.5 shard_map.147
  51.6 2.8 %collective-permute-start.1 = (bf16[128,1152]{1,0:T(8,128)(2,1)S(1)}, bf16[128,1152]{1,0:T(8,128)(2,1)S(1)}, u32[]{:S(2)}, u32[]{:S(2)}) collective-permute-start(bf16[128,1152]{1,0:T(8,128)(2,1)S(1)} %get-tuple-element.48), channel_id=1, source_target_pairs={{0,8},{8,0},{1,9},{9,1},{2,10},{10,2},{3,11},{11,3},{4,12},{12,4},... | collective-permute-start | bytes 884744 | tf_op jit(solution)/shard_map/ppermute | solution.py:129
  54.4 1.2 collective-permute-done.1.refs_1_
  55.7 15.8 %all_to_all.67.message = bf16[16,8,1152]{2,1,0:T(8,128)(2,1)S(1)} all-to-all(bf16[16,8,1152]{2,1,0:T(8,128)(2,1)S(1)} %bitcast.32), channel_id=1, replica_groups=mesh['rows'=16,'core'=2,'width'=8] {'rows'}, dimensions={0} | all-to-all | bytes 589824 | tf_op jit(solution)/shard_map/all_to_all | solution.py:104
  71.6 7.5 %all_to_all.68.refs_0_ = f32[8,8,128]{2,1,0:T(8,128)S(1)} all-to-all(f32[8,8,128]{2,1,0:T(8,128)S(1)} %get-tuple-element.50), channel_id=1, replica_groups=mesh['rows'=16,'core'=2,'width'=8] {'width'}, dimensions={0} | all-to-all | bytes 65536 | tf_op jit(solution)/shard_map/all_to_all | solution.py:104
  79.2 14.3 %all_to_all.69 = bf16[16,8,640]{2,1,0:T(8,128)(2,1)S(1)} all-to-all(bf16[16,8,640]{2,1,0:T(8,128)(2,1)S(1)} %get-tuple-element.52), channel_id=1, replica_groups=mesh['rows'=16,'core'=2,'width'=8] {'rows'}, dimensions={0} | all-to-all | bytes 327680 | tf_op jit(solution)/shard_map/all_to_all | solution.py:104
  93.5 3.6 %collective-permute-start.2 = (bf16[128,640]{1,0:T(8,128)(2,1)S(1)}, bf16[128,640]{1,0:T(8,128)(2,1)S(1)}, u32[]{:S(2)}, u32[]{:S(2)}) collective-permute-start(bf16[128,640]{1,0:T(8,128)(2,1)S(1)} %bitcast.35), channel_id=1, source_target_pairs={{0,8},{8,0},{1,9},{9,1},{2,10},{10,2},{3,11},{11,3},{4,12},{12,4},... | collective-permute-start | bytes 491528 | tf_op jit(solution)/shard_map/ppermute | solution.py:129
  97.1 1.1 shard_map.151
  98.2 1.1 shard_map.152
  99.3 28.9 %all_to_all.70.message = bf16[8,32,4096]{2,1,0:T(8,128)(2,1)S(1)} all-to-all(bf16[8,32,4096]{2,1,0:T(8,128)(2,1)S(1)} %bitcast.24), channel_id=1, replica_groups=mesh['rows'=16,'core'=2,'width'=8] {'width'}, dimensions={0} | all-to-all | bytes 4194304 | tf_op jit(solution)/shard_map/all_to_all | solution.py:104
  128.1 0.7 shard_map.153
  128.8 28.4 %all_to_all.71 = bf16[8,32,4224]{2,1,0:T(8,128)(2,1)S(1)} all-to-all(bf16[8,32,4224]{2,1,0:T(8,128)(2,1)S(1)} %shard_map.153), channel_id=1, replica_groups=mesh['rows'=16,'core'=2,'width'=8] {'width'}, dimensions={0} | all-to-all | bytes 4325376 | tf_op jit(solution)/shard_map/all_to_all | solution.py:104
  157.2 1.7 shard_map.155
  158.9 2.9 %collective-permute-start.3 = (bf16[128,640]{1,0:T(8,128)(2,1)S(1)}, bf16[128,640]{1,0:T(8,128)(2,1)S(1)}, u32[]{:S(2)}, u32[]{:S(2)}) collective-permute-start(bf16[128,640]{1,0:T(8,128)(2,1)S(1)} %shard_map.155), channel_id=1, source_target_pairs={{0,8},{8,0},{1,9},{9,1},{2,10},{10,2},{3,11},{11,3},{4,12},{12,4},... | collective-permute-start | bytes 491528 | tf_op jit(solution)/shard_map/ppermute | solution.py:129
  161.8 1.7 shard_map.154.refs_0_
  163.8 12.1 %all_to_all.72.refs_0_ = bf16[16,8,640]{2,1,0:T(8,128)(2,1)S(1)} all-to-all(bf16[16,8,640]{2,1,0:T(8,128)(2,1)S(1)} %bitcast.39), channel_id=1, replica_groups=mesh['rows'=16,'core'=2,'width'=8] {'rows'}, dimensions={0} | all-to-all | bytes 327680 | tf_op jit(solution)/shard_map/all_to_all | solution.py:104
  175.8 0.4 shard_map.157
  176.2 13.8 %all_to_all.73 = bf16[16,8,640]{2,1,0:T(8,128)(2,1)S(1)} all-to-all(bf16[16,8,640]{2,1,0:T(8,128)(2,1)S(1)} %get-tuple-element.62), channel_id=1, replica_groups=mesh['rows'=16,'core'=2,'width'=8] {'rows'}, dimensions={0} | all-to-all | bytes 327680 | tf_op jit(solution)/shard_map/all_to_all | solution.py:104
  189.9 2.4 %collective-permute-start.4 = (bf16[128,640]{1,0:T(8,128)(2,1)S(1)}, bf16[128,640]{1,0:T(8,128)(2,1)S(1)}, u32[]{:S(2)}, u32[]{:S(2)}) collective-permute-start(bf16[128,640]{1,0:T(8,128)(2,1)S(1)} %bitcast.37), channel_id=1, source_target_pairs={{0,8},{8,0},{1,9},{9,1},{2,10},{10,2},{3,11},{11,3},{4,12},{12,4},... | collective-permute-start | bytes 491528 | tf_op jit(solution)/shard_map/ppermute | solution.py:129
  192.4 1.0 shard_map.158
  193.4 1.7 shard_map.159
  195.1 13.1 %all_to_all.74.refs_0_ = bf16[8,32,1280]{2,1,0:T(8,128)(2,1)S(1)} all-to-all(bf16[8,32,1280]{2,1,0:T(8,128)(2,1)S(1)} %bitcast.28), channel_id=1, replica_groups=mesh['rows'=16,'core'=2,'width'=8] {'width'}, dimensions={0} | all-to-all | bytes 1310720 | tf_op jit(solution)/shard_map/all_to_all | solution.py:104
  208.2 0.2 shard_map.160
  208.5 12.2 %all_to_all.75 = bf16[8,32,1280]{2,1,0:T(8,128)(2,1)S(1)} all-to-all(bf16[8,32,1280]{2,1,0:T(8,128)(2,1)S(1)} %shard_map.160), channel_id=1, replica_groups=mesh['rows'=16,'core'=2,'width'=8] {'width'}, dimensions={0} | all-to-all | bytes 1310720 | tf_op jit(solution)/shard_map/all_to_all | solution.py:104
  220.7 0.8 shard_map.161
  221.6 0.2 slice_reduce_fusion.4
  221.8 3.0 %collective-permute-start.5 = (bf16[128,640]{1,0:T(8,128)(2,1)S(1)}, bf16[128,640]{1,0:T(8,128)(2,1)S(1)}, u32[]{:S(2)}, u32[]{:S(2)}) collective-permute-start(bf16[128,640]{1,0:T(8,128)(2,1)S(1)} %get-tuple-element.75), channel_id=1, source_target_pairs={{0,8},{8,0},{1,9},{9,1},{2,10},{10,2},{3,11},{11,3},{4,12},{12,4},... | collective-permute-start | bytes 491528 | tf_op jit(solution)/shard_map/ppermute | solution.py:129
  224.8 1.4 convolution_convert_fusion.3
  226.3 0.3 slice_reduce_fusion.1
  226.6 0.3 copy-done.13
  226.9 4.2 %all-to-all-start.12 = ((bf16[16,8,640]{2,1,0:T(8,128)(2,1)}), bf16[16,8,640]{2,1,0:T(8,128)(2,1)}, u32[]{:S(2)}, u32[]{:S(2)}) async-start(bf16[16,8,640]{2,1,0:T(8,128)(2,1)} %bitcast.41), calls=%async_computation.12 | async-start | bytes 327680 | tf_op jit(solution)/shard_map/all_to_all | solution.py:104
  231.2 4.9 %convolution_convert_fusion = bf16[576,4096]{1,0:T(8,128)(2,1)} fusion(bf16[256,576]{1,0:T(8,128)(2,1)} %copy-done.16, bf16[256,4224]{1,0:T(8,128)(2,1)S(1)} %bitcast.23, f32[256]{0:T(256)S(1)} %get-tuple-element.83, f32[256]{0:T(256)S(1)} %get-tuple-element.82, s32[256]{0:T(256)S(1)} %copy-done.22), kind=kOutput, calls=%fused_computation | convolution fusion | flops 1216610304 | bytes 7113728 | tf_op jit(solution)/shard_map/dot_general | solution.py:21
  236.1 1.4 convolution_convert_fusion.2
  237.5 1.4 convolution_convert_fusion.1
  238.9 1.7 all-to-all-done.12.message
  240.6 1.6 shard_map.163
  (70 shorter events, 1.3 us)
Async XLA Ops:
  2.0 20.7 %all-to-all-start = ((bf16[16,8,576]{2,1,0:T(8,128)(2,1)}), bf16[16,8,576]{2,1,0:T(8,128)(2,1)S(1)}, u32[]{:S(2)}, u32[]{:S(2)}) async-start(bf16[16,8,576]{2,1,0:T(8,128)(2,1)} %broadcast_in_dim.33), calls=%async_computation | async-start | bytes 327680 | tf_op jit(solution)/shard_map/all_to_all | solution.py:104
  14.7 4.3 %copy-start.21 = (s32[256]{0:T(256)}, s32[256]{0:T(256)S(1)}, u32[]{:S(2)}) copy-start(s32[256]{0:T(256)S(1)} %sub.22) | copy-start | bytes 3076
  14.7 4.1 %copy-start.23 = (f32[32]{0:T(128)S(1)}, f32[32]{0:T(128)}, u32[]{:S(2)}) copy-start(f32[32]{0:T(128)} %param.19) | copy-start | bytes 388
  14.8 10.4 %copy-start.17 = (f32[576]{0:T(1024)S(1)}, f32[576]{0:T(1024)}, u32[]{:S(2)}) copy-start(f32[576]{0:T(1024)} %param.12) | copy-start | bytes 6916
  14.8 10.4 %copy-start.18 = (f32[576]{0:T(1024)S(1)}, f32[576]{0:T(1024)}, u32[]{:S(2)}) copy-start(f32[576]{0:T(1024)} %param.13) | copy-start | bytes 6916
  14.8 10.4 %copy-start.19 = (f32[576]{0:T(1024)S(1)}, f32[576]{0:T(1024)}, u32[]{:S(2)}) copy-start(f32[576]{0:T(1024)} %param.11) | copy-start | bytes 6916
  14.8 11.3 %copy-start.2 = (bf16[576,576]{1,0:T(8,128)(2,1)S(1)}, bf16[576,576]{1,0:T(8,128)(2,1)}, u32[]{:S(2)}) copy-start(bf16[576,576]{1,0:T(8,128)(2,1)} %refs_1_.5) | copy-start | bytes 1990660
  14.8 11.3 %copy-start.4 = (bf16[576,576]{1,0:T(8,128)(2,1)S(1)}, bf16[576,576]{1,0:T(8,128)(2,1)}, u32[]{:S(2)}) copy-start(bf16[576,576]{1,0:T(8,128)(2,1)} %refs_2_.5) | copy-start | bytes 1990660
  18.9 32.3 %copy-start.1 = (bf16[576,576]{1,0:T(8,128)(2,1)S(1)}, bf16[576,576]{1,0:T(8,128)(2,1)}, u32[]{:S(2)}) copy-start(bf16[576,576]{1,0:T(8,128)(2,1)} %refs_2_.4) | copy-start | bytes 1990660
  22.7 3.4 %collective-permute-start = (bf16[128,576]{1,0:T(8,128)(2,1)S(1)}, bf16[128,576]{1,0:T(8,128)(2,1)S(1)}, u32[]{:S(2)}, u32[]{:S(2)}) collective-permute-start(bf16[128,576]{1,0:T(8,128)(2,1)S(1)} %bitcast.33), channel_id=1, source_target_pairs={{0,8},{8,0},{1,9},{9,1},{2,10},{10,2},{3,11},{11,3},{4,12},{12,4},... | collective-permute-start | bytes 442376 | tf_op jit(solution)/shard_map/ppermute | solution.py:129
  25.4 46.2 %copy-start.10 = (bf16[8,576]{1,0:T(8,128)(2,1)S(1)}, bf16[8,576]{1,0:T(8,128)(2,1)}, u32[]{:S(2)}) copy-start(bf16[8,576]{1,0:T(8,128)(2,1)} %inputs.3) | copy-start | bytes 27652
  25.6 45.9 %copy-start = (bf16[576,4096]{1,0:T(8,128)(2,1)S(1)}, bf16[576,4096]{1,0:T(8,128)(2,1)}, u32[]{:S(2)}) copy-start(bf16[576,4096]{1,0:T(8,128)(2,1)} %refs_1_.4) | copy-start | bytes 14155780
  26.9 197.9 %copy-start.8 = (bf16[256,576]{1,0:T(8,128)(2,1)}, bf16[256,576]{1,0:T(8,128)(2,1)S(1)}, u32[]{:S(2)}) copy-start(bf16[256,576]{1,0:T(8,128)(2,1)S(1)} %get-tuple-element.53.refs_1_) | copy-start | bytes 884740
  51.6 4.0 %collective-permute-start.1 = (bf16[128,1152]{1,0:T(8,128)(2,1)S(1)}, bf16[128,1152]{1,0:T(8,128)(2,1)S(1)}, u32[]{:S(2)}, u32[]{:S(2)}) collective-permute-start(bf16[128,1152]{1,0:T(8,128)(2,1)S(1)} %get-tuple-element.48), channel_id=1, source_target_pairs={{0,8},{8,0},{1,9},{9,1},{2,10},{10,2},{3,11},{11,3},{4,12},{12,4},... | collective-permute-start | bytes 884744 | tf_op jit(solution)/shard_map/ppermute | solution.py:129
  93.5 4.7 %collective-permute-start.2 = (bf16[128,640]{1,0:T(8,128)(2,1)S(1)}, bf16[128,640]{1,0:T(8,128)(2,1)S(1)}, u32[]{:S(2)}, u32[]{:S(2)}) collective-permute-start(bf16[128,640]{1,0:T(8,128)(2,1)S(1)} %bitcast.35), channel_id=1, source_target_pairs={{0,8},{8,0},{1,9},{9,1},{2,10},{10,2},{3,11},{11,3},{4,12},{12,4},... | collective-permute-start | bytes 491528 | tf_op jit(solution)/shard_map/ppermute | solution.py:129
  158.9 16.9 %copy-start.11 = (bf16[8,576]{1,0:T(8,128)(2,1)S(1)}, bf16[8,576]{1,0:T(8,128)(2,1)}, u32[]{:S(2)}) copy-start(bf16[8,576]{1,0:T(8,128)(2,1)} %inputs.3) | copy-start | bytes 27652
  158.9 4.7 %collective-permute-start.3 = (bf16[128,640]{1,0:T(8,128)(2,1)S(1)}, bf16[128,640]{1,0:T(8,128)(2,1)S(1)}, u32[]{:S(2)}, u32[]{:S(2)}) collective-permute-start(bf16[128,640]{1,0:T(8,128)(2,1)S(1)} %shard_map.155), channel_id=1, source_target_pairs={{0,8},{8,0},{1,9},{9,1},{2,10},{10,2},{3,11},{11,3},{4,12},{12,4},... | collective-permute-start | bytes 491528 | tf_op jit(solution)/shard_map/ppermute | solution.py:129
  175.8 44.9 %copy-start.3 = (bf16[576,576]{1,0:T(8,128)(2,1)S(1)}, bf16[576,576]{1,0:T(8,128)(2,1)}, u32[]{:S(2)}) copy-start(bf16[576,576]{1,0:T(8,128)(2,1)} %refs_1_.5) | copy-start | bytes 1990660
  175.8 44.9 %copy-start.5 = (bf16[576,576]{1,0:T(8,128)(2,1)S(1)}, bf16[576,576]{1,0:T(8,128)(2,1)}, u32[]{:S(2)}) copy-start(bf16[576,576]{1,0:T(8,128)(2,1)} %refs_2_.5) | copy-start | bytes 1990660
  176.2 16.2 %copy-start.14 = (f32[8,576]{1,0:T(8,128)}, f32[8,576]{1,0:T(8,128)S(1)}, u32[]{:S(2)}) copy-start(f32[8,576]{1,0:T(8,128)S(1)} %get-tuple-element.78.grad_resid) | copy-start | bytes 55300
  189.9 3.5 %collective-permute-start.4 = (bf16[128,640]{1,0:T(8,128)(2,1)S(1)}, bf16[128,640]{1,0:T(8,128)(2,1)S(1)}, u32[]{:S(2)}, u32[]{:S(2)}) collective-permute-start(bf16[128,640]{1,0:T(8,128)(2,1)S(1)} %bitcast.37), channel_id=1, source_target_pairs={{0,8},{8,0},{1,9},{9,1},{2,10},{10,2},{3,11},{11,3},{4,12},{12,4},... | collective-permute-start | bytes 491528 | tf_op jit(solution)/shard_map/ppermute | solution.py:129
  195.1 31.1 %copy-start.6 = (bf16[256,640]{1,0:T(8,128)(2,1)}, bf16[256,640]{1,0:T(8,128)(2,1)S(1)}, u32[]{:S(2)}) copy-start(bf16[256,640]{1,0:T(8,128)(2,1)S(1)} %get-tuple-element.72.refs_5_) | copy-start | bytes 983044
  195.1 29.7 %copy-start.20 = (f32[576]{0:T(1024)S(1)}, f32[576]{0:T(1024)}, u32[]{:S(2)}) copy-start(f32[576]{0:T(1024)} %param.11) | copy-start | bytes 6916
  208.5 22.6 %copy-start.22 = (s32[256]{0:T(256)S(1)}, s32[256]{0:T(256)}, u32[]{:S(2)}) copy-start(s32[256]{0:T(256)} %copy-done.21) | copy-start | bytes 3076
  221.6 5.0 %copy-start.16 = (bf16[256,576]{1,0:T(8,128)(2,1)}, bf16[256,576]{1,0:T(8,128)(2,1)S(1)}, u32[]{:S(2)}) copy-start(bf16[256,576]{1,0:T(8,128)(2,1)S(1)} %get-tuple-element.80) | copy-start | bytes 884740
  221.8 4.4 %collective-permute-start.5 = (bf16[128,640]{1,0:T(8,128)(2,1)S(1)}, bf16[128,640]{1,0:T(8,128)(2,1)S(1)}, u32[]{:S(2)}, u32[]{:S(2)}) collective-permute-start(bf16[128,640]{1,0:T(8,128)(2,1)S(1)} %get-tuple-element.75), channel_id=1, source_target_pairs={{0,8},{8,0},{1,9},{9,1},{2,10},{10,2},{3,11},{11,3},{4,12},{12,4},... | collective-permute-start | bytes 491528 | tf_op jit(solution)/shard_map/ppermute | solution.py:129
  226.3 0.7 copy-start.13
  226.9 13.6 %all-to-all-start.12 = ((bf16[16,8,640]{2,1,0:T(8,128)(2,1)}), bf16[16,8,640]{2,1,0:T(8,128)(2,1)}, u32[]{:S(2)}, u32[]{:S(2)}) async-start(bf16[16,8,640]{2,1,0:T(8,128)(2,1)} %bitcast.41), calls=%async_computation.12 | async-start | bytes 327680 | tf_op jit(solution)/shard_map/all_to_all | solution.py:104
  231.1 4.9 %copy-start.9 = (bf16[256,576]{1,0:T(8,128)(2,1)S(1)}, bf16[256,576]{1,0:T(8,128)(2,1)}, u32[]{:S(2)}) copy-start(bf16[256,576]{1,0:T(8,128)(2,1)} %copy-done.8) | copy-start | bytes 884740
  231.1 6.3 %copy-start.7 = (bf16[256,640]{1,0:T(8,128)(2,1)S(1)}, bf16[256,640]{1,0:T(8,128)(2,1)}, u32[]{:S(2)}) copy-start(bf16[256,640]{1,0:T(8,128)(2,1)} %copy-done.6) | copy-start | bytes 983044
  231.1 9.4 %copy-start.12 = (bf16[8,576]{1,0:T(8,128)(2,1)S(1)}, bf16[8,576]{1,0:T(8,128)(2,1)}, u32[]{:S(2)}) copy-start(bf16[8,576]{1,0:T(8,128)(2,1)} %inputs.3) | copy-start | bytes 27652
  231.2 9.4 %copy-start.15 = (f32[8,576]{1,0:T(8,128)S(1)}, f32[8,576]{1,0:T(8,128)}, u32[]{:S(2)}) copy-start(f32[8,576]{1,0:T(8,128)} %copy-done.14) | copy-start | bytes 55300

commit v9 on v7

--- a/solution.py
+++ b/solution.py
@@ -86,12 +86,17 @@
     return total
 
 
-def local(body, outs, *args):
+def local(body, outs, *args, reuse=None, off_chip=(), scratch=()):
     return pl.pallas_call(
         body,
         out_shape=tuple(jax.ShapeDtypeStruct(s, d) for s, d in outs),
-        in_specs=[pl.BlockSpec(memory_space=pltpu.VMEM) for _ in args],
+        in_specs=[
+            pl.BlockSpec(memory_space=pltpu.HBM if i in off_chip else pltpu.VMEM)
+            for i in range(len(args))
+        ],
+        scratch_shapes=scratch,
         out_specs=tuple(pl.BlockSpec(memory_space=pltpu.VMEM) for _ in outs),
+        input_output_aliases=reuse or {},
         compiler_params=pltpu.CompilerParams(vmem_limit_bytes=16 << 20),
     )(*args)
 
@@ -218,15 +223,18 @@
     put_copies(out, branch[...].astype(BF16), [post, final])
 
 
-def logit_step(near, far, inputs, gains, head, out, final, message):
-    rejoin(near, far, message)
-    width = final.shape[1]
-    post, scale = read_stats(message[:, tail_of(width)].astype(F32), width, 2)
-    resid = inputs[...].astype(F32) + message[:, :width].astype(F32) * post * gains[1:2]
-    final[...] = (resid * scale * gains[2:3]).astype(BF16)
+def logit_step(part, piece, inputs, gains, head, *rest):
+    out, final, message = rest[-3:]
+    half, width = piece.shape[0], final.shape[1]
+    rows = slice(part * half, (part + 1) * half)
+    message[rows] = piece[...]
+    post, scale = read_stats(piece[:, tail_of(width)].astype(F32), width, 2)
+    resid = inputs[rows].astype(F32) + piece[:, :width].astype(F32) * post * gains[1:2]
+    value = (resid * scale * gains[2:3]).astype(BF16)
+    final[rows] = value
     for i in range(0, head.shape[1], CHUNK):
         columns = slice(i, i + CHUNK)
-        out[:, columns] = contract(final[...], head[:, columns], 1, 0).astype(BF16)
+        out[rows, columns] = contract(value, head[:, columns], 1, 0).astype(BF16)
 
 
 def soft_step(message, ids, out):
@@ -257,7 +265,7 @@
 
 def row_step(message, head, mine, theirs):
     vocab = head.shape[1]
-    total = contract(message[:, :vocab], head[...], 1, 1)
+    total = contract(head[...], message[:, :vocab], 1, 1).T
     stats = read_stats(message[:, vocab : vocab + LANES].astype(F32), vocab, 3)
     put_halves(mine, theirs, total, stats)
 
@@ -363,7 +371,13 @@
     rates[...] = jnp.where(lane == 3, scale, tile)
 
 
-def last_step(message, grad_resid, inputs, out):
+def last_step(message_far, grad_far, inputs_far, out, message, grad_resid, inputs, sems):
+    pairs = ((message_far, message), (grad_far, grad_resid), (inputs_far, inputs))
+    copies = [pltpu.make_async_copy(*pair, sems.at[i]) for i, pair in enumerate(pairs)]
+    for copy in copies:
+        copy.start()
+    for copy in copies:
+        copy.wait()
     width = out.shape[1]
     (back,) = read_stats(summed(message, tail_of(width)), width, 1)
     total = grad_resid[...] + summed(message, slice(0, width))
@@ -452,19 +466,23 @@
         branch,
     )
     near, far = gathered(message)
-    message, final, branch_all = local(
-        logit_step,
-        [
-            ((tokens, vocab), BF16),
-            ((tokens, width), BF16),
-            ((tokens, padded(width)), BF16),
-        ],
-        near,
-        far,
-        inputs,
-        gains,
-        head_weight,
-    )
+    filled = ()
+    for part, piece in enumerate((near, far)):
+        filled = local(
+            lambda *refs, part=part: logit_step(part, *refs),
+            [
+                ((tokens, vocab), BF16),
+                ((tokens, width), BF16),
+                ((tokens, padded(width)), BF16),
+            ],
+            piece,
+            inputs,
+            gains,
+            head_weight,
+            *filled,
+            reuse={4 + i: i for i in range(len(filled))},
+        )
+    message, final, branch_all = filled
     (message,) = local(
         soft_step,
         [((cols_n, sub, vocab + LANES), BF16)],
@@ -522,8 +540,15 @@
         last_step,
         [((tok_dev, width), BF16)],
         message,
-        grad_resid,
-        hidden,
+        pltpu.with_memory_space_constraint(grad_resid, pltpu.HBM),
+        pltpu.with_memory_space_constraint(hidden, pltpu.HBM),
+        off_chip=(0, 1, 2),
+        scratch=(
+            pltpu.VMEM((rows_n, tok_dev, padded(width)), BF16),
+            pltpu.VMEM((tok_dev, width), F32),
+            pltpu.VMEM((tok_dev, width), BF16),
+            pltpu.SemaphoreType.DMA((3,)),
+        ),
     )
 
     spread, pull, along, late_scale = [rates[:, i : i + 1] for i in range(4)]

time: 243 us -> 242 us (level)
    pallas_call x16 -> x17, Pallas kernels: 11.4 us -> 11.3 us  [local(): pl.pallas_call(body, out_shape=tuple((jax.ShapeDtypeStruct(s, d) for s, d...]
  transfers between devices with their start and end apart: 8 -> 8, of which waited for: 7 -> 6; matrix products, arithmetic and copies ran while one was open for 6% -> 6% of each run, Pallas kernels for 0% -> 0%
where the time goes in v9:
time: 242 us; the launch traced here: 241 us
  blocking collectives  170 us (70%)
  starting transfers between devices  33 us (14%)
  matrix products  13.1 us (5%)
  Pallas kernels  11.3 us (5%)
  waiting for transfers between devices  9.06 us (4%)
  local copies, waits for them, and re-layouts  3.62 us (1%)
    all_to_all x11, blocking collectives, exchange(): return lax.all_to_all(parts, axis, 0, 0, tiled=True)  170 us
    ppermute x6, starting transfers between devices, swap(): return lax.ppermute(values, 'core', [(0, 1), (1, 0)])  17 us
    all_to_all x2, starting transfers between devices, exchange(): return lax.all_to_all(parts, axis, 0, 0, tiled=True)  15.9 us
    dot_general x5, matrix products, contract(): lax.dot_general(left, right, (((left_dim,), (right_dim,)), ((), ())), pre...  13.1 us
    pallas_call x17, Pallas kernels, local(): pl.pallas_call(body, out_shape=tuple((jax.ShapeDtypeStruct(s, d) for s, d...  11.3 us
    all_to_all x2, waiting for transfers between devices, exchange(): return lax.all_to_all(parts, axis, 0, 0, tiled=True)  5.28 us
  transfers between devices with their start and end apart: 8, of which 6 were waited for; matrix products, arithmetic and copies ran while one was open for 6% of the time, Pallas kernels for 0%

profile of v9, /device:TPU:1, one launch (start us, length us, event | category | flops | bytes accessed | tf_op | source)
XLA Modules:
  0.0 241.0 jit_solution(335562886004070747)
XLA Ops:
  0.6 1.4 broadcast_in_dim.33
  2.0 11.7 %all-to-all-start = ((bf16[16,8,576]{2,1,0:T(8,128)(2,1)}), bf16[16,8,576]{2,1,0:T(8,128)(2,1)S(1)}, u32[]{:S(2)}, u32[]{:S(2)}) async-start(bf16[16,8,576]{2,1,0:T(8,128)(2,1)} %broadcast_in_dim.33), calls=%async_computation | async-start | bytes 327680 | tf_op jit(solution)/shard_map/all_to_all | solution.py:108
  13.8 0.8 reshape.65
  14.8 4.0 %fusion.7 = bf16[256,576]{0,1:T(8,128)(2,1)S(1)} fusion(bf16[576,4096]{1,0:T(8,128)(2,1)} %head.3, s32[256]{0:T(256)S(1)} %sub.22), kind=kOutput, calls=%fused_computation.13 | convolution fusion | flops 1209155584 | bytes 5014528 | tf_op jit(solution)/shard_map/dot_general | solution.py:21
  19.1 3.6 %all-to-all-done = bf16[16,8,576]{2,1,0:T(8,128)(2,1)S(1)} async-done(((bf16[16,8,576]{2,1,0:T(8,128)(2,1)}), bf16[16,8,576]{2,1,0:T(8,128)(2,1)S(1)}, u32[]{:S(2)}, u32[]{:S(2)}) %all-to-all-start) | async-done | bytes 147488 | tf_op jit(solution)/shard_map/all_to_all | solution.py:108
  22.7 2.3 collective-permute-start
  25.4 0.2 copy.27.target_rows
  25.6 0.5 collective-permute-done.far
  26.1 0.8 shard_map.145
  26.9 14.6 %all_to_all.65.refs_0_ = bf16[8,32,1280]{2,1,0:T(8,128)(2,1)S(1)} all-to-all(bf16[8,32,1280]{2,1,0:T(8,128)(2,1)S(1)} %bitcast.36), channel_id=1, replica_groups=mesh['rows'=16,'core'=2,'width'=8] {'width'}, dimensions={0} | all-to-all | bytes 1310720 | tf_op jit(solution)/shard_map/all_to_all | solution.py:108
  41.5 0.2 shard_map.146
  41.7 9.4 %all_to_all.66 = bf16[8,32,640]{2,1,0:T(8,128)(2,1)S(1)} all-to-all(bf16[8,32,640]{2,1,0:T(8,128)(2,1)S(1)} %get-tuple-element.44), channel_id=1, replica_groups=mesh['rows'=16,'core'=2,'width'=8] {'width'}, dimensions={0} | all-to-all | bytes 655360 | tf_op jit(solution)/shard_map/all_to_all | solution.py:108
  51.1 0.5 shard_map.147
  51.6 2.8 %collective-permute-start.1 = (bf16[128,1152]{1,0:T(8,128)(2,1)S(1)}, bf16[128,1152]{1,0:T(8,128)(2,1)S(1)}, u32[]{:S(2)}, u32[]{:S(2)}) collective-permute-start(bf16[128,1152]{1,0:T(8,128)(2,1)S(1)} %get-tuple-element.47), channel_id=1, source_target_pairs={{0,8},{8,0},{1,9},{9,1},{2,10},{10,2},{3,11},{11,3},{4,12},{12,4},... | collective-permute-start | bytes 884744 | tf_op jit(solution)/shard_map/ppermute | solution.py:133
  54.4 1.2 collective-permute-done.1.refs_1_
  55.6 15.8 %all_to_all.67.message = bf16[16,8,1152]{2,1,0:T(8,128)(2,1)S(1)} all-to-all(bf16[16,8,1152]{2,1,0:T(8,128)(2,1)S(1)} %bitcast.30), channel_id=1, replica_groups=mesh['rows'=16,'core'=2,'width'=8] {'rows'}, dimensions={0} | all-to-all | bytes 589824 | tf_op jit(solution)/shard_map/all_to_all | solution.py:108
  71.6 7.5 %all_to_all.68.refs_0_ = f32[8,8,128]{2,1,0:T(8,128)S(1)} all-to-all(f32[8,8,128]{2,1,0:T(8,128)S(1)} %get-tuple-element.49), channel_id=1, replica_groups=mesh['rows'=16,'core'=2,'width'=8] {'width'}, dimensions={0} | all-to-all | bytes 65536 | tf_op jit(solution)/shard_map/all_to_all | solution.py:108
  79.2 14.3 %all_to_all.69 = bf16[16,8,640]{2,1,0:T(8,128)(2,1)S(1)} all-to-all(bf16[16,8,640]{2,1,0:T(8,128)(2,1)S(1)} %get-tuple-element.51), channel_id=1, replica_groups=mesh['rows'=16,'core'=2,'width'=8] {'rows'}, dimensions={0} | all-to-all | bytes 327680 | tf_op jit(solution)/shard_map/all_to_all | solution.py:108
  93.5 3.6 %collective-permute-start.2 = (bf16[128,640]{1,0:T(8,128)(2,1)S(1)}, bf16[128,640]{1,0:T(8,128)(2,1)S(1)}, u32[]{:S(2)}, u32[]{:S(2)}) collective-permute-start(bf16[128,640]{1,0:T(8,128)(2,1)S(1)} %bitcast.33), channel_id=1, source_target_pairs={{0,8},{8,0},{1,9},{9,1},{2,10},{10,2},{3,11},{11,3},{4,12},{12,4},... | collective-permute-start | bytes 491528 | tf_op jit(solution)/shard_map/ppermute | solution.py:133
  97.1 1.1 shard_map.151
  98.2 1.1 shard_map.152
  99.3 28.9 %all_to_all.70.message = bf16[8,32,4096]{2,1,0:T(8,128)(2,1)S(1)} all-to-all(bf16[8,32,4096]{2,1,0:T(8,128)(2,1)S(1)} %bitcast.23), channel_id=1, replica_groups=mesh['rows'=16,'core'=2,'width'=8] {'width'}, dimensions={0} | all-to-all | bytes 4194304 | tf_op jit(solution)/shard_map/all_to_all | solution.py:108
  128.1 0.7 shard_map.153
  128.8 28.4 %all_to_all.71 = bf16[8,32,4224]{2,1,0:T(8,128)(2,1)S(1)} all-to-all(bf16[8,32,4224]{2,1,0:T(8,128)(2,1)S(1)} %shard_map.153), channel_id=1, replica_groups=mesh['rows'=16,'core'=2,'width'=8] {'width'}, dimensions={0} | all-to-all | bytes 4325376 | tf_op jit(solution)/shard_map/all_to_all | solution.py:108
  157.2 1.5 shard_map.154
  158.7 2.9 %collective-permute-start.3 = (bf16[128,640]{1,0:T(8,128)(2,1)S(1)}, bf16[128,640]{1,0:T(8,128)(2,1)S(1)}, u32[]{:S(2)}, u32[]{:S(2)}) collective-permute-start(bf16[128,640]{1,0:T(8,128)(2,1)S(1)} %get-tuple-element.59), channel_id=1, source_target_pairs={{0,8},{8,0},{1,9},{9,1},{2,10},{10,2},{3,11},{11,3},{4,12},{12,4},... | collective-permute-start | bytes 491528 | tf_op jit(solution)/shard_map/ppermute | solution.py:133
  161.6 1.0 collective-permute-done.3.refs_1_
  162.8 12.0 %all_to_all.72.refs_0_ = bf16[16,8,640]{2,1,0:T(8,128)(2,1)S(1)} all-to-all(bf16[16,8,640]{2,1,0:T(8,128)(2,1)S(1)} %bitcast.35), channel_id=1, replica_groups=mesh['rows'=16,'core'=2,'width'=8] {'rows'}, dimensions={0} | all-to-all | bytes 327680 | tf_op jit(solution)/shard_map/all_to_all | solution.py:108
  174.8 0.4 shard_map.156
  175.1 13.7 %all_to_all.73 = bf16[16,8,640]{2,1,0:T(8,128)(2,1)S(1)} all-to-all(bf16[16,8,640]{2,1,0:T(8,128)(2,1)S(1)} %get-tuple-element.63), channel_id=1, replica_groups=mesh['rows'=16,'core'=2,'width'=8] {'rows'}, dimensions={0} | all-to-all | bytes 327680 | tf_op jit(solution)/shard_map/all_to_all | solution.py:108
  188.9 2.4 collective-permute-start.4
  191.3 1.0 collective-permute-done.4.refs_1_
  192.3 1.2 shard_map.157
  193.5 13.1 %all_to_all.74.refs_0_ = bf16[8,32,1280]{2,1,0:T(8,128)(2,1)S(1)} all-to-all(bf16[8,32,1280]{2,1,0:T(8,128)(2,1)S(1)} %bitcast.37), channel_id=1, replica_groups=mesh['rows'=16,'core'=2,'width'=8] {'width'}, dimensions={0} | all-to-all | bytes 1310720 | tf_op jit(solution)/shard_map/all_to_all | solution.py:108
  206.7 0.2 shard_map.158
  206.9 12.1 %all_to_all.75 = bf16[8,32,1280]{2,1,0:T(8,128)(2,1)S(1)} all-to-all(bf16[8,32,1280]{2,1,0:T(8,128)(2,1)S(1)} %shard_map.158), channel_id=1, replica_groups=mesh['rows'=16,'core'=2,'width'=8] {'width'}, dimensions={0} | all-to-all | bytes 1310720 | tf_op jit(solution)/shard_map/all_to_all | solution.py:108
  219.0 0.9 shard_map.159
  219.9 0.2 slice_reduce_fusion.4
  220.1 3.0 %collective-permute-start.5 = (bf16[128,640]{1,0:T(8,128)(2,1)S(1)}, bf16[128,640]{1,0:T(8,128)(2,1)S(1)}, u32[]{:S(2)}, u32[]{:S(2)}) collective-permute-start(bf16[128,640]{1,0:T(8,128)(2,1)S(1)} %get-tuple-element.73), channel_id=1, source_target_pairs={{0,8},{8,0},{1,9},{9,1},{2,10},{10,2},{3,11},{11,3},{4,12},{12,4},... | collective-permute-start | bytes 491528 | tf_op jit(solution)/shard_map/ppermute | solution.py:133
  223.1 1.4 convolution_convert_fusion.3
  224.5 0.8 shard_map.160
  225.2 0.3 slice_reduce_fusion.1
  225.6 4.2 %all-to-all-start.12 = ((bf16[16,8,640]{2,1,0:T(8,128)(2,1)}), bf16[16,8,640]{2,1,0:T(8,128)(2,1)}, u32[]{:S(2)}, u32[]{:S(2)}) async-start(bf16[16,8,640]{2,1,0:T(8,128)(2,1)} %bitcast.14), calls=%async_computation.12 | async-start | bytes 327680 | tf_op jit(solution)/shard_map/all_to_all | solution.py:108
  229.8 4.9 %convolution_convert_fusion = bf16[576,4096]{1,0:T(8,128)(2,1)} fusion(bf16[256,576]{1,0:T(8,128)(2,1)} %copy-done.15, bf16[256,4224]{1,0:T(8,128)(2,1)S(1)} %bitcast.22, f32[256]{0:T(256)S(1)} %get-tuple-element.81, f32[256]{0:T(256)S(1)} %get-tuple-element.80, s32[256]{0:T(256)} %copy-done.21), kind=kOutput, calls=%fused_computation | convolution fusion | flops 1216610304 | bytes 7113728 | tf_op jit(solution)/shard_map/dot_general | solution.py:21
  234.8 1.4 convolution_convert_fusion.2
  236.2 1.4 convolution_convert_fusion.1
  237.5 1.7 all-to-all-done.12.message_far
  239.2 1.6 shard_map.161
  (66 shorter events, 1.2 us)
Async XLA Ops:
  2.0 20.7 %all-to-all-start = ((bf16[16,8,576]{2,1,0:T(8,128)(2,1)}), bf16[16,8,576]{2,1,0:T(8,128)(2,1)S(1)}, u32[]{:S(2)}, u32[]{:S(2)}) async-start(bf16[16,8,576]{2,1,0:T(8,128)(2,1)} %broadcast_in_dim.33), calls=%async_computation | async-start | bytes 327680 | tf_op jit(solution)/shard_map/all_to_all | solution.py:108
  14.7 4.3 %copy-start.21 = (s32[256]{0:T(256)}, s32[256]{0:T(256)S(1)}, u32[]{:S(2)}) copy-start(s32[256]{0:T(256)S(1)} %sub.22) | copy-start | bytes 3076
  14.7 4.1 %copy-start.22 = (f32[32]{0:T(128)S(1)}, f32[32]{0:T(128)}, u32[]{:S(2)}) copy-start(f32[32]{0:T(128)} %param.19) | copy-start | bytes 388
  14.8 10.4 %copy-start.16 = (f32[576]{0:T(1024)S(1)}, f32[576]{0:T(1024)}, u32[]{:S(2)}) copy-start(f32[576]{0:T(1024)} %param.12) | copy-start | bytes 6916
  14.8 10.4 %copy-start.17 = (f32[576]{0:T(1024)S(1)}, f32[576]{0:T(1024)}, u32[]{:S(2)}) copy-start(f32[576]{0:T(1024)} %param.13) | copy-start | bytes 6916
  14.8 10.4 %copy-start.18 = (f32[576]{0:T(1024)S(1)}, f32[576]{0:T(1024)}, u32[]{:S(2)}) copy-start(f32[576]{0:T(1024)} %param.11) | copy-start | bytes 6916
  14.8 11.3 %copy-start.1 = (bf16[576,576]{1,0:T(8,128)(2,1)S(1)}, bf16[576,576]{1,0:T(8,128)(2,1)}, u32[]{:S(2)}) copy-start(bf16[576,576]{1,0:T(8,128)(2,1)} %refs_1_.1) | copy-start | bytes 1990660
  14.8 11.3 %copy-start.2 = (bf16[576,576]{1,0:T(8,128)(2,1)S(1)}, bf16[576,576]{1,0:T(8,128)(2,1)}, u32[]{:S(2)}) copy-start(bf16[576,576]{1,0:T(8,128)(2,1)} %refs_2_.1) | copy-start | bytes 1990660
  18.9 32.3 %copy-start.4 = (bf16[576,576]{1,0:T(8,128)(2,1)S(1)}, bf16[576,576]{1,0:T(8,128)(2,1)}, u32[]{:S(2)}) copy-start(bf16[576,576]{1,0:T(8,128)(2,1)} %refs_3_.7) | copy-start | bytes 1990660
  22.7 3.4 %collective-permute-start = (bf16[128,576]{1,0:T(8,128)(2,1)S(1)}, bf16[128,576]{1,0:T(8,128)(2,1)S(1)}, u32[]{:S(2)}, u32[]{:S(2)}) collective-permute-start(bf16[128,576]{1,0:T(8,128)(2,1)S(1)} %bitcast.31), channel_id=1, source_target_pairs={{0,8},{8,0},{1,9},{9,1},{2,10},{10,2},{3,11},{11,3},{4,12},{12,4},... | collective-permute-start | bytes 442376 | tf_op jit(solution)/shard_map/ppermute | solution.py:133
  25.4 46.1 %copy-start.12 = (bf16[8,576]{1,0:T(8,128)(2,1)S(1)}, bf16[8,576]{1,0:T(8,128)(2,1)}, u32[]{:S(2)}) copy-start(bf16[8,576]{1,0:T(8,128)(2,1)} %inputs_far.1) | copy-start | bytes 27652
  25.6 45.9 %copy-start = (bf16[576,4096]{1,0:T(8,128)(2,1)S(1)}, bf16[576,4096]{1,0:T(8,128)(2,1)}, u32[]{:S(2)}) copy-start(bf16[576,4096]{1,0:T(8,128)(2,1)} %head.3) | copy-start | bytes 14155780
  26.9 196.2 %copy-start.8 = (bf16[256,576]{1,0:T(8,128)(2,1)}, bf16[256,576]{1,0:T(8,128)(2,1)S(1)}, u32[]{:S(2)}) copy-start(bf16[256,576]{1,0:T(8,128)(2,1)S(1)} %get-tuple-element.52.refs_1_) | copy-start | bytes 884740
  51.6 4.0 %collective-permute-start.1 = (bf16[128,1152]{1,0:T(8,128)(2,1)S(1)}, bf16[128,1152]{1,0:T(8,128)(2,1)S(1)}, u32[]{:S(2)}, u32[]{:S(2)}) collective-permute-start(bf16[128,1152]{1,0:T(8,128)(2,1)S(1)} %get-tuple-element.47), channel_id=1, source_target_pairs={{0,8},{8,0},{1,9},{9,1},{2,10},{10,2},{3,11},{11,3},{4,12},{12,4},... | collective-permute-start | bytes 884744 | tf_op jit(solution)/shard_map/ppermute | solution.py:133
  93.5 4.7 %collective-permute-start.2 = (bf16[128,640]{1,0:T(8,128)(2,1)S(1)}, bf16[128,640]{1,0:T(8,128)(2,1)S(1)}, u32[]{:S(2)}, u32[]{:S(2)}) collective-permute-start(bf16[128,640]{1,0:T(8,128)(2,1)S(1)} %bitcast.33), channel_id=1, source_target_pairs={{0,8},{8,0},{1,9},{9,1},{2,10},{10,2},{3,11},{11,3},{4,12},{12,4},... | collective-permute-start | bytes 491528 | tf_op jit(solution)/shard_map/ppermute | solution.py:133
  157.2 17.6 %copy-start.13 = (bf16[8,576]{1,0:T(8,128)(2,1)S(1)}, bf16[8,576]{1,0:T(8,128)(2,1)}, u32[]{:S(2)}) copy-start(bf16[8,576]{1,0:T(8,128)(2,1)} %inputs_far.1) | copy-start | bytes 27652
  157.2 35.1 %copy-start.5 = (bf16[576,576]{1,0:T(8,128)(2,1)S(1)}, bf16[576,576]{1,0:T(8,128)(2,1)}, u32[]{:S(2)}) copy-start(bf16[576,576]{1,0:T(8,128)(2,1)} %refs_3_.7) | copy-start | bytes 1990660
  158.7 60.3 %copy-start.3 = (bf16[576,576]{1,0:T(8,128)(2,1)S(1)}, bf16[576,576]{1,0:T(8,128)(2,1)}, u32[]{:S(2)}) copy-start(bf16[576,576]{1,0:T(8,128)(2,1)} %refs_2_.1) | copy-start | bytes 1990660
  158.7 3.9 %collective-permute-start.3 = (bf16[128,640]{1,0:T(8,128)(2,1)S(1)}, bf16[128,640]{1,0:T(8,128)(2,1)S(1)}, u32[]{:S(2)}, u32[]{:S(2)}) collective-permute-start(bf16[128,640]{1,0:T(8,128)(2,1)S(1)} %get-tuple-element.59), channel_id=1, source_target_pairs={{0,8},{8,0},{1,9},{9,1},{2,10},{10,2},{3,11},{11,3},{4,12},{12,4},... | collective-permute-start | bytes 491528 | tf_op jit(solution)/shard_map/ppermute | solution.py:133
  175.1 44.7 %copy-start.14 = (f32[8,576]{1,0:T(8,128)}, f32[8,576]{1,0:T(8,128)S(1)}, u32[]{:S(2)}) copy-start(f32[8,576]{1,0:T(8,128)S(1)} %get-tuple-element.76.grad_far) | copy-start | bytes 55300
  188.9 3.4 %collective-permute-start.4 = (bf16[128,640]{1,0:T(8,128)(2,1)S(1)}, bf16[128,640]{1,0:T(8,128)(2,1)S(1)}, u32[]{:S(2)}, u32[]{:S(2)}) collective-permute-start(bf16[128,640]{1,0:T(8,128)(2,1)S(1)} %bitcast.38), channel_id=1, source_target_pairs={{0,8},{8,0},{1,9},{9,1},{2,10},{10,2},{3,11},{11,3},{4,12},{12,4},... | collective-permute-start | bytes 491528 | tf_op jit(solution)/shard_map/ppermute | solution.py:133
  193.5 30.9 %copy-start.10 = (bf16[256,640]{1,0:T(8,128)(2,1)}, bf16[256,640]{1,0:T(8,128)(2,1)S(1)}, u32[]{:S(2)}) copy-start(bf16[256,640]{1,0:T(8,128)(2,1)S(1)} %get-tuple-element.70.refs_5_) | copy-start | bytes 983044
  193.5 29.5 %copy-start.19 = (f32[576]{0:T(1024)S(1)}, f32[576]{0:T(1024)}, u32[]{:S(2)}) copy-start(f32[576]{0:T(1024)} %param.11) | copy-start | bytes 6916
  219.0 4.1 %copy-start.6 = (bf16[8,32,1280]{2,1,0:T(8,128)(2,1)}, bf16[8,32,1280]{2,1,0:T(8,128)(2,1)S(1)}, u32[]{:S(2)}) copy-start(bf16[8,32,1280]{2,1,0:T(8,128)(2,1)S(1)} %all_to_all.75) | copy-start | bytes 1966084
  219.9 5.7 %copy-start.15 = (bf16[256,576]{1,0:T(8,128)(2,1)}, bf16[256,576]{1,0:T(8,128)(2,1)S(1)}, u32[]{:S(2)}) copy-start(bf16[256,576]{1,0:T(8,128)(2,1)S(1)} %get-tuple-element.78) | copy-start | bytes 884740
  220.1 4.4 %collective-permute-start.5 = (bf16[128,640]{1,0:T(8,128)(2,1)S(1)}, bf16[128,640]{1,0:T(8,128)(2,1)S(1)}, u32[]{:S(2)}, u32[]{:S(2)}) collective-permute-start(bf16[128,640]{1,0:T(8,128)(2,1)S(1)} %get-tuple-element.73), channel_id=1, source_target_pairs={{0,8},{8,0},{1,9},{9,1},{2,10},{10,2},{3,11},{11,3},{4,12},{12,4},... | collective-permute-start | bytes 491528 | tf_op jit(solution)/shard_map/ppermute | solution.py:133
  225.6 13.6 %all-to-all-start.12 = ((bf16[16,8,640]{2,1,0:T(8,128)(2,1)}), bf16[16,8,640]{2,1,0:T(8,128)(2,1)}, u32[]{:S(2)}, u32[]{:S(2)}) async-start(bf16[16,8,640]{2,1,0:T(8,128)(2,1)} %bitcast.14), calls=%async_computation.12 | async-start | bytes 327680 | tf_op jit(solution)/shard_map/all_to_all | solution.py:108
  229.8 5.0 %copy-start.7 = (bf16[8,32,1280]{2,1,0:T(8,128)(2,1)S(1)}, bf16[8,32,1280]{2,1,0:T(8,128)(2,1)}, u32[]{:S(2)}) copy-start(bf16[8,32,1280]{2,1,0:T(8,128)(2,1)} %copy-done.6) | copy-start | bytes 1966084
  229.8 5.0 %copy-start.9 = (bf16[256,576]{1,0:T(8,128)(2,1)S(1)}, bf16[256,576]{1,0:T(8,128)(2,1)}, u32[]{:S(2)}) copy-start(bf16[256,576]{1,0:T(8,128)(2,1)} %copy-done.8) | copy-start | bytes 884740
  229.8 5.0 %copy-start.20 = (f32[576]{0:T(1024)S(1)}, f32[576]{0:T(1024)}, u32[]{:S(2)}) copy-start(f32[576]{0:T(1024)} %param.11) | copy-start | bytes 6916
  229.8 6.3 %copy-start.11 = (bf16[256,640]{1,0:T(8,128)(2,1)S(1)}, bf16[256,640]{1,0:T(8,128)(2,1)}, u32[]{:S(2)}) copy-start(bf16[256,640]{1,0:T(8,128)(2,1)} %copy-done.10) | copy-start | bytes 983044
